TPU v7x, 32 devices: a whole 2x2x4 slice. The times are simulated.
32 devices in a mesh: dp: 8 (over z, x), fsdp: 4 (over y, core).
Axes of the slice: x: 2, y: 2, z: 4, core: 2. Of those that a mesh axis runs over, the one named last changes fastest.
Arguments:
- first_half: float32 [2, 8, 1280, 1024], P(None, 'dp', 'fsdp'), may hold values from -6 to 6
- second_half: float32 [2, 8, 1280, 1024], P(None, 'dp', 'fsdp'), may hold values from -6 to 6
- grad_first: float32 [2, 8, 1280, 1024], P(None, 'dp', 'fsdp'), may hold values from -6 to 6
- grad_second: float32 [2, 8, 1280, 1024], P(None, 'dp', 'fsdp'), may hold values from -6 to 6
- query_weight: bfloat16 [1024, 1024], P(('dp', 'fsdp')), may hold values from -0.1875 to 0.1875
- value_weight: bfloat16 [1024, 1024], P(('dp', 'fsdp')), may hold values from -0.1875 to 0.1875
- output_weight: bfloat16 [1024, 1024], P(('dp', 'fsdp')), may hold values from -1.5 to 1.5
- inner_weight: bfloat16 [1024, 4096], P(('dp', 'fsdp')), may hold values from -0.1875 to 0.1875
- inner_bias: bfloat16 [4096], P(('dp', 'fsdp')), may hold values from -3 to 3
- outer_weight: bfloat16 [4096, 1024], P(('dp', 'fsdp')), may hold values from -0.09375 to 0.09375
- outer_bias: bfloat16 [1024], P(('dp', 'fsdp')), may hold values from -2 to 2
- mixer_gain: bfloat16 [1024], P(('dp', 'fsdp')), may hold values from 0.5 to 1.5
- mixer_shift: bfloat16 [1024], P(('dp', 'fsdp')), may hold values from -2 to 2
- feed_gain: bfloat16 [1024], P(('dp', 'fsdp')), may hold values from 0.5 to 1.5
- feed_shift: bfloat16 [1024], P(('dp', 'fsdp')), may hold values from -2 to 2
- parents: int32 [2, 8, 10], P(None, 'dp'), may hold values from 0 to 5, as said below
- buckets: int32 [2, 8, 4, 1280], P(None, 'dp'), may hold values from 0 to 31
- order: int32 [2, 8, 4, 1280], P(None, 'dp'), may hold values from 0 to 1279, as said below
Outputs:
- first_out: float32 [2, 8, 1280, 1024], P(None, 'dp', 'fsdp')
- second_out: float32 [2, 8, 1280, 1024], P(None, 'dp', 'fsdp')
- grad_first_in: float32 [2, 8, 1280, 1024], P(None, 'dp', 'fsdp')
- grad_second_in: float32 [2, 8, 1280, 1024], P(None, 'dp', 'fsdp')
- query_grad: float32 [1024, 1024], P(('dp', 'fsdp'))
- value_grad: float32 [1024, 1024], P(('dp', 'fsdp'))
- output_grad: float32 [1024, 1024], P(('dp', 'fsdp'))
- inner_grad: float32 [1024, 4096], P(('dp', 'fsdp'))
- inner_bias_grad: float32 [4096], P(('dp', 'fsdp'))
- outer_grad: float32 [4096, 1024], P(('dp', 'fsdp'))
- outer_bias_grad: float32 [1024], P(('dp', 'fsdp'))
- mixer_gain_grad: float32 [1024], P(('dp', 'fsdp'))
- mixer_shift_grad: float32 [1024], P(('dp', 'fsdp'))
- feed_gain_grad: float32 [1024], P(('dp', 'fsdp'))
- feed_shift_grad: float32 [1024], P(('dp', 'fsdp'))
Inputs may be any that keep to these rules, and one draw needn't show every extreme that they name: In each tree the first 4 segments form a chain (segment i has parent i - 1, segment 0 is its own parent); each of the next 2 segments has a parent that is trunk segment 2 or 3; the last 4 segments have parents among the branch segments, 2 on each branch. `order`: for each tree and round, every position once, ordered by that round's bucket and, within a bucket, by position.
All inputs are finite; a program needn't handle non-finite values.
Results may differ from a plain program's by a relative error of at most 0.019.
Values may be sent and summed in bfloat16 or wider, within the bound.
No kernel may reach another device: no remote copies, remote signals or barrier semaphores. Data moves between devices by JAX's collectives and lax.ppermute only.
A program may use at most 384 MiB of HBM per device.

v0:
```python
import math

import jax
import jax.numpy as jnp
from jax import lax
from jax.sharding import PartitionSpec as P

H = 8
DH = 128
CH = 64
SEG = 128


SELF_SCORE = -10000.0
NEG_SCORE = -1e30
EPSILON = 1e-06


def layer_norm(values, gain_vec, shift_vec):
    center = values - jnp.mean(values, axis=-1, keepdims=True)
    factor = lax.rsqrt(jnp.mean(center * center, axis=-1, keepdims=True) + EPSILON)
    return center * factor * gain_vec + shift_vec


def key_norm(rows_in, head_count):
    heads_view = rows_in.reshape(rows_in.shape[:-1] + (head_count, rows_in.shape[-1] // head_count))
    factor = lax.rsqrt(jnp.mean(heads_view * heads_view, axis=-1, keepdims=True) + EPSILON)
    return (heads_view * factor / math.sqrt(heads_view.shape[-1])).reshape(rows_in.shape)


def fast_gelu(values):
    return jax.nn.gelu(values, approximate=True)


def ancestry(parent_row):
    segments = parent_row.shape[0]
    indices = jnp.arange(segments, dtype=jnp.int32)
    step_map = (parent_row[:, None] == indices[None, :]).astype(jnp.float32)
    reached = jnp.minimum(jnp.eye(segments, dtype=jnp.float32) + step_map, 1.0)
    for _ in range(segments.bit_length()):
        reached = jnp.minimum(jnp.dot(reached, reached, precision=lax.Precision.HIGHEST), 1.0)
    return reached


def project(second, query_full, value_full, gain_vec, shift_vec):
    mixed_low = layer_norm(second, gain_vec, shift_vec).astype(jnp.bfloat16)
    query_key = jnp.dot(mixed_low, query_full, preferred_element_type=jnp.float32).astype(
        jnp.bfloat16
    )
    value_low = jnp.dot(mixed_low, value_full, preferred_element_type=jnp.float32).astype(
        jnp.bfloat16
    )
    return (mixed_low, query_key, value_low)


def invert(ranking):
    tree_len = ranking.shape[0]
    return jnp.zeros((tree_len,), jnp.int32).at[ranking].set(jnp.arange(tree_len, dtype=jnp.int32))


def per_device(
    first_half,
    second_half,
    grad_first,
    grad_second,
    query_weight,
    value_weight,
    output_weight,
    inner_weight,
    inner_bias,
    outer_weight,
    outer_bias,
    mixer_gain,
    mixer_shift,
    feed_gain,
    feed_shift,
    parents,
    buckets,
    order,
):
    batches = first_half.shape[0]
    row_count = first_half.shape[2]
    features = first_half.shape[3]
    hidden = inner_weight.shape[1]
    rounds = order.shape[2]
    tree_len = order.shape[3]
    window = (row_count // CH + 3) * CH
    position = lax.axis_index("fsdp")
    first_row = position * row_count
    key_start = jnp.clip((first_row // CH - 1) * CH, 0, tree_len - window)
    shards = (
        query_weight,
        value_weight,
        output_weight,
        inner_weight,
        inner_bias,
        outer_weight,
        outer_bias,
        mixer_gain,
        mixer_shift,
        feed_gain,
        feed_shift,
    )
    bfloat = jnp.bfloat16
    single = jnp.float32

    def one_batch(batch_index, state_in):
        sums_in, outputs = state_in
        full_set = (
            lax.all_gather(shards[0], ("dp", "fsdp"), axis=0, tiled=True),
            lax.all_gather(shards[1], ("dp", "fsdp"), axis=0, tiled=True),
            lax.all_gather(shards[2], ("dp", "fsdp"), axis=0, tiled=True),
            lax.all_gather(shards[3], ("dp", "fsdp"), axis=0, tiled=True),
            lax.all_gather(shards[4], ("dp", "fsdp"), axis=0, tiled=True),
            lax.all_gather(shards[5], ("dp", "fsdp"), axis=0, tiled=True),
            lax.all_gather(shards[6], ("dp", "fsdp"), axis=0, tiled=True),
            lax.all_gather(shards[7], ("dp", "fsdp"), axis=0, tiled=True),
            lax.all_gather(shards[8], ("dp", "fsdp"), axis=0, tiled=True),
            lax.all_gather(shards[9], ("dp", "fsdp"), axis=0, tiled=True),
            lax.all_gather(shards[10], ("dp", "fsdp"), axis=0, tiled=True),
        )
        first_rows = lax.dynamic_index_in_dim(first_half, batch_index, 0, False)[0]
        second = lax.dynamic_index_in_dim(second_half, batch_index, 0, False)[0]
        grad_first_rows = lax.dynamic_index_in_dim(grad_first, batch_index, 0, False)[0]
        grad_second_rows = lax.dynamic_index_in_dim(grad_second, batch_index, 0, False)[0]
        parent_row = lax.dynamic_index_in_dim(parents, batch_index, 0, False)[0]
        bucket_rows = lax.dynamic_index_in_dim(buckets, batch_index, 0, False)[0]
        order_rows = lax.dynamic_index_in_dim(order, batch_index, 0, False)[0]
        ancestors = ancestry(parent_row)
        query_tok = lax.dynamic_slice_in_dim(order_rows, first_row, row_count, 1)
        key_tok = lax.dynamic_slice_in_dim(order_rows, key_start, window, 1)
        sorted_bucket = jnp.take_along_axis(bucket_rows, order_rows, axis=1)
        query_bucket = lax.dynamic_slice_in_dim(sorted_bucket, first_row, row_count, 1)
        key_bucket = lax.dynamic_slice_in_dim(sorted_bucket, key_start, window, 1)
        query_block = (first_row + jnp.arange(row_count, dtype=jnp.int32)) // CH
        key_block = (key_start + jnp.arange(window, dtype=jnp.int32)) // CH
        nearby = (key_block[None, :] == query_block[:, None]) | (
            key_block[None, :] == query_block[:, None] - 1
        )
        segment_ids = jnp.arange(ancestors.shape[0], dtype=jnp.int32)
        query_seg = ((query_tok // SEG)[..., None] == segment_ids).astype(single)
        key_seg = ((key_tok // SEG)[..., None] == segment_ids).astype(single)
        linked = jnp.einsum("rqs,st,rkt->rqk", query_seg, ancestors, key_seg) > 0.5
        usable = (
            nearby[None]
            & (query_bucket[:, :, None] == key_bucket[:, None, :])
            & (key_tok[:, None, :] <= query_tok[:, :, None])
            & linked
        )
        itself = (key_tok[:, None, :] == query_tok[:, :, None])[:, None]
        usable = usable[:, None]
        inverse = jax.vmap(invert)(order_rows)

        def scores_of(query_all, value_all):
            queries = query_all[query_tok].reshape(rounds, row_count, H, DH)
            key_rows = query_all[key_tok].astype(single)
            unit_low = key_norm(key_rows, H).astype(bfloat).reshape(rounds, window, H, DH)
            values = value_all[key_tok].reshape(rounds, window, H, DH)
            scores = jnp.einsum("rqhd,rkhd->rhqk", queries, unit_low, preferred_element_type=single)
            masked = jnp.where(itself, SELF_SCORE, jnp.where(usable, scores, NEG_SCORE))
            return (queries, key_rows, unit_low, values, masked)

        def totals_of(gathered_lse):
            token_lse = jnp.take_along_axis(gathered_lse, inverse[:, None, :], axis=2)
            overall = jax.nn.logsumexp(token_lse, axis=0)
            return jnp.moveaxis(jnp.take(overall, query_tok, axis=1), 0, 1)

        gain_mix = full_set[7].astype(single)
        shift_mix = full_set[8].astype(single)
        gain_feed = full_set[9].astype(single)
        shift_feed = full_set[10].astype(single)
        mixed_low, query_key, value_low = project(
            second, full_set[0], full_set[1], gain_mix, shift_mix
        )
        query_all, value_all = (
            lax.all_gather(query_key, "fsdp", axis=0, tiled=True),
            lax.all_gather(value_low, "fsdp", axis=0, tiled=True),
        )
        queries, key_rows, unit_low, values, masked = scores_of(query_all, value_all)
        block_lse = jax.nn.logsumexp(masked, axis=-1)
        query_total = totals_of(lax.all_gather(block_lse, "fsdp", axis=2, tiled=True))
        chances = jnp.exp(masked - query_total[..., None])
        weighted = jnp.einsum(
            "rhqk,rkhd->rqhd", chances.astype(bfloat), values, preferred_element_type=single
        ).reshape(rounds * row_count, features)
        spread = jnp.zeros((tree_len, features), single).at[query_tok.reshape(-1)].add(weighted)
        attended = lax.psum_scatter(
            spread.astype(jnp.bfloat16), "fsdp", scatter_dimension=0, tiled=True
        ).astype(jnp.float32)
        attended_low = attended.astype(bfloat)
        first_out = first_rows + jnp.dot(attended_low, full_set[2], preferred_element_type=single)
        feed_low = layer_norm(first_out, gain_feed, shift_feed).astype(bfloat)
        inner_pre = jnp.dot(feed_low, full_set[3], preferred_element_type=single) + full_set[
            4
        ].astype(single)
        active_low = fast_gelu(inner_pre).astype(bfloat)
        second_out = (
            second
            + jnp.dot(active_low, full_set[5], preferred_element_type=single)
            + full_set[6].astype(single)
        )
        weights_back = (
            lax.all_gather(shards[0], ("dp", "fsdp"), axis=0, tiled=True),
            lax.all_gather(shards[1], ("dp", "fsdp"), axis=0, tiled=True),
            lax.all_gather(shards[2], ("dp", "fsdp"), axis=0, tiled=True),
            lax.all_gather(shards[3], ("dp", "fsdp"), axis=0, tiled=True),
            lax.all_gather(shards[4], ("dp", "fsdp"), axis=0, tiled=True),
            lax.all_gather(shards[5], ("dp", "fsdp"), axis=0, tiled=True),
            lax.all_gather(shards[6], ("dp", "fsdp"), axis=0, tiled=True),
            lax.all_gather(shards[7], ("dp", "fsdp"), axis=0, tiled=True),
            lax.all_gather(shards[8], ("dp", "fsdp"), axis=0, tiled=True),
            lax.all_gather(shards[9], ("dp", "fsdp"), axis=0, tiled=True),
            lax.all_gather(shards[10], ("dp", "fsdp"), axis=0, tiled=True),
        )
        outer_low = grad_second_rows.astype(bfloat)
        outer_bias_sum = jnp.sum(outer_low.astype(single), axis=0)
        outer_sum = jnp.dot(active_low.T, outer_low, preferred_element_type=single)
        grad_active = jnp.dot(outer_low, weights_back[5].T, preferred_element_type=single)
        inner_low = jax.vjp(fast_gelu, inner_pre)[1](grad_active)[0].astype(bfloat)
        inner_sum = jnp.dot(feed_low.T, inner_low, preferred_element_type=single)
        inner_bias_sum = jnp.sum(inner_low.astype(single), axis=0)
        grad_feed = jnp.dot(inner_low, weights_back[3].T, preferred_element_type=single)
        feed_pull = jax.vjp(
            layer_norm, first_out, weights_back[9].astype(single), weights_back[10].astype(single)
        )[1]
        feed_through, feed_gain_sum, feed_shift_sum = feed_pull(grad_feed)
        grad_first_in = grad_first_rows + feed_through
        branch_low = grad_first_in.astype(bfloat)
        output_sum = jnp.dot(attended_low.T, branch_low, preferred_element_type=single)
        grad_attended = jnp.dot(
            branch_low, weights_back[2].T, preferred_element_type=single
        ).astype(bfloat)
        delta_sum = jnp.sum(
            (grad_attended.astype(single) * attended).reshape(row_count, H, DH), axis=-1
        )
        grad_all = lax.all_gather(grad_attended, "fsdp", axis=0, tiled=True)
        delta_all = lax.all_gather(delta_sum, "fsdp", axis=0, tiled=True)
        mixed_back, query_back, value_back = project(
            second,
            weights_back[0],
            weights_back[1],
            weights_back[7].astype(single),
            weights_back[8].astype(single),
        )
        query_again, value_again = (
            lax.all_gather(query_back, "fsdp", axis=0, tiled=True),
            lax.all_gather(value_back, "fsdp", axis=0, tiled=True),
        )
        queries_b, key_rows_b, unit_b, values_b, masked_b = scores_of(query_again, value_again)
        total_b = totals_of(
            lax.all_gather(jax.nn.logsumexp(masked_b, axis=-1), "fsdp", axis=2, tiled=True)
        )
        chances_b = jnp.exp(masked_b - total_b[..., None])
        grad_rows = grad_all[query_tok].reshape(rounds, row_count, H, DH)
        dot_rows = jnp.einsum("rqhd,rkhd->rhqk", grad_rows, values_b, preferred_element_type=single)
        delta_rows = jnp.moveaxis(jnp.take(delta_all, query_tok, axis=0), -1, 1)
        grad_scores = jnp.where(
            usable & jnp.logical_not(itself), chances_b * (dot_rows - delta_rows[..., None]), 0.0
        ).astype(bfloat)
        grad_queries = jnp.einsum(
            "rhqk,rkhd->rqhd", grad_scores, unit_b, preferred_element_type=single
        ).reshape(rounds * row_count, features)
        grad_units = jnp.einsum(
            "rhqk,rqhd->rkhd", grad_scores, queries_b, preferred_element_type=single
        ).reshape(rounds, window, features)
        grad_values = jnp.einsum(
            "rhqk,rqhd->rkhd", chances_b.astype(bfloat), grad_rows, preferred_element_type=single
        ).reshape(rounds * window, features)
        grad_keys = jax.vjp(lambda rows_in: key_norm(rows_in, H), key_rows_b)[1](grad_units)[
            0
        ].reshape(rounds * window, features)
        key_flat = key_tok.reshape(-1)
        spread_query = (
            jnp.zeros((tree_len, features), single)
            .at[query_tok.reshape(-1)]
            .add(grad_queries)
            .at[key_flat]
            .add(grad_keys)
        )
        spread_value = jnp.zeros((tree_len, features), single).at[key_flat].add(grad_values)
        grad_query_key, grad_value = (
            lax.psum_scatter(
                spread_query.astype(jnp.bfloat16), "fsdp", scatter_dimension=0, tiled=True
            ).astype(jnp.float32),
            lax.psum_scatter(
                spread_value.astype(jnp.bfloat16), "fsdp", scatter_dimension=0, tiled=True
            ).astype(jnp.float32),
        )
        query_low = grad_query_key.astype(bfloat)
        value_grad_low = grad_value.astype(bfloat)
        query_sum = jnp.dot(mixed_back.T, query_low, preferred_element_type=single)
        value_sum = jnp.dot(mixed_back.T, value_grad_low, preferred_element_type=single)
        grad_mixed = jnp.dot(query_low, weights_back[0].T, preferred_element_type=single) + jnp.dot(
            value_grad_low, weights_back[1].T, preferred_element_type=single
        )
        mix_pull = jax.vjp(
            layer_norm, second, weights_back[7].astype(single), weights_back[8].astype(single)
        )[1]
        mix_through, mix_gain_sum, mix_shift_sum = mix_pull(grad_mixed)
        grad_second_in = grad_second_rows + mix_through
        terms = (
            query_sum,
            value_sum,
            output_sum,
            inner_sum,
            inner_bias_sum,
            outer_sum,
            outer_bias_sum,
            mix_gain_sum,
            mix_shift_sum,
            feed_gain_sum,
            feed_shift_sum,
        )
        sums_out = tuple((older + newer for older, newer in zip(sums_in, terms)))
        fresh = (first_out, second_out, grad_first_in, grad_second_in)
        outputs = tuple(
            (
                lax.dynamic_update_slice_in_dim(buffer, value_rows[None, None], batch_index, 0)
                for buffer, value_rows in zip(outputs, fresh)
            )
        )
        return (sums_out, outputs)

    sums_start = (
        jnp.zeros((features, features), single),
        jnp.zeros((features, features), single),
        jnp.zeros((features, features), single),
        jnp.zeros((features, hidden), single),
        jnp.zeros((hidden,), single),
        jnp.zeros((hidden, features), single),
        jnp.zeros((features,), single),
        jnp.zeros((features,), single),
        jnp.zeros((features,), single),
        jnp.zeros((features,), single),
        jnp.zeros((features,), single),
    )
    outputs_start = tuple((jnp.zeros(first_half.shape, single) for _ in range(4)))
    sums_end, outputs_end = lax.fori_loop(0, batches, one_batch, (sums_start, outputs_start))
    reduced = (
        lax.psum_scatter(sums_end[0], ("dp", "fsdp"), scatter_dimension=0, tiled=True),
        lax.psum_scatter(sums_end[1], ("dp", "fsdp"), scatter_dimension=0, tiled=True),
        lax.psum_scatter(sums_end[2], ("dp", "fsdp"), scatter_dimension=0, tiled=True),
        lax.psum_scatter(sums_end[3], ("dp", "fsdp"), scatter_dimension=0, tiled=True),
        lax.psum_scatter(sums_end[4], ("dp", "fsdp"), scatter_dimension=0, tiled=True),
        lax.psum_scatter(sums_end[5], ("dp", "fsdp"), scatter_dimension=0, tiled=True),
        lax.psum_scatter(sums_end[6], ("dp", "fsdp"), scatter_dimension=0, tiled=True),
        lax.psum_scatter(sums_end[7], ("dp", "fsdp"), scatter_dimension=0, tiled=True),
        lax.psum_scatter(sums_end[8], ("dp", "fsdp"), scatter_dimension=0, tiled=True),
        lax.psum_scatter(sums_end[9], ("dp", "fsdp"), scatter_dimension=0, tiled=True),
        lax.psum_scatter(sums_end[10], ("dp", "fsdp"), scatter_dimension=0, tiled=True),
    )
    return (
        outputs_end[0],
        outputs_end[1],
        outputs_end[2],
        outputs_end[3],
        reduced[0],
        reduced[1],
        reduced[2],
        reduced[3],
        reduced[4],
        reduced[5],
        reduced[6],
        reduced[7],
        reduced[8],
        reduced[9],
        reduced[10],
    )


def solution(mesh):
    return jax.shard_map(
        per_device,
        mesh=mesh,
        in_specs=(
            P(None, "dp", "fsdp", None),
            P(None, "dp", "fsdp", None),
            P(None, "dp", "fsdp", None),
            P(None, "dp", "fsdp", None),
            P(("dp", "fsdp"), None),
            P(("dp", "fsdp"), None),
            P(("dp", "fsdp"), None),
            P(("dp", "fsdp"), None),
            P(("dp", "fsdp")),
            P(("dp", "fsdp"), None),
            P(("dp", "fsdp")),
            P(("dp", "fsdp")),
            P(("dp", "fsdp")),
            P(("dp", "fsdp")),
            P(("dp", "fsdp")),
            P(None, "dp", None),
            P(None, "dp", None, None),
            P(None, "dp", None, None),
        ),
        out_specs=(
            P(None, "dp", "fsdp", None),
            P(None, "dp", "fsdp", None),
            P(None, "dp", "fsdp", None),
            P(None, "dp", "fsdp", None),
            P(("dp", "fsdp"), None),
            P(("dp", "fsdp"), None),
            P(("dp", "fsdp"), None),
            P(("dp", "fsdp"), None),
            P(("dp", "fsdp")),
            P(("dp", "fsdp"), None),
            P(("dp", "fsdp")),
            P(("dp", "fsdp")),
            P(("dp", "fsdp")),
            P(("dp", "fsdp")),
            P(("dp", "fsdp")),
        ),
        check_vma=False,
    )
```

profile of v0, /device:TPU:0, one launch (start us, length us, event | category | flops | bytes accessed | tf_op | source)
XLA Modules:
  0.0 2555.4 jit_solution(1333209142435961352)
XLA Ops:
  8.2 1746.9 %while.45 = (s32[]{:T(128)}, f32[1024,1024]{1,0:T(8,128)}, f32[1024,1024]{1,0:T(8,128)}, f32[1024,1024]{1,0:T(8,128)}, f32[1024,4096]{1,0:T(8,128)}, /*index=5*/...) while((s32[]{:T(128)}, f32[1024,1024]{1,0:T(8,128)}, ...), condition=%wide.region_30.33_spmd.clone, body=%wide.region_0.32_spmd.clone.sunk | while | flops 30479316992 | bytes 1245874560 | solution.py:338
  14.2 42.2 %all-reduce.19 = (bf16[1024]{0:T(1024)(128)(2,1)S(1)}, bf16[1024]{0:T(1024)(128)(2,1)S(1)}, bf16[1024]{0:T(1024)(128)(2,1)S(1)}, bf16[1024]{0:T(1024)(128)(2,1)}, bf16[1024]{0:T(1024)(128)(2,1)}) all-reduce(bf16[1024]{0:T(1024)(128)(2,1)S(1)} %dynamic-update-slice.15, ...), channel_id=1, replica_groups=mesh['dp'=8,'fsdp'=4] {'dp','fsdp'}, use_global_device_ids=true, to_apply=%add.1 | all-reduce | flops 5120 | bytes 20480 | tf_op jit(solution)/shard_map/while
  74.7 54.8 %all-gather.21.cloned.1.call-done = bf16[1024,1024]{1,0:T(8,128)(2,1)} async-done(((bf16[32,1024]{1,0:T(8,128)(2,1)}), bf16[1024,1024]{1,0:T(8,128)(2,1)}) %all-gather.21.cloned.1.call-update) | async-done | bytes 2097168 | tf_op jit(solution)/shard_map/while/body/eval_jaxpr/all_gather | solution.py:111
  134.0 19.9 scatter_custom_fusion.30
  156.7 43.6 %gather_fusion = s32[5120]{0:T(1024)S(1)} fusion(s32[4,1280]{1,0:T(4,128)S(1)} %dynamic-slice_bitcast_fusion.6, s32[5120]{0:T(1024)S(1)} %reshape.1010), kind=kCustom, calls=%fused_computation.7.clone.clone.1 | custom fusion | bytes 81920 | tf_op jit(solution)/shard_map/while/body/eval_jaxpr/jit(take_along_axis)/gather | solution.py:132
  247.7 13.1 fusion.244
  271.6 18.6 all_gather.209
  291.9 50.5 %gather_fusion.4 = f32[5120,8]{1,0:T(8,128)S(1)} fusion(f32[4,8,1280]{1,2,0:T(8,128)} %copy.263, s32[5120]{0:T(1024)S(1)} %reshape.1015), kind=kCustom, calls=%fused_computation.clone.clone.1 | custom fusion | bytes 368640 | tf_op jit(solution)/shard_map/while/body/eval_jaxpr/jit(take_along_axis)/gather | solution.py:164
  343.5 13.0 gather_fusion.3
  382.8 19.1 scatter_custom_fusion.31
  407.9 39.3 %all-gather.6 = bf16[32,1,128]{2,1,0:T(2,128)(2,1)S(1)} all-gather(bf16[1,1,128]{2,1,0:T(2,128)(2,1)S(1)} %bitcast.411), channel_id=1, replica_groups=mesh['dp'=8,'fsdp'=4] {'dp','fsdp'}, dimensions={0}, use_global_device_ids=true | all-gather | bytes 8448 | tf_op jit(solution)/shard_map/while/body/eval_jaxpr/all_gather | solution.py:114
  452.4 68.8 %all-gather.27.cloned.1.call-done = bf16[4096,1024]{1,0:T(8,128)(2,1)} async-done(((bf16[128,1024]{1,0:T(8,128)(2,1)}), bf16[4096,1024]{1,0:T(8,128)(2,1)}) %all-gather.27.cloned.1.call-update) | async-done | bytes 8388624 | tf_op jit(solution)/shard_map/while/body/eval_jaxpr/all_gather | solution.py:208
  532.3 68.3 %all-gather.29.cloned.1.call-done = bf16[1024,4096]{1,0:T(8,128)(2,1)} async-done(((bf16[32,4096]{1,0:T(8,128)(2,1)}), bf16[1024,4096]{1,0:T(8,128)(2,1)}) %all-gather.29.cloned.1.call-update) | async-done | bytes 8388624 | tf_op jit(solution)/shard_map/while/body/eval_jaxpr/all_gather | solution.py:113
  600.7 13.9 convert_reduce_fusion.5
  634.7 13.1 all-gather.31.cloned.1.call-done
  660.7 16.4 select_convert_fusion.2
  702.6 19.0 scatter_custom_fusion.32
  721.6 12.2 add_add_fusion.6
  744.0 25.8 %scatter_custom_fusion.33 = f32[1280,1024]{1,0:T(8,128)} fusion(f32[1280,1024]{1,0:T(8,128)} %scatter_custom_fusion.32, s32[2048]{0:T(1024)S(1)} %bitcast.409, f32[256,8,8,128]{3,2,1,0:T(8,128)} %bitcast.385), kind=kCustom, calls=%fused_computation.25.clone.1 | custom fusion | flops 2097152 | bytes 13631488 | tf_op jit(solution)/shard_map/while/body/eval_jaxpr/scatter-add | solution.py:278
  775.8 14.9 convolution_bitcast_fusion.5
  800.8 23.9 scatter_custom_fusion.34
  883.1 39.7 %all-reduce.19 = (bf16[1024]{0:T(1024)(128)(2,1)S(1)}, bf16[1024]{0:T(1024)(128)(2,1)S(1)}, bf16[1024]{0:T(1024)(128)(2,1)S(1)}, bf16[1024]{0:T(1024)(128)(2,1)}, bf16[1024]{0:T(1024)(128)(2,1)}) all-reduce(bf16[1024]{0:T(1024)(128)(2,1)S(1)} %dynamic-update-slice.15, ...), channel_id=1, replica_groups=mesh['dp'=8,'fsdp'=4] {'dp','fsdp'}, use_global_device_ids=true, to_apply=%add.1 | all-reduce | flops 5120 | bytes 20480 | tf_op jit(solution)/shard_map/while
  940.8 54.8 %all-gather.21.cloned.1.call-done = bf16[1024,1024]{1,0:T(8,128)(2,1)} async-done(((bf16[32,1024]{1,0:T(8,128)(2,1)}), bf16[1024,1024]{1,0:T(8,128)(2,1)}) %all-gather.21.cloned.1.call-update) | async-done | bytes 2097168 | tf_op jit(solution)/shard_map/while/body/eval_jaxpr/all_gather | solution.py:111
  1000.0 19.7 scatter_custom_fusion.30
  1022.6 43.6 %gather_fusion = s32[5120]{0:T(1024)S(1)} fusion(s32[4,1280]{1,0:T(4,128)S(1)} %dynamic-slice_bitcast_fusion.6, s32[5120]{0:T(1024)S(1)} %reshape.1010), kind=kCustom, calls=%fused_computation.7.clone.clone.1 | custom fusion | bytes 81920 | tf_op jit(solution)/shard_map/while/body/eval_jaxpr/jit(take_along_axis)/gather | solution.py:132
  1113.6 13.1 fusion.244
  1137.4 18.7 all_gather.209
  1157.8 50.6 %gather_fusion.4 = f32[5120,8]{1,0:T(8,128)S(1)} fusion(f32[4,8,1280]{1,2,0:T(8,128)} %copy.263, s32[5120]{0:T(1024)S(1)} %reshape.1015), kind=kCustom, calls=%fused_computation.clone.clone.1 | custom fusion | bytes 368640 | tf_op jit(solution)/shard_map/while/body/eval_jaxpr/jit(take_along_axis)/gather | solution.py:164
  1209.4 13.0 gather_fusion.3
  1248.7 19.1 scatter_custom_fusion.31
  1273.6 39.3 %all-gather.6 = bf16[32,1,128]{2,1,0:T(2,128)(2,1)S(1)} all-gather(bf16[1,1,128]{2,1,0:T(2,128)(2,1)S(1)} %bitcast.411), channel_id=1, replica_groups=mesh['dp'=8,'fsdp'=4] {'dp','fsdp'}, dimensions={0}, use_global_device_ids=true | all-gather | bytes 8448 | tf_op jit(solution)/shard_map/while/body/eval_jaxpr/all_gather | solution.py:114
  1318.1 68.9 %all-gather.27.cloned.1.call-done = bf16[4096,1024]{1,0:T(8,128)(2,1)} async-done(((bf16[128,1024]{1,0:T(8,128)(2,1)}), bf16[4096,1024]{1,0:T(8,128)(2,1)}) %all-gather.27.cloned.1.call-update) | async-done | bytes 8388624 | tf_op jit(solution)/shard_map/while/body/eval_jaxpr/all_gather | solution.py:208
  1398.1 68.3 %all-gather.29.cloned.1.call-done = bf16[1024,4096]{1,0:T(8,128)(2,1)} async-done(((bf16[32,4096]{1,0:T(8,128)(2,1)}), bf16[1024,4096]{1,0:T(8,128)(2,1)}) %all-gather.29.cloned.1.call-update) | async-done | bytes 8388624 | tf_op jit(solution)/shard_map/while/body/eval_jaxpr/all_gather | solution.py:113
  1466.4 13.9 convert_reduce_fusion.5
  1500.4 13.1 all-gather.31.cloned.1.call-done
  1526.4 16.4 select_convert_fusion.2
  1568.3 19.0 scatter_custom_fusion.32
  1587.4 12.2 add_add_fusion.6
  1609.7 25.8 %scatter_custom_fusion.33 = f32[1280,1024]{1,0:T(8,128)} fusion(f32[1280,1024]{1,0:T(8,128)} %scatter_custom_fusion.32, s32[2048]{0:T(1024)S(1)} %bitcast.409, f32[256,8,8,128]{3,2,1,0:T(8,128)} %bitcast.385), kind=kCustom, calls=%fused_computation.25.clone.1 | custom fusion | flops 2097152 | bytes 13631488 | tf_op jit(solution)/shard_map/while/body/eval_jaxpr/scatter-add | solution.py:278
  1641.5 14.9 convolution_bitcast_fusion.5
  1666.5 23.9 scatter_custom_fusion.34
  1710.2 13.6 select_add_fusion.25
  1758.4 40.7 %all-reduce.17 = (f32[4096]{0:T(1024)S(1)}, f32[1024]{0:T(1024)S(1)}, f32[1024]{0:T(1024)S(1)}, f32[1024]{0:T(1024)S(1)}, f32[1024]{0:T(1024)S(1)}, /*index=5*/f32[1024]{0:T(1024)S(1)}) all-reduce(f32[4096]{0:T(1024)S(1)} %copy-done.43, f32[1024]{0:T(1024)S(1)} %copy-done.66, ...), channel_id=9, replica_groups=mesh['dp'=8,'fsdp'=4] {'dp','fsdp'}, use_global_device_ids=true, to_apply=%region_35.38.clone | all-reduce | flops 9216 | bytes 73728
  1802.6 97.2 %reduce-scatter.9.cloned.1.call-done = f32[32,1024]{1,0:T(8,128)} async-done(((f32[1024,1024]{1,0:T(8,128)}), f32[32,1024]{1,0:T(8,128)}) %reduce-scatter.9.cloned.1.call-update) | async-done | bytes 131088 | tf_op jit(solution)/shard_map/reduce_scatter | solution.py:340
  1899.8 139.3 %reduce-scatter.11.cloned.1.call-done = f32[32,1024]{1,0:T(8,128)} async-done(((f32[1024,1024]{1,0:T(8,128)}), f32[32,1024]{1,0:T(8,128)}) %reduce-scatter.11.cloned.1.call-update) | async-done | bytes 131088 | tf_op jit(solution)/shard_map/reduce_scatter | solution.py:341
  2039.1 139.3 %reduce-scatter.13.cloned.1.call-done = f32[32,1024]{1,0:T(8,128)} async-done(((f32[1024,1024]{1,0:T(8,128)}), f32[32,1024]{1,0:T(8,128)}) %reduce-scatter.13.cloned.1.call-update) | async-done | bytes 131088 | tf_op jit(solution)/shard_map/reduce_scatter | solution.py:342
  2178.4 181.7 %reduce-scatter.15.cloned.1.call-done = f32[32,4096]{1,0:T(8,128)} async-done(((f32[1024,4096]{1,0:T(8,128)}), f32[32,4096]{1,0:T(8,128)}) %reduce-scatter.15.cloned.1.call-update) | async-done | bytes 524304 | tf_op jit(solution)/shard_map/reduce_scatter | solution.py:343
  2360.1 187.4 %reduce-scatter.17.cloned.1.call-done = f32[128,1024]{1,0:T(8,128)} async-done(((f32[4096,1024]{1,0:T(8,128)}), f32[128,1024]{1,0:T(8,128)}) %reduce-scatter.17.cloned.1.call-update) | async-done | bytes 524304 | tf_op jit(solution)/shard_map/reduce_scatter | solution.py:345
  (708 shorter events, 555.9 us)
Async XLA Ops:
  8.5 62.8 %all-gather.17.cloned.1.call-start = ((), (), s32[]{:S(2)}) async-start(), calls=%async_computation.13 | async-start | bytes 2162688 | tf_op jit(solution)/shard_map/while/body/eval_jaxpr/all_gather | solution.py:203
  9.2 120.3 %all-gather.21.cloned.1.call-start = ((), (), s32[]{:S(2)}) async-start(), calls=%async_computation.15 | async-start | bytes 2162688 | tf_op jit(solution)/shard_map/while/body/eval_jaxpr/all_gather | solution.py:111
  10.0 193.8 %all-gather.19.cloned.1.call-start = ((), (), s32[]{:S(2)}) async-start(), calls=%async_computation.14 | async-start | bytes 3276800 | tf_op jit(solution)/shard_map/while/body/eval_jaxpr/all_gather | solution.py:246
  62.4 70.4 %copy-start.10 = (bf16[320,1024]{1,0:T(8,128)(2,1)}, bf16[320,1024]{1,0:T(8,128)(2,1)S(1)}, u32[]{:S(2)}) copy-start(bf16[320,1024]{1,0:T(8,128)(2,1)S(1)} %add_convert_fusion.7) | copy-start | bytes 1966084 | tf_op jit(solution)/shard_map/while
  74.6 58.8 %copy-start.30 = (s32[2,1,4,1280]{3,2,1,0:T(4,128)S(1)}, s32[2,1,4,1280]{3,2,1,0:T(4,128)}, u32[]{:S(2)}) copy-start(s32[2,1,4,1280]{3,2,1,0:T(4,128)} %get-tuple-element.1692) | copy-start | bytes 122884 | tf_op jit(solution)/shard_map/while
  74.6 59.1 %copy-start.72 = (s32[2]{0:T(128)S(1)}, s32[2]{0:T(128)}, u32[]{:S(2)}) copy-start(s32[2]{0:T(128)} %get-tuple-element.1716) | copy-start | bytes 28 | tf_op jit(solution)/shard_map/while
  74.6 59.2 %copy-start.71 = (s32[2]{0:T(128)S(1)}, s32[2]{0:T(128)}, u32[]{:S(2)}) copy-start(s32[2]{0:T(128)} %get-tuple-element.1717) | copy-start | bytes 28 | tf_op jit(solution)/shard_map/while
  74.6 79.9 %copy-start.80 = (s32[2,1,10]{2,1,0:T(1,128)S(1)}, s32[2,1,10]{2,1,0:T(1,128)}, u32[]{:S(2)}) copy-start(s32[2,1,10]{2,1,0:T(1,128)} %get-tuple-element.1700) | copy-start | bytes 244 | tf_op jit(solution)/shard_map/while
  74.7 82.1 %copy-start.51 = (s32[2,1,4,1280]{3,2,1,0:T(4,128)S(1)}, s32[2,1,4,1280]{3,2,1,0:T(4,128)}, u32[]{:S(2)}) copy-start(s32[2,1,4,1280]{3,2,1,0:T(4,128)} %get-tuple-element.1698) | copy-start | bytes 122884 | tf_op jit(solution)/shard_map/while
  74.7 268.8 %all-gather.23.cloned.1.call-start = ((), (), s32[]{:S(2)}) async-start(), calls=%async_computation.16 | async-start | bytes 3276800 | tf_op jit(solution)/shard_map/while/body/eval_jaxpr/all_gather | solution.py:177
  132.8 315.9 %all-gather.25.cloned.1.call-start = ((), (), s32[]{:S(2)}) async-start(), calls=%async_computation.18 | async-start | bytes 2162688 | tf_op jit(solution)/shard_map/while/body/eval_jaxpr/all_gather | solution.py:112
  133.4 315.4 %reduce-scatter.19.cloned.1.call-start = ((), (), s32[]{:S(2)}) async-start(), calls=%async_computation.17 | async-start | bytes 3276800 | tf_op jit(solution)/shard_map/while/body/eval_jaxpr/reduce_scatter | solution.py:187
  133.5 232.2 %copy-start.49 = (pred[4,320]{1,0:T(4,128)(4,1)}, pred[4,320]{1,0:T(4,128)(4,1)S(1)}, u32[]{:S(2)}) copy-start(pred[4,320]{1,0:T(4,128)(4,1)S(1)} %get-tuple-element.1551) | copy-start | bytes 3844 | tf_op jit(solution)/shard_map/while
  203.8 57.1 %copy-start.22 = (pred[4,320,512]{2,1,0:T(8,128)(4,1)}, pred[4,320,512]{2,1,0:T(8,128)(4,1)S(1)}, u32[]{:S(2)}) copy-start(pred[4,320,512]{2,1,0:T(8,128)(4,1)S(1)} %get-tuple-element.1546) | copy-start | bytes 1966084 | tf_op jit(solution)/shard_map/while
  290.2 52.2 %copy-start.35 = (pred[4,1280]{1,0:T(4,128)(4,1)S(1)}, pred[4,1280]{1,0:T(4,128)(4,1)}, u32[]{:S(2)}) copy-start(pred[4,1280]{1,0:T(4,128)(4,1)} %and_bitcast_fusion.2) | copy-start | bytes 15364 | tf_op jit(solution)/shard_map/while
  406.3 114.9 %all-gather.27.cloned.1.call-start = ((), (), s32[]{:S(2)}) async-start(), calls=%async_computation.19 | async-start | bytes 8650752 | tf_op jit(solution)/shard_map/while/body/eval_jaxpr/all_gather | solution.py:208
  407.0 193.6 %all-gather.29.cloned.1.call-start = ((), (), s32[]{:S(2)}) async-start(), calls=%async_computation.20 | async-start | bytes 8650752 | tf_op jit(solution)/shard_map/while/body/eval_jaxpr/all_gather | solution.py:113
  407.8 240.0 %all-gather.31.cloned.1.call-start = ((), (), s32[]{:S(2)}) async-start(), calls=%async_computation.21 | async-start | bytes 3276800 | tf_op jit(solution)/shard_map/while/body/eval_jaxpr/all_gather | solution.py:236
  448.7 83.6 %copy-start.13 = (bf16[320,1024]{1,0:T(8,128)(2,1)}, bf16[320,1024]{1,0:T(8,128)(2,1)S(1)}, u32[]{:S(2)}) copy-start(bf16[320,1024]{1,0:T(8,128)(2,1)S(1)} %get-tuple-element.1555) | copy-start | bytes 1966084 | tf_op jit(solution)/shard_map/while
  623.5 236.3 %reduce-scatter.21.cloned.1.call-start = ((), (), s32[]{:S(2)}) async-start(), calls=%async_computation.22 | async-start | bytes 3276800 | tf_op jit(solution)/shard_map/while/body/eval_jaxpr/reduce_scatter | solution.py:282
  774.4 89.7 %reduce-scatter.23.cloned.1.call-start = ((), (), s32[]{:S(2)}) async-start(), calls=%async_computation.23 | async-start | bytes 3276800 | tf_op jit(solution)/shard_map/while/body/eval_jaxpr/reduce_scatter | solution.py:285
  877.5 59.9 %all-gather.17.cloned.1.call-start = ((), (), s32[]{:S(2)}) async-start(), calls=%async_computation.13 | async-start | bytes 2162688 | tf_op jit(solution)/shard_map/while/body/eval_jaxpr/all_gather | solution.py:203
  878.1 117.4 %all-gather.21.cloned.1.call-start = ((), (), s32[]{:S(2)}) async-start(), calls=%async_computation.15 | async-start | bytes 2162688 | tf_op jit(solution)/shard_map/while/body/eval_jaxpr/all_gather | solution.py:111
  878.9 190.8 %all-gather.19.cloned.1.call-start = ((), (), s32[]{:S(2)}) async-start(), calls=%async_computation.14 | async-start | bytes 3276800 | tf_op jit(solution)/shard_map/while/body/eval_jaxpr/all_gather | solution.py:246
  928.7 70.1 %copy-start.10 = (bf16[320,1024]{1,0:T(8,128)(2,1)}, bf16[320,1024]{1,0:T(8,128)(2,1)S(1)}, u32[]{:S(2)}) copy-start(bf16[320,1024]{1,0:T(8,128)(2,1)S(1)} %add_convert_fusion.7) | copy-start | bytes 1966084 | tf_op jit(solution)/shard_map/while
  940.7 58.8 %copy-start.30 = (s32[2,1,4,1280]{3,2,1,0:T(4,128)S(1)}, s32[2,1,4,1280]{3,2,1,0:T(4,128)}, u32[]{:S(2)}) copy-start(s32[2,1,4,1280]{3,2,1,0:T(4,128)} %get-tuple-element.1692) | copy-start | bytes 122884 | tf_op jit(solution)/shard_map/while
  940.7 59.1 %copy-start.72 = (s32[2]{0:T(128)S(1)}, s32[2]{0:T(128)}, u32[]{:S(2)}) copy-start(s32[2]{0:T(128)} %get-tuple-element.1716) | copy-start | bytes 28 | tf_op jit(solution)/shard_map/while
  940.7 59.2 %copy-start.71 = (s32[2]{0:T(128)S(1)}, s32[2]{0:T(128)}, u32[]{:S(2)}) copy-start(s32[2]{0:T(128)} %get-tuple-element.1717) | copy-start | bytes 28 | tf_op jit(solution)/shard_map/while
  940.7 79.7 %copy-start.80 = (s32[2,1,10]{2,1,0:T(1,128)S(1)}, s32[2,1,10]{2,1,0:T(1,128)}, u32[]{:S(2)}) copy-start(s32[2,1,10]{2,1,0:T(1,128)} %get-tuple-element.1700) | copy-start | bytes 244 | tf_op jit(solution)/shard_map/while
  940.7 81.9 %copy-start.51 = (s32[2,1,4,1280]{3,2,1,0:T(4,128)S(1)}, s32[2,1,4,1280]{3,2,1,0:T(4,128)}, u32[]{:S(2)}) copy-start(s32[2,1,4,1280]{3,2,1,0:T(4,128)} %get-tuple-element.1698) | copy-start | bytes 122884 | tf_op jit(solution)/shard_map/while
  940.7 268.7 %all-gather.23.cloned.1.call-start = ((), (), s32[]{:S(2)}) async-start(), calls=%async_computation.16 | async-start | bytes 3276800 | tf_op jit(solution)/shard_map/while/body/eval_jaxpr/all_gather | solution.py:177
  998.8 315.6 %all-gather.25.cloned.1.call-start = ((), (), s32[]{:S(2)}) async-start(), calls=%async_computation.18 | async-start | bytes 2162688 | tf_op jit(solution)/shard_map/while/body/eval_jaxpr/all_gather | solution.py:112
  999.4 315.0 %reduce-scatter.19.cloned.1.call-start = ((), (), s32[]{:S(2)}) async-start(), calls=%async_computation.17 | async-start | bytes 3276800 | tf_op jit(solution)/shard_map/while/body/eval_jaxpr/reduce_scatter | solution.py:187
  999.6 232.1 %copy-start.49 = (pred[4,320]{1,0:T(4,128)(4,1)}, pred[4,320]{1,0:T(4,128)(4,1)S(1)}, u32[]{:S(2)}) copy-start(pred[4,320]{1,0:T(4,128)(4,1)S(1)} %get-tuple-element.1551) | copy-start | bytes 3844 | tf_op jit(solution)/shard_map/while
  1069.6 57.1 %copy-start.22 = (pred[4,320,512]{2,1,0:T(8,128)(4,1)}, pred[4,320,512]{2,1,0:T(8,128)(4,1)S(1)}, u32[]{:S(2)}) copy-start(pred[4,320,512]{2,1,0:T(8,128)(4,1)S(1)} %get-tuple-element.1546) | copy-start | bytes 1966084 | tf_op jit(solution)/shard_map/while
  1156.1 52.2 %copy-start.35 = (pred[4,1280]{1,0:T(4,128)(4,1)S(1)}, pred[4,1280]{1,0:T(4,128)(4,1)}, u32[]{:S(2)}) copy-start(pred[4,1280]{1,0:T(4,128)(4,1)} %and_bitcast_fusion.2) | copy-start | bytes 15364 | tf_op jit(solution)/shard_map/while
  1272.2 114.7 %all-gather.27.cloned.1.call-start = ((), (), s32[]{:S(2)}) async-start(), calls=%async_computation.19 | async-start | bytes 8650752 | tf_op jit(solution)/shard_map/while/body/eval_jaxpr/all_gather | solution.py:208
  1272.8 193.6 %all-gather.29.cloned.1.call-start = ((), (), s32[]{:S(2)}) async-start(), calls=%async_computation.20 | async-start | bytes 8650752 | tf_op jit(solution)/shard_map/while/body/eval_jaxpr/all_gather | solution.py:113
  1273.5 240.0 %all-gather.31.cloned.1.call-start = ((), (), s32[]{:S(2)}) async-start(), calls=%async_computation.21 | async-start | bytes 3276800 | tf_op jit(solution)/shard_map/while/body/eval_jaxpr/all_gather | solution.py:236
  1314.4 83.7 %copy-start.13 = (bf16[320,1024]{1,0:T(8,128)(2,1)}, bf16[320,1024]{1,0:T(8,128)(2,1)S(1)}, u32[]{:S(2)}) copy-start(bf16[320,1024]{1,0:T(8,128)(2,1)S(1)} %get-tuple-element.1555) | copy-start | bytes 1966084 | tf_op jit(solution)/shard_map/while
  1489.2 246.7 %reduce-scatter.21.cloned.1.call-start = ((), (), s32[]{:S(2)}) async-start(), calls=%async_computation.22 | async-start | bytes 3276800 | tf_op jit(solution)/shard_map/while/body/eval_jaxpr/reduce_scatter | solution.py:282
  1640.1 99.7 %reduce-scatter.23.cloned.1.call-start = ((), (), s32[]{:S(2)}) async-start(), calls=%async_computation.23 | async-start | bytes 3276800 | tf_op jit(solution)/shard_map/while/body/eval_jaxpr/reduce_scatter | solution.py:285
  1700.8 23.0 slice-start.2
  1755.1 144.7 %reduce-scatter.9.cloned.1.call-start = ((), (), s32[]{:S(2)}) async-start(), calls=%async_computation.8 | async-start | bytes 4325376 | tf_op jit(solution)/shard_map/reduce_scatter | solution.py:340
  1755.7 283.4 %reduce-scatter.11.cloned.1.call-start = ((), (), s32[]{:S(2)}) async-start(), calls=%async_computation.9 | async-start | bytes 4325376 | tf_op jit(solution)/shard_map/reduce_scatter | solution.py:341
  1756.3 422.0 %reduce-scatter.13.cloned.1.call-start = ((), (), s32[]{:S(2)}) async-start(), calls=%async_computation.10 | async-start | bytes 4325376 | tf_op jit(solution)/shard_map/reduce_scatter | solution.py:342
  1756.9 603.2 %reduce-scatter.15.cloned.1.call-start = ((), (), s32[]{:S(2)}) async-start(), calls=%async_computation.11 | async-start | bytes 17301504 | tf_op jit(solution)/shard_map/reduce_scatter | solution.py:343
  1757.6 789.9 %reduce-scatter.17.cloned.1.call-start = ((), (), s32[]{:S(2)}) async-start(), calls=%async_computation.12 | async-start | bytes 17301504 | tf_op jit(solution)/shard_map/reduce_scatter | solution.py:345
  (147 other events, 765.6 us)
Sparse Core Ops, SparseCore 0:
  12.2 59.1 all-gather.16
  74.2 55.2 all-gather.20
  131.1 24.4 all-gather.18
  156.9 25.5 all-gather.22
  185.2 56.4 all-gather.24
  406.4 33.9 reduce-scatter.18
  443.6 77.5 all-gather.26
  524.5 76.1 all-gather.28
  623.6 24.1 all-gather.30
  774.5 34.6 reduce-scatter.20
  829.4 34.6 reduce-scatter.22
  880.9 56.4 all-gather.16
  940.3 55.2 all-gather.20
  997.0 24.4 all-gather.18
  1022.8 25.5 all-gather.22
  1051.1 56.3 all-gather.24
  1272.3 33.8 reduce-scatter.18
  1309.3 77.5 all-gather.26
  1390.2 76.1 all-gather.28
  1489.4 24.1 all-gather.30
  1640.2 34.6 reduce-scatter.20
  1695.1 34.6 reduce-scatter.22
Sparse Core Ops, SparseCore 1:
  1758.5 141.3 reduce-scatter.8
  1902.6 136.5 reduce-scatter.10
  2041.8 136.5 reduce-scatter.12
  2181.2 178.8 reduce-scatter.14
  2363.0 184.5 reduce-scatter.16
where the time goes:
time: 2560 us
  waiting for transfers between devices  1180 us (46%)
  local copies, waits for them, and re-layouts  479 us (19%)
  matrix products  333 us (13%)
  other arithmetic  289 us (11%)
  blocking collectives  249 us (10%)
    reduce_scatter x1, waiting for transfers between devices, per_device(): lax.psum_scatter(sums_end[5], ('dp', 'fsdp'), scatter_dimension=0, tiled=...  187 us
    reduce_scatter x1, waiting for transfers between devices, per_device(): lax.psum_scatter(sums_end[3], ('dp', 'fsdp'), scatter_dimension=0, tiled=...  182 us
    reduce_scatter x1, waiting for transfers between devices, per_device(): lax.psum_scatter(sums_end[1], ('dp', 'fsdp'), scatter_dimension=0, tiled=...  139 us
    reduce_scatter x1, waiting for transfers between devices, per_device(): lax.psum_scatter(sums_end[2], ('dp', 'fsdp'), scatter_dimension=0, tiled=...  139 us
    all_gather x2, waiting for transfers between devices, one_batch(): lax.all_gather(shards[5], ('dp', 'fsdp'), axis=0, tiled=True)  138 us
    all_gather x2, waiting for transfers between devices, one_batch(): lax.all_gather(shards[3], ('dp', 'fsdp'), axis=0, tiled=True)  137 us
    all_gather x2, waiting for transfers between devices, one_batch(): lax.all_gather(shards[1], ('dp', 'fsdp'), axis=0, tiled=True)  110 us
    while x366, local copies, waits for them, and re-layouts  105 us
  transfers between devices with their start and end apart: 27, of which 16 were waited for; matrix products, arithmetic and copies ran while one was open for 30% of the time, Pallas kernels for 0%

commit v1 on v0

v1 whole, which is shorter than its diff:
```python
import functools
import math

import jax
import jax.numpy as jnp
from jax import lax
from jax.experimental import pallas as pl
from jax.experimental.pallas import tpu as pltpu
from jax.sharding import PartitionSpec as P

H = 8
DH = 128
CH = 64
SEG = 128
TRUNK = 4
BRANCHES = 2
NBUCK = 32
SELF_SCORE = -10000.0
NEG_SCORE = -1e30
EPSILON = 1e-06
BF = jnp.bfloat16
F32 = jnp.float32
AXES = ("dp", "fsdp")
GELU_A = math.sqrt(2.0 / math.pi)
GELU_B = 0.044715


def norm_stats(values):
    center = values - jnp.mean(values, axis=-1, keepdims=True)
    factor = lax.rsqrt(jnp.mean(center * center, axis=-1, keepdims=True) + EPSILON)
    return center * factor, factor


def norm_back(unit, factor, gain_vec, grad):
    scaled = grad * gain_vec
    inner = jnp.mean(scaled * unit, axis=-1, keepdims=True)
    return factor * (scaled - jnp.mean(scaled, axis=-1, keepdims=True) - unit * inner)


def position_codes(bucket_rows):
    rounds, tree_len = bucket_rows.shape
    buckets_t = bucket_rows.T
    lanes = jnp.arange(rounds * NBUCK, dtype=jnp.int32)
    member = (jnp.repeat(buckets_t, NBUCK, axis=1) == (lanes % NBUCK)[None, :]).astype(F32)
    rows = jnp.arange(tree_len, dtype=jnp.int32)
    lower = (rows[:, None] >= rows[None, :]).astype(BF)
    ranks = jnp.dot(lower, member.astype(BF), preferred_element_type=F32)
    totals = ranks[-1]
    before = ((lanes[:, None] // NBUCK == lanes[None, :] // NBUCK) & (lanes[:, None] < lanes[None, :])).astype(F32)
    offsets = jnp.sum(totals[:, None] * before, axis=0)
    places = jnp.sum((member * (ranks - 1.0 + offsets[None, :])).reshape(tree_len, rounds, NBUCK), axis=-1)
    return buckets_t.astype(F32) * tree_len + jnp.floor((places + 0.5) / CH)


def seg_parts(seg, info_ref):
    parts = []
    prefix = min(seg, TRUNK) * SEG
    if prefix:
        parts.append((0, prefix, 0, False))
    if seg >= TRUNK + BRANCHES:
        start = pl.multiple_of(info_ref[seg] * SEG, SEG)
        parts.append((start, SEG, TRUNK * SEG, False))
    parts.append((seg * SEG, SEG, (TRUNK + 1) * SEG, True))
    return parts


def unit_rows(rows_f32):
    factor = lax.rsqrt(jnp.mean(rows_f32 * rows_f32, axis=-1, keepdims=True) + EPSILON)
    return rows_f32 * factor * (1.0 / math.sqrt(DH)), factor


def own_diagonal():
    row = lax.broadcasted_iota(jnp.int32, (SEG, SEG), 0)
    col = lax.broadcasted_iota(jnp.int32, (SEG, SEG), 1)
    return row == col


def attention_forward_kernel(segments, rounds, info_ref, q_ref, v_ref, cq_ref, ck_ref, out_ref, total_ref, count_ref, unit_ref):
    head = pl.program_id(0)

    @pl.when(head == 0)
    def _():
        row = lax.broadcasted_iota(jnp.int32, (SEG, SEG), 0)
        col = lax.broadcasted_iota(jnp.int32, (SEG, SEG), 1)
        total_ref[...] = jnp.zeros_like(total_ref)
        for seg in range(segments):
            query = cq_ref[seg * SEG:(seg + 1) * SEG, :]
            for start, size, column, own in seg_parts(seg, info_ref):
                for piece in range(size // SEG):
                    first = start + piece * SEG
                    key = ck_ref[:, pl.ds(first, SEG)]
                    counted = jnp.zeros((SEG, SEG), F32)
                    for turn in range(rounds):
                        gap = query[:, turn:turn + 1] - key[turn:turn + 1, :]
                        counted = counted + jnp.where(jnp.abs(gap - 0.5) < 0.75, 1.0, 0.0)
                    if own:
                        counted = jnp.where(row >= col, counted, 0.0)
                    elif column == 0 and seg >= TRUNK:
                        counted = counted * jnp.where(info_ref[segments + seg] >= piece, 1.0, 0.0)
                    begin = column + piece * SEG
                    count_ref[seg * SEG:(seg + 1) * SEG, begin:begin + SEG] = counted.astype(BF)

    unit_ref[...] = unit_rows(q_ref[...].astype(F32))[0].astype(BF)
    diagonal = own_diagonal()
    lane = lax.broadcasted_iota(jnp.int32, (SEG, 128), 1)
    for seg in range(segments):
        rows = slice(seg * SEG, (seg + 1) * SEG)
        query = q_ref[rows, :]
        scored = []
        top = None
        for start, size, column, own in seg_parts(seg, info_ref):
            keys = pl.ds(start, size)
            scores = lax.dot_general(query, unit_ref[keys, :], (((1,), (1,)), ((), ())), preferred_element_type=F32)
            counted = count_ref[rows, column:column + size].astype(F32)
            if own:
                scores = jnp.where(diagonal, SELF_SCORE, scores)
            scores = jnp.where(counted > 0.0, scores, NEG_SCORE)
            best = jnp.max(scores, axis=-1, keepdims=True)
            top = best if top is None else jnp.maximum(top, best)
            scored.append((keys, scores, counted))
        amount = jnp.zeros((SEG, 1), F32)
        result = jnp.zeros((SEG, DH), F32)
        for keys, scores, counted in scored:
            weight = counted * jnp.exp(scores - top)
            amount = amount + jnp.sum(weight, axis=-1, keepdims=True)
            result = result + jnp.dot(weight.astype(BF), v_ref[keys, :], preferred_element_type=F32)
        out_ref[rows, :] = (result / amount).astype(BF)
        total = top + jnp.log(amount)
        total_ref[rows, :] = jnp.where(lane == head, total, total_ref[rows, :])


def attention_backward_kernel(segments, info_ref, q_ref, v_ref, out_ref, grad_ref, total_ref, count_ref, dq_ref, dv_ref, unit_ref, chance_ref, slope_ref, key_acc, value_acc, query_acc):
    head = pl.program_id(0)
    trunk = TRUNK * SEG
    whole = q_ref[...].astype(F32)
    unit, factor = unit_rows(whole)
    unit_ref[...] = unit.astype(BF)

    @pl.when(head == 0)
    def _():
        chance_ref[0:trunk, 0:trunk] = jnp.zeros((trunk, trunk), BF)
        slope_ref[0:trunk, 0:trunk] = jnp.zeros((trunk, trunk), BF)

    diagonal = own_diagonal()
    lane = lax.broadcasted_iota(jnp.int32, (SEG, 128), 1)
    for seg in range(segments):
        rows = slice(seg * SEG, (seg + 1) * SEG)
        query = q_ref[rows, :]
        grad = grad_ref[rows, :]
        total = jnp.sum(jnp.where(lane == head, total_ref[rows, :], 0.0), axis=-1, keepdims=True)
        delta = jnp.sum(grad.astype(F32) * out_ref[rows, :].astype(F32), axis=-1, keepdims=True)
        query_grad = jnp.zeros((SEG, DH), F32)
        for start, size, column, own in seg_parts(seg, info_ref):
            keys = pl.ds(start, size)
            scores = lax.dot_general(query, unit_ref[keys, :], (((1,), (1,)), ((), ())), preferred_element_type=F32)
            counted = count_ref[rows, column:column + size].astype(F32)
            if own:
                scores = jnp.where(diagonal, SELF_SCORE, scores)
            scores = jnp.where(counted > 0.0, scores, NEG_SCORE)
            chance = counted * jnp.exp(scores - total)
            reach = lax.dot_general(grad, v_ref[keys, :], (((1,), (1,)), ((), ())), preferred_element_type=F32)
            slope = chance * (reach - delta)
            if own:
                slope = jnp.where(diagonal, 0.0, slope)
            slope = slope.astype(BF)
            chance_ref[rows, column:column + size] = chance.astype(BF)
            slope_ref[rows, column:column + size] = slope
            query_grad = query_grad + jnp.dot(slope, unit_ref[keys, :], preferred_element_type=F32)
        query_acc[rows, :] = query_grad

    for weight_ref, side_ref, acc in ((chance_ref, grad_ref, value_acc), (slope_ref, q_ref, key_acc)):
        acc[0:trunk, :] = lax.dot_general(weight_ref[:, 0:trunk], side_ref[...], (((0,), (0,)), ((), ())), preferred_element_type=F32)
        for seg in range(segments):
            rows = slice(seg * SEG, (seg + 1) * SEG)
            leaf = seg >= TRUNK + BRANCHES
            begin = trunk if leaf else trunk + SEG
            added = lax.dot_general(weight_ref[rows, begin:trunk + 2 * SEG], side_ref[rows, :], (((0,), (0,)), ((), ())), preferred_element_type=F32)
            if leaf:
                above = pl.ds(pl.multiple_of(info_ref[seg] * SEG, SEG), SEG)
                acc[above, :] += added[0:SEG]
                added = added[SEG:]
            acc[rows, :] = added if seg >= TRUNK else acc[rows, :] + added

    key_grad = key_acc[...]
    along = jnp.mean(key_grad * whole, axis=-1, keepdims=True) * (factor * factor)
    dq_ref[...] = (query_acc[...] + (factor * (1.0 / math.sqrt(DH))) * (key_grad - whole * along)).astype(BF)
    dv_ref[...] = value_acc[...].astype(BF)


def attention_calls(tree_len, local_heads, rounds, segments):
    head_spec = pl.BlockSpec((tree_len, DH), lambda h, info: (0, h))
    side = pl.BlockSpec((tree_len, 128), lambda h, info: (0, 0))
    count_spec = pl.BlockSpec((tree_len, (TRUNK + 2) * SEG), lambda h, info: (0, 0))
    wide = local_heads * DH
    forward = pl.pallas_call(
        functools.partial(attention_forward_kernel, segments, rounds),
        grid_spec=pltpu.PrefetchScalarGridSpec(
            num_scalar_prefetch=1,
            grid=(local_heads,),
            in_specs=[head_spec, head_spec, side, pl.BlockSpec((8, tree_len), lambda h, info: (0, 0))],
            out_specs=[head_spec, side, count_spec],
            scratch_shapes=[pltpu.VMEM((tree_len, DH), BF)],
        ),
        out_shape=[
            jax.ShapeDtypeStruct((tree_len, wide), BF),
            jax.ShapeDtypeStruct((tree_len, 128), F32),
            jax.ShapeDtypeStruct((tree_len, (TRUNK + 2) * SEG), BF),
        ],
        compiler_params=pltpu.CompilerParams(vmem_limit_bytes=40 << 20),
        name="attention_forward",
    )
    backward = pl.pallas_call(
        functools.partial(attention_backward_kernel, segments),
        grid_spec=pltpu.PrefetchScalarGridSpec(
            num_scalar_prefetch=1,
            grid=(local_heads,),
            in_specs=[head_spec, head_spec, head_spec, head_spec, side, count_spec],
            out_specs=[head_spec, head_spec],
            scratch_shapes=[pltpu.VMEM((tree_len, DH), BF)]
            + [pltpu.VMEM((tree_len, (TRUNK + 2) * SEG), BF)] * 2
            + [pltpu.VMEM((tree_len, DH), F32)] * 3,
        ),
        out_shape=[jax.ShapeDtypeStruct((tree_len, wide), BF)] * 2,
        compiler_params=pltpu.CompilerParams(vmem_limit_bytes=40 << 20),
        name="attention_backward",
    )
    return forward, backward


def feed_kernel(feed_ref, grad_ref, inner_ref, bias_ref, outer_ref, out_ref, back_ref, inner_grad_ref, outer_grad_ref, bias_grad_ref):
    step = pl.program_id(0)

    @pl.when(step == 0)
    def _():
        out_ref[...] = jnp.zeros_like(out_ref)
        back_ref[...] = jnp.zeros_like(back_ref)

    feed = feed_ref[...]
    grad = grad_ref[...]
    weight = inner_ref[...]
    value = jnp.dot(feed, weight, preferred_element_type=F32) + bias_ref[...]
    square = value * value
    bend = jnp.tanh(GELU_A * (value + GELU_B * (square * value)))
    half = 0.5 * (1.0 + bend)
    active = (value * half).astype(BF)
    slope = half + 0.5 * value * (1.0 - bend * bend) * (GELU_A * (1.0 + 3.0 * GELU_B * square))
    out_ref[...] += jnp.dot(active, outer_ref[...], preferred_element_type=F32)
    outer_grad_ref[...] = lax.dot_general(active, grad, (((0,), (0,)), ((), ())), preferred_element_type=F32).astype(BF)
    pulled = lax.dot_general(grad, outer_ref[...], (((1,), (1,)), ((), ())), preferred_element_type=F32)
    inner_low = (pulled * slope).astype(BF)
    bias_grad_ref[...] = jnp.sum(inner_low.astype(F32), axis=0, keepdims=True)
    inner_grad_ref[...] = lax.dot_general(feed, inner_low, (((0,), (0,)), ((), ())), preferred_element_type=F32).astype(BF)
    back_ref[...] += lax.dot_general(inner_low, weight, (((1,), (1,)), ((), ())), preferred_element_type=F32)


def feed_call(rows, features, hidden, tile):
    fixed = pl.BlockSpec((rows, features), lambda j: (0, 0))
    return pl.pallas_call(
        feed_kernel,
        grid=(hidden // tile,),
        in_specs=[
            fixed,
            fixed,
            pl.BlockSpec((features, tile), lambda j: (0, j)),
            pl.BlockSpec((1, tile), lambda j: (0, j)),
            pl.BlockSpec((tile, features), lambda j: (j, 0)),
        ],
        out_specs=[
            fixed,
            fixed,
            pl.BlockSpec((features, tile), lambda j: (0, j)),
            pl.BlockSpec((tile, features), lambda j: (j, 0)),
            pl.BlockSpec((1, tile), lambda j: (0, j)),
        ],
        out_shape=[
            jax.ShapeDtypeStruct((rows, features), F32),
            jax.ShapeDtypeStruct((rows, features), F32),
            jax.ShapeDtypeStruct((features, hidden), BF),
            jax.ShapeDtypeStruct((hidden, features), BF),
            jax.ShapeDtypeStruct((1, hidden), F32),
        ],
        compiler_params=pltpu.CompilerParams(vmem_limit_bytes=60 << 20),
        name="feed_forward_backward",
    )


def pick(flag, when_true, when_false):
    return jnp.where(flag, when_true, when_false)


class PairPlan:
    def __init__(self):
        me = lax.axis_index("fsdp")
        self.upper = me // 2 == 1
        self.odd = me % 2 == 1
        self.tree = me // 2
        self.head_group = me % 2

    def near(self, value):
        return lax.ppermute(value, "fsdp", [(i, i ^ 1) for i in range(4)])

    def far(self, value):
        return lax.ppermute(value, "fsdp", [(i, i ^ 2) for i in range(4)])

    def rows_to_tree(self, rows):
        mine = pick(self.upper, rows[1], rows[0])
        got = self.far(pick(self.upper, rows[0], rows[1]))
        pair = jnp.stack([pick(self.upper, got, mine), pick(self.upper, mine, got)])
        other = self.near(pair)
        whole = jnp.stack([pick(self.odd, other, pair), pick(self.odd, pair, other)], axis=1)
        return whole.reshape((-1, rows.shape[2]))

    def heads_to_rows(self, heads):
        blocks = heads.reshape(2, 2, -1, heads.shape[1])
        keep = pick(self.odd, blocks[:, 1], blocks[:, 0])
        got = self.near(pick(self.odd, blocks[:, 0], blocks[:, 1]))
        full = jnp.concatenate([pick(self.odd, got, keep), pick(self.odd, keep, got)], axis=-1)
        return self.swap_trees(full)

    def swap_trees(self, full):
        mine = pick(self.upper, full[1], full[0])
        got = self.far(pick(self.upper, full[0], full[1]))
        return jnp.stack([pick(self.upper, got, mine), pick(self.upper, mine, got)])

    def rows_to_heads(self, rows):
        wide = rows.shape[2] // 2
        mine = pick(self.upper, rows[1], rows[0])
        got = self.far(pick(self.upper, rows[0], rows[1]))
        pair = jnp.stack([pick(self.upper, got, mine), pick(self.upper, mine, got)])
        keep = pick(self.odd, pair[..., wide:], pair[..., :wide])
        other = self.near(pick(self.odd, pair[..., :wide], pair[..., wide:]))
        whole = jnp.stack([pick(self.odd, other, keep), pick(self.odd, keep, other)], axis=1)
        return whole.reshape((-1, wide))

    def partial_to_rows(self, partial):
        blocks = partial.reshape(2, 2, -1, partial.shape[1])
        keep = pick(self.odd, blocks[:, 1], blocks[:, 0])
        got = self.near(pick(self.odd, blocks[:, 0], blocks[:, 1]).astype(BF))
        return self.swap_trees((keep + got.astype(F32)).astype(BF)).astype(F32)


class GroupPlan:
    def __init__(self, size, trees):
        me = lax.axis_index("fsdp")
        self.size = size
        self.trees = trees
        self.group = size // trees
        self.tree = me // self.group
        self.head_group = me % self.group
        self.me = me

    def rows_to_tree(self, rows):
        every = lax.all_gather(rows, "fsdp", axis=1, tiled=True)
        return lax.dynamic_index_in_dim(every, self.tree, 0, False)

    def heads_to_rows(self, heads):
        count = heads.shape[0] // self.size
        every = lax.all_gather(heads, "fsdp", axis=0, tiled=False)
        mine = lax.dynamic_slice_in_dim(every, self.me * count, count, 1)
        mine = mine.reshape(self.trees, self.group, count, heads.shape[1])
        return jnp.moveaxis(mine, 1, 2).reshape(self.trees, count, -1)

    def rows_to_heads(self, rows):
        wide = rows.shape[2] // self.group
        whole = self.rows_to_tree(rows)
        return lax.dynamic_slice_in_dim(whole, self.head_group * wide, wide, 1)

    def partial_to_rows(self, partial):
        every = jnp.zeros((self.trees,) + partial.shape, F32)
        every = lax.dynamic_update_index_in_dim(every, partial, self.tree, 0)
        return lax.psum_scatter(every, "fsdp", scatter_dimension=1, tiled=True)


def per_device(
    first_half,
    second_half,
    grad_first,
    grad_second,
    query_weight,
    value_weight,
    output_weight,
    inner_weight,
    inner_bias,
    outer_weight,
    outer_bias,
    mixer_gain,
    mixer_shift,
    feed_gain,
    feed_shift,
    parents,
    buckets,
    order,
    *,
    dp_size,
    fsdp_size,
):
    trees = first_half.shape[0]
    row_count = first_half.shape[2]
    features = first_half.shape[3]
    hidden = inner_weight.shape[1]
    rounds = buckets.shape[2]
    tree_len = buckets.shape[3]
    segments = parents.shape[2]
    all_rows = trees * row_count
    devices = dp_size * fsdp_size
    plan = PairPlan() if (fsdp_size, trees) == (4, 2) else GroupPlan(fsdp_size, trees)
    local_heads = H // (fsdp_size // trees)
    wide = local_heads * DH

    first = first_half[:, 0]
    second = second_half[:, 0]
    grad_a = grad_first[:, 0]
    grad_b = grad_second[:, 0]

    def gather(shard):
        return lax.all_gather(shard, AXES, axis=0, tiled=True)

    small_sizes = [v.shape[0] for v in (inner_bias, outer_bias, mixer_gain, mixer_shift, feed_gain, feed_shift)]
    small = lax.all_gather(
        jnp.concatenate([inner_bias, outer_bias, mixer_gain, mixer_shift, feed_gain, feed_shift])[None], AXES, axis=0, tiled=True
    ).astype(F32)
    vectors = []
    begin = 0
    for size in small_sizes:
        vectors.append(small[:, begin:begin + size].reshape(-1))
        begin += size
    bias_inner, bias_outer, gain_mix, shift_mix, gain_feed, shift_feed = vectors

    query_full = gather(query_weight)
    value_full = gather(value_weight)
    output_full = gather(output_weight)
    inner_full = gather(inner_weight)
    outer_full = gather(outer_weight)

    mix_unit, mix_factor = norm_stats(second)
    mixed_low = (mix_unit * gain_mix + shift_mix).astype(BF)
    mixed_tree = plan.rows_to_tree(mixed_low)
    parent_row = lax.dynamic_index_in_dim(parents[:, 0], plan.tree, 0, False)
    bucket_rows = lax.dynamic_index_in_dim(buckets[:, 0], plan.tree, 0, False)
    branch = parent_row[jnp.clip(parent_row, 0, segments - 1)]
    trunk_end = jnp.where(jnp.arange(segments) >= TRUNK + BRANCHES, branch, parent_row)
    info = jnp.concatenate([parent_row, trunk_end])
    codes = position_codes(bucket_rows)
    codes_q = jnp.pad(codes, ((0, 0), (0, 128 - rounds)))
    codes_k = jnp.pad(codes.T, ((0, 8 - rounds), (0, 0)))
    query_cols = lax.dynamic_slice_in_dim(query_full, plan.head_group * wide, wide, 1)
    value_cols = lax.dynamic_slice_in_dim(value_full, plan.head_group * wide, wide, 1)
    query_key = jnp.dot(mixed_tree, query_cols, preferred_element_type=F32).astype(BF)
    value_rows = jnp.dot(mixed_tree, value_cols, preferred_element_type=F32).astype(BF)
    attend, attend_back = attention_calls(tree_len, local_heads, rounds, segments)
    attended, totals, counts = attend(info, query_key, value_rows, codes_q, codes_k)
    attended_low = plan.heads_to_rows(attended)

    first_out = first + jnp.dot(attended_low.reshape(all_rows, features), output_full, preferred_element_type=F32).reshape(first.shape)
    feed_unit, feed_factor = norm_stats(first_out)
    feed_low = (feed_unit * gain_feed + shift_feed).astype(BF).reshape(all_rows, features)
    outer_low = grad_b.astype(BF).reshape(all_rows, features)
    fed, grad_feed, inner_grad, outer_grad, inner_bias_sum = feed_call(all_rows, features, hidden, 512)(
        feed_low, outer_low, inner_full, bias_inner[None], outer_full
    )
    second_out = second + fed.reshape(second.shape) + bias_outer
    outer_bias_sum = jnp.sum(outer_low.astype(F32), axis=0)
    grad_feed = grad_feed.reshape(first.shape)
    feed_gain_sum = jnp.sum(grad_feed * feed_unit, axis=(0, 1))
    feed_shift_sum = jnp.sum(grad_feed, axis=(0, 1))
    grad_first_in = grad_a + norm_back(feed_unit, feed_factor, gain_feed, grad_feed)
    branch_low = grad_first_in.astype(BF).reshape(all_rows, features)

    output_grad = lax.dot_general(
        attended_low.reshape(all_rows, features), branch_low, (((0,), (0,)), ((), ())), preferred_element_type=F32
    ).astype(BF)
    grad_attended = lax.dot_general(branch_low, output_full, (((1,), (1,)), ((), ())), preferred_element_type=F32).astype(BF)
    grad_heads = plan.rows_to_heads(grad_attended.reshape(trees, row_count, features))
    query_low, value_low = attend_back(info, query_key, value_rows, attended, grad_heads, totals, counts)
    query_grad = lax.dot_general(mixed_tree, query_low, (((0,), (0,)), ((), ())), preferred_element_type=F32).astype(BF)
    value_grad = lax.dot_general(mixed_tree, value_low, (((0,), (0,)), ((), ())), preferred_element_type=F32).astype(BF)
    partial = lax.dot_general(query_low, query_cols, (((1,), (1,)), ((), ())), preferred_element_type=F32) + lax.dot_general(
        value_low, value_cols, (((1,), (1,)), ((), ())), preferred_element_type=F32
    )
    grad_mixed = plan.partial_to_rows(partial)
    mix_gain_sum = jnp.sum(grad_mixed * mix_unit, axis=(0, 1))
    mix_shift_sum = jnp.sum(grad_mixed, axis=(0, 1))
    grad_second_in = grad_b + norm_back(mix_unit, mix_factor, gain_mix, grad_mixed)

    def scatter(total):
        return lax.psum_scatter(total, AXES, scatter_dimension=0, tiled=True).astype(F32)

    def spread(cols):
        return lax.dynamic_update_slice_in_dim(jnp.zeros((features, features), BF), cols, plan.head_group * wide, 1)

    small_sums = [inner_bias_sum[0], outer_bias_sum, mix_gain_sum, mix_shift_sum, feed_gain_sum, feed_shift_sum]
    packed = jnp.concatenate([v.reshape(devices, -1) for v in small_sums], axis=1)
    packed = lax.psum_scatter(packed, AXES, scatter_dimension=0, tiled=True)[0]
    pieces = []
    begin = 0
    for size in small_sizes:
        pieces.append(packed[begin:begin + size])
        begin += size
    return (
        first_out[:, None],
        second_out[:, None],
        grad_first_in[:, None],
        grad_second_in[:, None],
        scatter(spread(query_grad)),
        scatter(spread(value_grad)),
        scatter(output_grad),
        scatter(inner_grad),
        pieces[0],
        scatter(outer_grad),
        pieces[1],
        pieces[2],
        pieces[3],
        pieces[4],
        pieces[5],
    )


def solution(mesh):
    rows = P(None, "dp", "fsdp", None)
    matrix = P(AXES, None)
    vector = P(AXES)
    weights = (matrix, matrix, matrix, matrix, vector, matrix, vector, vector, vector, vector, vector)
    return jax.shard_map(
        functools.partial(per_device, dp_size=mesh.shape["dp"], fsdp_size=mesh.shape["fsdp"]),
        mesh=mesh,
        in_specs=(rows,) * 4 + weights + (P(None, "dp", None), P(None, "dp", None, None), P(None, "dp", None, None)),
        out_specs=(rows,) * 4 + weights,
        check_vma=False,
    )
```

time: 2560 us -> 1120 us (0.44)
  local copies, waits for them, and re-layouts: 479 us -> 24.2 us
  waiting for transfers between devices: 1180 us -> 824 us
  matrix products: 333 us -> 28.6 us
  other arithmetic: 289 us -> 44 us
  blocking collectives: 249 us -> 84 us
  Pallas kernels: 0 us -> 83.3 us
    dot_general x52 -> x10, matrix products: 333 us -> 28.6 us  [the longest x1 4.41 us: per_device(): jnp.dot(attended_low.reshape(all_rows, features), output_full, preferred_...]
    gather x28 -> x1, local copies, waits for them, and re-layouts: 280 us -> 0.66 us  [per_device(): branch = parent_row[jnp.clip(parent_row, 0, segments - 1)]]
    all_gather x16 -> x5, waiting for transfers between devices: 428 us -> 200 us  [gather(): return lax.all_gather(shard, AXES, axis=0, tiled=True)]
    reduce_scatter x11 -> x5, waiting for transfers between devices: 745 us -> 550 us  [scatter(): lax.psum_scatter(total, AXES, scatter_dimension=0, tiled=True).astype(F32)]
    scatter-add x8 -> x0, other arithmetic: 176 us -> none  [the longest x4 89.8 us: one_batch(): spread_query = jnp.zeros((tree_len, features), single).at[query_tok.resha...]
    all_gather x6 -> x0, blocking collectives: 126 us -> none  [the longest x2 78.6 us: one_batch(): lax.all_gather(shards[4], ('dp', 'fsdp'), axis=0, tiled=True)]
    while x366 -> x0, local copies, waits for them, and re-layouts: 105 us -> none
    pallas_call x0 -> x3, Pallas kernels: none -> 83.3 us  [the longest x1 43.8 us: per_device(): feed_call(all_rows, features, hidden, 512)]
  transfers between devices with their start and end apart: 27 -> 18, of which waited for: 16 -> 16; matrix products, arithmetic and copies ran while one was open for 30% -> 6% of each run, Pallas kernels for 0% -> 4%
where the time goes in v1:
time: 1120 us; the launch traced here: 1110 us
  waiting for transfers between devices  824 us (74%)
  blocking collectives  84 us (8%)
  Pallas kernels  83.3 us (7%)
  other arithmetic  44 us (4%)
  matrix products  28.6 us (3%)
  local copies, waits for them, and re-layouts  24.2 us (2%)
  between operations  15.1 us (1%)
    reduce_scatter x5, waiting for transfers between devices, scatter(): lax.psum_scatter(total, AXES, scatter_dimension=0, tiled=True).astype(F32)  550 us
    all_gather x5, waiting for transfers between devices, gather(): return lax.all_gather(shard, AXES, axis=0, tiled=True)  200 us
    unnamed x2, blocking collectives  84 us
    ppermute x4, waiting for transfers between devices, far(): return lax.ppermute(value, 'fsdp', [(i, i ^ 2) for i in range(4)])  60.1 us
    pallas_call x1, Pallas kernels, per_device(): feed_call(all_rows, features, hidden, 512)  43.8 us
  transfers between devices with their start and end apart: 18, of which 16 were waited for; matrix products, arithmetic and copies ran while one was open for 6% of the time, Pallas kernels for 4%

profile of v1, /device:TPU:0, one launch (start us, length us, event | category | flops | bytes accessed | tf_op | source)
XLA Modules:
  0.0 1112.3 jit_solution(4859036607832854207)
XLA Ops:
  10.6 4.1 concatenate.20
  15.0 42.2 %all-reduce.2 = bf16[9216]{0:T(1024)(128)(2,1)S(1)} all-reduce(bf16[9216]{0:T(1024)(128)(2,1)S(1)} %dynamic-update-slice), channel_id=2, replica_groups=mesh['dp'=8,'fsdp'=4] {'dp','fsdp'}, use_global_device_ids=true, to_apply=%add.2 | all-reduce | flops 9216 | bytes 36864
  57.5 2.0 reduce_sum.135
  61.5 2.4 collective-permute-start
  65.8 11.6 %collective-permute-done = bf16[320,1024]{1,0:T(8,128)(2,1)} collective-permute-done((bf16[320,1024]{1,0:T(8,128)(2,1)S(1)}, bf16[320,1024]{1,0:T(8,128)(2,1)}, u32[]{:S(2)}, u32[]{:S(2)}) %collective-permute-start) | collective-permute-done | bytes 655392 | tf_op jit(solution)/shard_map/ppermute | solution.py:303
  81.0 2.2 collective-permute-done.1
  84.9 1.7 copy.64
  86.7 3.6 convolution_convert_fusion.v_ref
  90.2 38.0 %all-gather.7.cloned.1.call-done = bf16[1024,1024]{1,0:T(8,128)(2,1)} async-done(((bf16[32,1024]{1,0:T(8,128)(2,1)}), bf16[1024,1024]{1,0:T(8,128)(2,1)}) %all-gather.7.cloned.1.call-update) | async-done | bytes 2097168 | tf_op jit(solution)/shard_map/all_gather | solution.py:416
  128.2 3.5 convolution_convert_fusion.1.q_ref
  131.7 18.5 %attention_forward.1 = (bf16[1280,512]{1,0:T(8,128)(2,1)S(1)}, f32[1280,128]{1,0:T(8,128)S(1)}, bf16[1280,768]{1,0:T(8,128)(2,1)S(1)}) custom-call(s32[20]{0:T(128)S(1)} %pad_add_fusion.info_ref, bf16[1280,512]{1,0:T(8,128)(2,1)S(1)} %convolution_convert_fusion.1.q_ref, bf16[1280,512]{1,0:T(8,128)(2,1)S(1)} %convolution_convert_fusion.v_ref, ...), custom_call_target="tpu_custom_call" | custom-call | tf_op jit(solution)/shard_map/attention_forward/pallas_call | solution.py:451
  150.7 1.8 collective-permute-done.2
  156.7 3.1 convert_reduce_fusion.1
  159.8 12.2 %collective-permute-done.3 = bf16[320,1024]{1,0:T(8,128)(2,1)} collective-permute-done((bf16[320,1024]{1,0:T(8,128)(2,1)}, bf16[320,1024]{1,0:T(8,128)(2,1)}, u32[]{:S(2)}, u32[]{:S(2)}) %collective-permute-start.3) | collective-permute-done | bytes 655392 | tf_op jit(solution)/shard_map/ppermute | solution.py:303
  172.1 2.5 fusion.21
  174.6 11.9 %all-gather.11.cloned.1.call-done = bf16[1024,1024]{1,0:T(8,128)(2,1)} async-done(((bf16[32,1024]{1,0:T(8,128)(2,1)}), bf16[1024,1024]{1,0:T(8,128)(2,1)}) %all-gather.11.cloned.1.call-update) | async-done | bytes 2097168 | tf_op jit(solution)/shard_map/all_gather | solution.py:416
  186.5 4.4 fusion.42
  192.4 1.5 add_convert_fusion
  193.9 71.7 %all-gather.13.cloned.1.call-done.inner_ref = bf16[1024,4096]{1,0:T(8,128)(2,1)} async-done(((bf16[32,4096]{1,0:T(8,128)(2,1)}), bf16[1024,4096]{1,0:T(8,128)(2,1)}) %all-gather.13.cloned.1.call-update) | async-done | bytes 8388624 | tf_op jit(solution)/shard_map/all_gather | solution.py:416
  265.7 78.9 %all-gather.15.cloned.1.call-done.outer_ref = bf16[4096,1024]{1,0:T(8,128)(2,1)} async-done(((bf16[128,1024]{1,0:T(8,128)(2,1)}), bf16[4096,1024]{1,0:T(8,128)(2,1)}) %all-gather.15.cloned.1.call-update) | async-done | bytes 8388624 | tf_op jit(solution)/shard_map/all_gather | solution.py:416
  344.6 43.8 %feed_forward_backward.1 = (f32[640,1024]{1,0:T(8,128)}, f32[640,1024]{1,0:T(8,128)}, bf16[1024,4096]{1,0:T(8,128)(2,1)}, bf16[4096,1024]{1,0:T(8,128)(2,1)}, f32[1,4096]{1,0:T(1,128)}) custom-call(bf16[640,1024]{1,0:T(8,128)(2,1)} %bitcast.209, bf16[640,1024]{1,0:T(8,128)(2,1)} %bitcast.208, bf16[1024,4096]{1,0:T(8,128)(2,1)} %all-gather.13.cloned.1.call-done.inner_ref, ...), custom_call_target="tpu_custom_call" | custom-call | tf_op jit(solution)/shard_map/feed_forward_backward/pallas_call | solution.py:458
  388.4 2.1 fusion.39
  390.6 3.6 multiply_reduce_fusion
  394.7 3.5 fusion.40
  399.2 3.2 bitcast_convert_fusion
  402.5 3.5 convolution_convert_fusion.2
  406.1 1.5 collective-permute-start.4
  407.6 18.6 %collective-permute-done.4 = bf16[320,1024]{1,0:T(8,128)(2,1)S(1)} collective-permute-done((bf16[320,1024]{1,0:T(8,128)(2,1)S(1)}, bf16[320,1024]{1,0:T(8,128)(2,1)S(1)}, u32[]{:S(2)}, u32[]{:S(2)}) %collective-permute-start.4) | collective-permute-done | bytes 655392 | tf_op jit(solution)/shard_map/ppermute | solution.py:303
  426.6 2.1 collective-permute-done.5
  431.1 21.1 %attention_backward.1 = (bf16[1280,512]{1,0:T(8,128)(2,1)S(1)}, bf16[1280,512]{1,0:T(8,128)(2,1)S(1)}) custom-call(s32[20]{0:T(128)S(1)} %pad_add_fusion.info_ref, bf16[1280,512]{1,0:T(8,128)(2,1)S(1)} %copy-done.1, bf16[1280,512]{1,0:T(8,128)(2,1)S(1)} %convolution_convert_fusion.v_ref, bf16[1280,512]{1,0:T(8,128)(2,1)S(1)} %get-tuple-element.25.out_ref, ...), custom_call_target="tpu_custom_call" | custom-call | tf_op jit(solution)/shard_map/attention_backward/pallas_call | solution.py:474
  454.3 1.6 fusion.12
  458.0 3.3 fusion.11
  465.0 2.9 fusion.16
  468.0 1.6 convolution_add_fusion
  470.0 2.9 collective-permute-done.6
  473.8 2.4 collective-permute-start.7
  476.5 17.7 %collective-permute-done.7 = bf16[320,1024]{1,0:T(8,128)(2,1)S(1)} collective-permute-done((bf16[320,1024]{1,0:T(8,128)(2,1)S(1)}, bf16[320,1024]{1,0:T(8,128)(2,1)S(1)}, u32[]{:S(2)}, u32[]{:S(2)}) %collective-permute-start.7) | collective-permute-done | bytes 655392 | tf_op jit(solution)/shard_map/ppermute | solution.py:303
  495.1 2.2 fusion.27
  498.9 41.8 %all-reduce.3 = f32[32,288]{1,0:T(8,128)S(1)} all-reduce(f32[32,288]{1,0:T(8,128)S(1)} %concatenate.22), channel_id=7, replica_groups=mesh['dp'=8,'fsdp'=4] {'dp','fsdp'}, use_global_device_ids=true, to_apply=%region_19.20.clone | all-reduce | flops 9216 | bytes 73728
  541.9 4.9 multiply_add_fusion
  546.8 1.5 convert_element_type.123
  548.3 125.7 %reduce-scatter.6.cloned.1.call-done = bf16[32,1024]{1,0:T(8,128)(2,1)} async-done(((bf16[1024,1024]{1,0:T(8,128)(2,1)}), bf16[32,1024]{1,0:T(8,128)(2,1)}) %reduce-scatter.6.cloned.1.call-update) | async-done | bytes 65552 | tf_op jit(solution)/shard_map/reduce_scatter | solution.py:486
  674.0 1.5 convert_element_type.119
  675.5 133.4 %reduce-scatter.8.cloned.1.call-done = bf16[32,1024]{1,0:T(8,128)(2,1)} async-done(((bf16[1024,1024]{1,0:T(8,128)(2,1)}), bf16[32,1024]{1,0:T(8,128)(2,1)}) %reduce-scatter.8.cloned.1.call-update) | async-done | bytes 65552 | tf_op jit(solution)/shard_map/reduce_scatter | solution.py:486
  810.4 145.9 %reduce-scatter.12.cloned.1.call-done = bf16[32,4096]{1,0:T(8,128)(2,1)} async-done(((bf16[1024,4096]{1,0:T(8,128)(2,1)}), bf16[32,4096]{1,0:T(8,128)(2,1)}) %reduce-scatter.12.cloned.1.call-update) | async-done | bytes 262160 | tf_op jit(solution)/shard_map/reduce_scatter | solution.py:486
  956.3 1.8 convert_element_type.124
  958.1 145.3 %reduce-scatter.14.cloned.1.call-done = bf16[128,1024]{1,0:T(8,128)(2,1)} async-done(((bf16[4096,1024]{1,0:T(8,128)(2,1)}), bf16[128,1024]{1,0:T(8,128)(2,1)}) %reduce-scatter.14.cloned.1.call-update) | async-done | bytes 262160 | tf_op jit(solution)/shard_map/reduce_scatter | solution.py:486
  1103.4 1.8 convert_element_type.126
  (160 shorter events, 38.2 us)
Async XLA Ops:
  7.2 52.3 %copy-start.10 = (f32[2,1,320,1024]{3,2,1,0:T(8,128)S(1)}, f32[2,1,320,1024]{3,2,1,0:T(8,128)}, u32[]{:S(2)}) copy-start(f32[2,1,320,1024]{3,2,1,0:T(8,128)} %param.19) | copy-start | bytes 7864324
  7.2 79.5 %all-gather.9.cloned.1.call-start = ((), (), s32[]{:S(2)}) async-start(), calls=%async_computation.6 | async-start | bytes 2162688 | tf_op jit(solution)/shard_map/all_gather | solution.py:416
  7.9 120.3 %all-gather.7.cloned.1.call-start = ((), (), s32[]{:S(2)}) async-start(), calls=%async_computation.5 | async-start | bytes 2162688 | tf_op jit(solution)/shard_map/all_gather | solution.py:416
  8.7 177.8 %all-gather.11.cloned.1.call-start = ((), (), s32[]{:S(2)}) async-start(), calls=%async_computation.7 | async-start | bytes 2162688 | tf_op jit(solution)/shard_map/all_gather | solution.py:416
  9.4 256.3 %all-gather.13.cloned.1.call-start = ((), (), s32[]{:S(2)}) async-start(), calls=%async_computation.8 | async-start | bytes 8650752 | tf_op jit(solution)/shard_map/all_gather | solution.py:416
  10.0 334.6 %all-gather.15.cloned.1.call-start = ((), (), s32[]{:S(2)}) async-start(), calls=%async_computation.9 | async-start | bytes 8650752 | tf_op jit(solution)/shard_map/all_gather | solution.py:416
  10.6 536.2 %reduce-scatter.10.cloned.1.call-start = ((), (), s32[]{:S(2)}) async-start(), calls=%async_computation.12 | async-start | bytes 2162688 | tf_op jit(solution)/shard_map/reduce_scatter | solution.py:486
  59.9 4.0 copy-start.27
  60.4 1.1 copy-start.15
  61.5 15.9 %collective-permute-start = (bf16[320,1024]{1,0:T(8,128)(2,1)S(1)}, bf16[320,1024]{1,0:T(8,128)(2,1)}, u32[]{:S(2)}, u32[]{:S(2)}) collective-permute-start(bf16[320,1024]{1,0:T(8,128)(2,1)S(1)} %select_bitcast_fusion.9), channel_id=1, source_target_pairs={{0,2},{1,3},{2,0},{3,1},{4,6},{5,7},{6,4},{7,5},{8,10},{9,11},{10,... | collective-permute-start | bytes 1966088 | tf_op jit(solution)/shard_map/ppermute | solution.py:303
  65.3 12.2 %copy-start.16 = (bf16[2,320,1024]{2,1,0:T(8,128)(2,1)S(1)}, bf16[2,320,1024]{2,1,0:T(8,128)(2,1)}, u32[]{:S(2)}) copy-start(bf16[2,320,1024]{2,1,0:T(8,128)(2,1)} %copy-done.15) | copy-start | bytes 3932164
  78.6 1.6 copy-start.29
  79.8 3.4 collective-permute-start.1
  131.7 18.6 %copy-start = (bf16[1280,512]{1,0:T(8,128)(2,1)}, bf16[1280,512]{1,0:T(8,128)(2,1)S(1)}, u32[]{:S(2)}) copy-start(bf16[1280,512]{1,0:T(8,128)(2,1)S(1)} %convolution_convert_fusion.1.q_ref) | copy-start | bytes 3932164
  150.2 2.4 copy-start.4
  150.2 2.4 copy-start.6
  150.3 2.2 collective-permute-start.2
  152.6 0.8 copy-start.19
  154.5 17.6 %collective-permute-start.3 = (bf16[320,1024]{1,0:T(8,128)(2,1)}, bf16[320,1024]{1,0:T(8,128)(2,1)}, u32[]{:S(2)}, u32[]{:S(2)}) collective-permute-start(bf16[320,1024]{1,0:T(8,128)(2,1)} %select_bitcast_fusion.7), channel_id=1, source_target_pairs={{0,2},{1,3},{2,0},{3,1},{4,6},{5,7},{6,4},{7,5},{8,10},{9,11},{10,... | collective-permute-start | bytes 1966088 | tf_op jit(solution)/shard_map/ppermute | solution.py:303
  156.7 15.4 %copy-start.20 = (bf16[2,320,512]{2,1,0:T(8,128)(2,1)S(1)}, bf16[2,320,512]{2,1,0:T(8,128)(2,1)}, u32[]{:S(2)}) copy-start(bf16[2,320,512]{2,1,0:T(8,128)(2,1)} %copy-done.19) | copy-start | bytes 1966084
  190.9 1.5 copy-start.12
  390.6 3.6 copy-start.13
  390.6 4.1 copy-start.14
  394.7 4.6 copy-start.24
  394.7 4.6 copy-start.25
  398.1 1.1 copy-start.23
  402.4 271.6 %reduce-scatter.6.cloned.1.call-start = ((), (), s32[]{:S(2)}) async-start(), calls=%async_computation.10 | async-start | bytes 2162688 | tf_op jit(solution)/shard_map/reduce_scatter | solution.py:486
  406.1 20.1 %collective-permute-start.4 = (bf16[320,1024]{1,0:T(8,128)(2,1)S(1)}, bf16[320,1024]{1,0:T(8,128)(2,1)S(1)}, u32[]{:S(2)}, u32[]{:S(2)}) collective-permute-start(bf16[320,1024]{1,0:T(8,128)(2,1)S(1)} %broadcast_select_fusion.7), channel_id=1, source_target_pairs={{0,2},{1,3},{2,0},{3,1},{4,6},{5,7},{6,4},{7,5},{8,10},{9,11},{10,... | collective-permute-start | bytes 1966088 | tf_op jit(solution)/shard_map/ppermute | solution.py:303
  426.6 2.2 collective-permute-start.5
  429.1 1.3 copy-start.1
  429.1 1.9 copy-start.5
  429.1 2.1 copy-start.7
  431.1 23.2 %copy-start.21 = (bf16[2,2,320,1024]{3,2,1,0:T(8,128)(2,1)S(1)}, bf16[2,2,320,1024]{3,2,1,0:T(8,128)(2,1)}, u32[]{:S(2)}) copy-start(bf16[2,2,320,1024]{3,2,1,0:T(8,128)(2,1)} %copy.64) | copy-start | bytes 7864324
  452.2 1.1 copy-start.2
  453.3 1.0 copy-start.8
  455.9 1.3 copy-start.18
  455.9 2.1 copy-start.3
  457.2 351.7 %reduce-scatter.8.cloned.1.call-start = ((), (), s32[]{:S(2)}) async-start(), calls=%async_computation.11 | async-start | bytes 2162688 | tf_op jit(solution)/shard_map/reduce_scatter | solution.py:486
  461.3 1.3 copy-start.17
  462.6 493.7 %reduce-scatter.12.cloned.1.call-start = ((), (), s32[]{:S(2)}) async-start(), calls=%async_computation.13 | async-start | bytes 8650752 | tf_op jit(solution)/shard_map/reduce_scatter | solution.py:486
  463.4 640.0 %reduce-scatter.14.cloned.1.call-start = ((), (), s32[]{:S(2)}) async-start(), calls=%async_computation.14 | async-start | bytes 8650752 | tf_op jit(solution)/shard_map/reduce_scatter | solution.py:486
  463.7 1.3 copy-start.9
  465.0 2.9 copy-start.26
  469.8 3.1 collective-permute-start.6
  473.8 20.4 %collective-permute-start.7 = (bf16[320,1024]{1,0:T(8,128)(2,1)S(1)}, bf16[320,1024]{1,0:T(8,128)(2,1)S(1)}, u32[]{:S(2)}, u32[]{:S(2)}) collective-permute-start(bf16[320,1024]{1,0:T(8,128)(2,1)S(1)} %select_bitcast_fusion.2), channel_id=1, source_target_pairs={{0,2},{1,3},{2,0},{3,1},{4,6},{5,7},{6,4},{7,5},{8,10},{9,11},{10,... | collective-permute-start | bytes 1966088 | tf_op jit(solution)/shard_map/ppermute | solution.py:303
  494.1 0.8 copy-start.22
  495.1 2.3 copy-start.11
  497.3 1.5 copy-start.28
Sparse Core Ops, SparseCore 0:
  10.9 59.1 all-gather.8
  72.9 55.2 all-gather.6
  131.1 55.3 all-gather.10
  189.2 76.4 all-gather.12
  268.4 76.1 all-gather.14
  402.5 135.9 reduce-scatter.9
  540.9 133.0 reduce-scatter.5
  676.2 132.5 reduce-scatter.7
  811.3 144.9 reduce-scatter.11
  958.5 144.8 reduce-scatter.13

commit v2 on v1

--- a/solution.py
+++ b/solution.py
@@ -227,61 +227,326 @@
     return forward, backward
 
 
-def feed_kernel(feed_ref, grad_ref, inner_ref, bias_ref, outer_ref, out_ref, back_ref, inner_grad_ref, outer_grad_ref, bias_grad_ref):
+def row_block(where_fn, coords_ref, span):
+    return pl.ds(pl.multiple_of(where_fn(coords_ref) * span, span), span)
+
+
+def piece_view(refs, piece):
+    view = refs[piece[0]].at[piece[1]] if piece[1] else refs[piece[0]]
+    return view if piece[2] is None else view.at[pl.ds(piece[2], piece[3])]
+
+
+def load_pieces(coords_ref, refs, pieces, target, sems, first):
+    copies = []
+    for number, piece in enumerate(pieces):
+        span = piece[3]
+        copies.append(pltpu.make_async_copy(piece_view(refs, piece), target.at[row_block(piece[4], coords_ref, span)], sems.at[first + number]))
+    return copies
+
+
+def store_pieces(coords_ref, source, refs, pieces, sems, first):
+    copies = []
+    for number, piece in enumerate(pieces):
+        span = piece[3]
+        copies.append(pltpu.make_async_copy(source.at[row_block(piece[4], coords_ref, span)], piece_view(refs, piece), sems.at[first + number]))
+    return copies
+
+
+def project_kernel(q_pieces, v_pieces, q_count, v_count, coords_ref, mixed_ref, *refs):
+    q_refs, v_refs = refs[:q_count], refs[q_count:q_count + v_count]
+    q_out, v_out, q_weight, v_weight, sems = refs[q_count + v_count:]
+    to_q = load_pieces(coords_ref, q_refs, q_pieces, q_weight, sems, 0)
+    to_v = load_pieces(coords_ref, v_refs, v_pieces, v_weight, sems, len(q_pieces))
+    for copy in to_q + to_v:
+        copy.start()
+    for copy in to_q:
+        copy.wait()
+    q_out[...] = jnp.dot(mixed_ref[...], q_weight[...], preferred_element_type=F32).astype(BF)
+    for copy in to_v:
+        copy.wait()
+    v_out[...] = jnp.dot(mixed_ref[...], v_weight[...], preferred_element_type=F32).astype(BF)
+
+
+VM = pl.BlockSpec(memory_space=pltpu.VMEM)
+ANYWHERE = pl.BlockSpec(memory_space=pl.ANY)
+
+
+def kernel_call(body, ins, outs, scratch, name, limit, grid=(), semantics=None):
+    return pl.pallas_call(
+        body,
+        grid_spec=pltpu.PrefetchScalarGridSpec(num_scalar_prefetch=1, grid=grid, in_specs=ins, out_specs=outs[0], scratch_shapes=scratch),
+        out_shape=outs[1],
+        compiler_params=pltpu.CompilerParams(vmem_limit_bytes=limit << 20),
+        name=name,
+    )
+
+
+def project(coords, mixed_tree, q_side, v_side, wide):
+    q_arrays, q_pieces = q_side
+    v_arrays, v_pieces = v_side
+    rows, features = mixed_tree.shape
+    body = functools.partial(project_kernel, q_pieces, v_pieces, len(q_arrays), len(v_arrays))
+    return kernel_call(
+        body,
+        [VM] + [ANYWHERE] * (len(q_arrays) + len(v_arrays)),
+        ([VM, VM], [jax.ShapeDtypeStruct((rows, wide), BF)] * 2),
+        [pltpu.VMEM((features, wide), BF)] * 2 + [pltpu.SemaphoreType.DMA((len(q_pieces) + len(v_pieces),))],
+        "project",
+        40,
+    )(coords, mixed_tree, *q_arrays, *v_arrays)
+
+
+def project_back_kernel(q_pieces, v_pieces, q_count, v_count, q_outs, v_outs, q_made, v_made, coords_ref, mixed_ref, dq_ref, dv_ref, *refs):
+    q_refs, v_refs = refs[:q_count], refs[q_count:q_count + v_count]
+    rest = refs[q_count + v_count:]
+    partial_ref = rest[0]
+    q_grads, v_grads = rest[1:1 + q_made], rest[1 + q_made:1 + q_made + v_made]
+    q_weight, v_weight, q_sum, v_sum, sems = rest[1 + q_made + v_made:]
+    to_q = load_pieces(coords_ref, q_refs, q_pieces, q_weight, sems, 0)
+    to_v = load_pieces(coords_ref, v_refs, v_pieces, v_weight, sems, len(q_pieces))
+    for copy in to_q + to_v:
+        copy.start()
+    used = len(q_pieces) + len(v_pieces)
+    turned = (((0,), (0,)), ((), ()))
+    crossed = (((1,), (1,)), ((), ()))
+    q_sum[...] = lax.dot_general(mixed_ref[...], dq_ref[...], turned, preferred_element_type=F32).astype(BF)
+    from_q = store_pieces(coords_ref, q_sum, q_grads, q_outs, sems, used)
+    for copy in from_q:
+        copy.start()
+    v_sum[...] = lax.dot_general(mixed_ref[...], dv_ref[...], turned, preferred_element_type=F32).astype(BF)
+    from_v = store_pieces(coords_ref, v_sum, v_grads, v_outs, sems, used + len(q_outs))
+    for copy in from_v:
+        copy.start()
+    for copy in to_q + to_v:
+        copy.wait()
+    partial_ref[...] = (
+        lax.dot_general(dq_ref[...], q_weight[...], crossed, preferred_element_type=F32)
+        + lax.dot_general(dv_ref[...], v_weight[...], crossed, preferred_element_type=F32)
+    ).astype(BF)
+    for copy in from_q + from_v:
+        copy.wait()
+
+
+def project_back(coords, mixed_tree, dq, dv, q_side, v_side, q_form, v_form):
+    q_arrays, q_pieces = q_side
+    v_arrays, v_pieces = v_side
+    q_shapes, q_outs = q_form
+    v_shapes, v_outs = v_form
+    rows, features = mixed_tree.shape
+    wide = dq.shape[1]
+    body = functools.partial(
+        project_back_kernel, q_pieces, v_pieces, len(q_arrays), len(v_arrays), q_outs, v_outs, len(q_shapes), len(v_shapes)
+    )
+    made = kernel_call(
+        body,
+        [VM] * 3 + [ANYWHERE] * (len(q_arrays) + len(v_arrays)),
+        (
+            [VM] + [ANYWHERE] * (len(q_shapes) + len(v_shapes)),
+            [jax.ShapeDtypeStruct((rows, features), BF)] + [jax.ShapeDtypeStruct(s, BF) for s in q_shapes + v_shapes],
+        ),
+        [pltpu.VMEM((features, wide), BF)] * 4
+        + [pltpu.SemaphoreType.DMA((len(q_pieces) + len(v_pieces) + len(q_outs) + len(v_outs),))],
+        "project_back",
+        50,
+    )(coords, mixed_tree, dq, dv, *q_arrays, *v_arrays)
+    return made[0], made[1:1 + len(q_shapes)], made[1 + len(q_shapes):]
+
+
+def normalised(values):
+    center = values - jnp.mean(values, axis=-1, keepdims=True)
+    factor = lax.rsqrt(jnp.mean(center * center, axis=-1, keepdims=True) + EPSILON)
+    return center * factor, factor
+
+
+def out_kernel(pieces, count, coords_ref, att_ref, first_ref, gain_ref, shift_ref, *refs):
+    o_refs = refs[:count]
+    first_out, feed_out, weight, sems = refs[count:]
+    copies = load_pieces(coords_ref, o_refs, pieces, weight, sems, 0)
+    for copy in copies:
+        copy.start()
+    for copy in copies:
+        copy.wait()
+    made = first_ref[...] + jnp.dot(att_ref[...], weight[...], preferred_element_type=F32)
+    first_out[...] = made
+    feed_out[...] = (normalised(made)[0] * gain_ref[...] + shift_ref[...]).astype(BF)
+
+
+def out_project(coords, att, first, gain, shift, side):
+    arrays, pieces = side
+    rows, features = first.shape
+    return kernel_call(
+        functools.partial(out_kernel, pieces, len(arrays)),
+        [VM] * 4 + [ANYWHERE] * len(arrays),
+        ([VM, VM], [jax.ShapeDtypeStruct((rows, features), F32), jax.ShapeDtypeStruct((rows, features), BF)]),
+        [pltpu.VMEM((features, features), BF), pltpu.SemaphoreType.DMA((len(pieces),))],
+        "out_project",
+        50,
+    )(coords, att, first, gain, shift, *arrays)
+
+
+def out_back_kernel(pieces, count, outs, made, coords_ref, back_ref, first_ref, grad_ref, att_ref, gain_ref, *refs):
+    o_refs = refs[:count]
+    rest = refs[count:]
+    grad_in, grad_att, gain_sum, shift_sum = rest[:4]
+    grads = rest[4:4 + made]
+    weight, total, sems = rest[4 + made:]
+    copies = load_pieces(coords_ref, o_refs, pieces, weight, sems, 0)
+    for copy in copies:
+        copy.start()
+    back = back_ref[...]
+    unit, factor = normalised(first_ref[...])
+    gain_sum[...] = jnp.sum(back * unit, axis=0, keepdims=True)
+    shift_sum[...] = jnp.sum(back, axis=0, keepdims=True)
+    scaled = back * gain_ref[...]
+    inner = jnp.mean(scaled * unit, axis=-1, keepdims=True)
+    value = grad_ref[...] + factor * (scaled - jnp.mean(scaled, axis=-1, keepdims=True) - unit * inner)
+    grad_in[...] = value
+    low = value.astype(BF)
+    total[...] = lax.dot_general(att_ref[...], low, (((0,), (0,)), ((), ())), preferred_element_type=F32).astype(BF)
+    stores = store_pieces(coords_ref, total, grads, outs, sems, len(pieces))
+    for copy in stores:
+        copy.start()
+    for copy in copies:
+        copy.wait()
+    grad_att[...] = lax.dot_general(low, weight[...], (((1,), (1,)), ((), ())), preferred_element_type=F32).astype(BF)
+    for copy in stores:
+        copy.wait()
+
+
+def out_back(coords, back, first_out, grad, att, gain, side, form):
+    arrays, pieces = side
+    shapes, outs = form
+    rows, features = back.shape
+    full = jax.ShapeDtypeStruct((rows, features), F32)
+    line = jax.ShapeDtypeStruct((1, features), F32)
+    made = kernel_call(
+        functools.partial(out_back_kernel, pieces, len(arrays), outs, len(shapes)),
+        [VM] * 5 + [ANYWHERE] * len(arrays),
+        (
+            [VM] * 4 + [ANYWHERE] * len(shapes),
+            [full, jax.ShapeDtypeStruct((rows, features), BF), line, line] + [jax.ShapeDtypeStruct(s, BF) for s in shapes],
+        ),
+        [pltpu.VMEM((features, features), BF)] * 2 + [pltpu.SemaphoreType.DMA((len(pieces) + len(outs),))],
+        "out_back",
+        60,
+    )(coords, back, first_out, grad, att, gain, *arrays)
+    return made[:4], made[4:]
+
+
+def feed_kernel(plan, counts, coords_ref, feed_ref, grad_ref, bias_ref, *refs):
+    i_pieces, i_outs, steps, step_outs = plan
+    i_count, u_count, i_made, u_made = counts
+    i_refs, u_refs = refs[:i_count], refs[i_count:i_count + u_count]
+    rest = refs[i_count + u_count:]
+    out_ref, back_ref, bias_sum = rest[:3]
+    i_grads, u_grads = rest[3:3 + i_made], rest[3 + i_made:3 + i_made + u_made]
+    weight, weight_sum, outer, outer_sum, i_sems, u_sems, iout_sems, uout_sems = rest[3 + i_made + u_made:]
     step = pl.program_id(0)
+    slot = lax.rem(step, 2)
+    tile = outer.shape[1]
+    count = len(steps)
+
+    def u_load(number):
+        return load_pieces(coords_ref, u_refs, steps[number][1], outer.at[number % 2], u_sems.at[number % 2], 0)
+
+    def u_store(number):
+        return store_pieces(coords_ref, outer_sum.at[number % 2], u_grads, step_outs[number], uout_sems.at[number % 2], 0)
 
     @pl.when(step == 0)
     def _():
+        copies = load_pieces(coords_ref, i_refs, i_pieces, weight, i_sems, 0)
+        for copy in copies + u_load(0):
+            copy.start()
         out_ref[...] = jnp.zeros_like(out_ref)
         back_ref[...] = jnp.zeros_like(back_ref)
-
+        for copy in copies:
+            copy.wait()
+
+    block = jnp.int32(0)
+    for number in range(count):
+        block = jnp.where(step == number, steps[number][0](coords_ref), block)
+
+        @pl.when(step == number)
+        def _(number=number):
+            if number + 1 < count:
+                for copy in u_load(number + 1):
+                    copy.start()
+            if number >= 2:
+                for copy in u_store(number - 2):
+                    copy.wait()
+            for copy in u_load(number):
+                copy.wait()
+
+    columns = pl.ds(pl.multiple_of(block * tile, tile), tile)
     feed = feed_ref[...]
     grad = grad_ref[...]
-    weight = inner_ref[...]
-    value = jnp.dot(feed, weight, preferred_element_type=F32) + bias_ref[...]
+    inner = weight[:, columns]
+    value = jnp.dot(feed, inner, preferred_element_type=F32) + bias_ref[:, columns]
     square = value * value
     bend = jnp.tanh(GELU_A * (value + GELU_B * (square * value)))
     half = 0.5 * (1.0 + bend)
     active = (value * half).astype(BF)
     slope = half + 0.5 * value * (1.0 - bend * bend) * (GELU_A * (1.0 + 3.0 * GELU_B * square))
-    out_ref[...] += jnp.dot(active, outer_ref[...], preferred_element_type=F32)
-    outer_grad_ref[...] = lax.dot_general(active, grad, (((0,), (0,)), ((), ())), preferred_element_type=F32).astype(BF)
-    pulled = lax.dot_general(grad, outer_ref[...], (((1,), (1,)), ((), ())), preferred_element_type=F32)
+    out_ref[...] += jnp.dot(active, outer[slot], preferred_element_type=F32)
+    outer_sum[slot] = lax.dot_general(active, grad, (((0,), (0,)), ((), ())), preferred_element_type=F32).astype(BF)
+    pulled = lax.dot_general(grad, outer[slot], (((1,), (1,)), ((), ())), preferred_element_type=F32)
     inner_low = (pulled * slope).astype(BF)
-    bias_grad_ref[...] = jnp.sum(inner_low.astype(F32), axis=0, keepdims=True)
-    inner_grad_ref[...] = lax.dot_general(feed, inner_low, (((0,), (0,)), ((), ())), preferred_element_type=F32).astype(BF)
-    back_ref[...] += lax.dot_general(inner_low, weight, (((1,), (1,)), ((), ())), preferred_element_type=F32)
-
-
-def feed_call(rows, features, hidden, tile):
-    fixed = pl.BlockSpec((rows, features), lambda j: (0, 0))
-    return pl.pallas_call(
-        feed_kernel,
-        grid=(hidden // tile,),
-        in_specs=[
-            fixed,
-            fixed,
-            pl.BlockSpec((features, tile), lambda j: (0, j)),
-            pl.BlockSpec((1, tile), lambda j: (0, j)),
-            pl.BlockSpec((tile, features), lambda j: (j, 0)),
+    bias_sum[:, columns] = jnp.sum(inner_low.astype(F32), axis=0, keepdims=True)
+    weight_sum[:, columns] = lax.dot_general(feed, inner_low, (((0,), (0,)), ((), ())), preferred_element_type=F32).astype(BF)
+    back_ref[...] += lax.dot_general(inner_low, inner, (((1,), (1,)), ((), ())), preferred_element_type=F32)
+
+    for number in range(count):
+
+        @pl.when(step == number)
+        def _(number=number):
+            for copy in u_store(number):
+                copy.start()
+            if number == count - 1:
+                copies = store_pieces(coords_ref, weight_sum, i_grads, i_outs, iout_sems, 0)
+                for copy in copies:
+                    copy.start()
+                if count > 1:
+                    for copy in u_store(number - 1):
+                        copy.wait()
+                for copy in u_store(number):
+                    copy.wait()
+                for copy in copies:
+                    copy.wait()
+
+
+def feed_call(coords, feed, grad, bias, i_side, u_side, i_form, u_form):
+    i_arrays, i_pieces = i_side
+    u_arrays, steps = u_side
+    i_shapes, i_outs = i_form
+    u_shapes, step_outs = u_form
+    rows, features = feed.shape
+    hidden = bias.shape[1]
+    tile = hidden // len(steps)
+    most = max(len(pieces) for _, pieces in steps)
+    made = kernel_call(
+        functools.partial(feed_kernel, (i_pieces, i_outs, steps, step_outs), (len(i_arrays), len(u_arrays), len(i_shapes), len(u_shapes))),
+        [VM] * 3 + [ANYWHERE] * (len(i_arrays) + len(u_arrays)),
+        (
+            [VM] * 3 + [ANYWHERE] * (len(i_shapes) + len(u_shapes)),
+            [jax.ShapeDtypeStruct((rows, features), F32)] * 2
+            + [jax.ShapeDtypeStruct((1, hidden), F32)]
+            + [jax.ShapeDtypeStruct(s, BF) for s in i_shapes + u_shapes],
+        ),
+        [
+            pltpu.VMEM((features, hidden), BF),
+            pltpu.VMEM((features, hidden), BF),
+            pltpu.VMEM((2, tile, features), BF),
+            pltpu.VMEM((2, tile, features), BF),
+            pltpu.SemaphoreType.DMA((len(i_pieces),)),
+            pltpu.SemaphoreType.DMA((2, most)),
+            pltpu.SemaphoreType.DMA((len(i_outs),)),
+            pltpu.SemaphoreType.DMA((2, most)),
         ],
-        out_specs=[
-            fixed,
-            fixed,
-            pl.BlockSpec((features, tile), lambda j: (0, j)),
-            pl.BlockSpec((tile, features), lambda j: (j, 0)),
-            pl.BlockSpec((1, tile), lambda j: (0, j)),
-        ],
-        out_shape=[
-            jax.ShapeDtypeStruct((rows, features), F32),
-            jax.ShapeDtypeStruct((rows, features), F32),
-            jax.ShapeDtypeStruct((features, hidden), BF),
-            jax.ShapeDtypeStruct((hidden, features), BF),
-            jax.ShapeDtypeStruct((1, hidden), F32),
-        ],
-        compiler_params=pltpu.CompilerParams(vmem_limit_bytes=60 << 20),
-        name="feed_forward_backward",
-    )
+        "feed_forward_backward",
+        60,
+        grid=(len(steps),),
+    )(coords, feed, grad, bias, *i_arrays, *u_arrays)
+    return made[0], made[1], made[2], made[3:3 + len(i_shapes)], made[3 + len(i_shapes):]
 
 
 def pick(flag, when_true, when_false):
@@ -336,7 +601,7 @@
         blocks = partial.reshape(2, 2, -1, partial.shape[1])
         keep = pick(self.odd, blocks[:, 1], blocks[:, 0])
         got = self.near(pick(self.odd, blocks[:, 0], blocks[:, 1]).astype(BF))
-        return self.swap_trees((keep + got.astype(F32)).astype(BF)).astype(F32)
+        return self.swap_trees((keep.astype(F32) + got.astype(F32)).astype(BF)).astype(F32)
 
 
 class GroupPlan:
@@ -367,8 +632,291 @@
 
     def partial_to_rows(self, partial):
         every = jnp.zeros((self.trees,) + partial.shape, F32)
-        every = lax.dynamic_update_index_in_dim(every, partial, self.tree, 0)
+        every = lax.dynamic_update_index_in_dim(every, partial.astype(F32), self.tree, 0)
         return lax.psum_scatter(every, "fsdp", scatter_dimension=1, tiled=True)
+
+
+def low(value):
+    return value.astype(BF)
+
+
+def wide_of(value):
+    return value.astype(F32)
+
+
+def swap_pairs(size, bit):
+    return [(i, i ^ bit) for i in range(size)]
+
+
+class LinkMoves:
+    def __init__(self):
+        dp, fsdp = lax.axis_index("dp"), lax.axis_index("fsdp")
+        self.bits = [fsdp % 2, fsdp // 2, dp % 2, dp // 2 % 2, dp // 4]
+        self.coords = jnp.stack([dp // 2, dp % 2, fsdp // 2, fsdp % 2]).astype(jnp.int32)
+        self.odd = fsdp % 2 == 1
+
+    def core(self, value):
+        return lax.ppermute(value, "fsdp", swap_pairs(4, 1))
+
+    def over_y(self, value):
+        return lax.ppermute(value, "fsdp", swap_pairs(4, 2))
+
+    def over_x(self, value):
+        return lax.ppermute(value, "dp", swap_pairs(8, 1))
+
+    def up_z(self, value):
+        return lax.ppermute(value, "dp", [(i, (i + 2) % 8) for i in range(8)])
+
+    def bit_move(self, bit, value):
+        if bit < 2:
+            return lax.ppermute(value, "fsdp", swap_pairs(4, 1 << bit))
+        return lax.ppermute(value, "dp", swap_pairs(8, 1 << (bit - 2)))
+
+    def ring(self, value):
+        made = [value]
+        for _ in range(3):
+            made.append(self.up_z(made[-1]))
+        return made
+
+    def ring_sum(self, blocks):
+        total = blocks[1]
+        for k in (2, 3, 0):
+            total = wide_of(self.up_z(low(total))) + blocks[k]
+        return total
+
+    def gather_small(self, shard):
+        made = shard
+        for bit in range(5):
+            got = self.bit_move(bit, made)
+            one = self.bits[bit] == 1
+            made = pick(one, jnp.concatenate([got, made]), jnp.concatenate([made, got]))
+        return made
+
+    def scatter_small(self, total):
+        made = total
+        for bit in (4, 3, 2, 1, 0):
+            half = made.shape[0] // 2
+            one = self.bits[bit] == 1
+            keep = pick(one, made[half:], made[:half])
+            made = keep + self.bit_move(bit, pick(one, made[:half], made[half:]))
+        return made
+
+    @staticmethod
+    def place32(k, rx, ry, rc):
+        return lambda co: ((((co[0] + 4 - k) & 3) * 2 + (co[1] ^ rx)) * 2 + (co[2] ^ ry)) * 2 + (co[3] ^ rc)
+
+    @staticmethod
+    def place16(k, rx, ry):
+        return lambda co: (((co[0] + 4 - k) & 3) * 2 + (co[1] ^ rx)) * 2 + (co[2] ^ ry)
+
+    @staticmethod
+    def place8(k, rx):
+        return lambda co: ((co[0] + 4 - k) & 3) * 2 + (co[1] ^ rx)
+
+    @staticmethod
+    def place4(ry, rc):
+        return lambda co: (co[2] ^ ry) * 2 + (co[3] ^ rc)
+
+    def gather_heads(self, query, value):
+        count, features = query.shape
+        half = features // 2
+        both = jnp.stack([query, value])
+        keep = pick(self.odd, both[:, :, half:], both[:, :, :half])
+        got = self.core(pick(self.odd, both[:, :, :half], both[:, :, half:]))
+        chip = pick(self.odd, jnp.concatenate([got, keep], axis=1), jnp.concatenate([keep, got], axis=1))
+        made = self.ring(chip)
+        sides = []
+        for which, first, second in ((0, self.over_y, self.over_x), (1, self.over_x, self.over_y)):
+            near = jnp.stack([m[which] for m in made])
+            near = jnp.stack([near, first(near)])
+            arrays = [near, second(near)]
+            pieces = []
+            for outer in range(2):
+                for inner in range(2):
+                    for k in range(4):
+                        rx, ry = (outer, inner) if which == 0 else (inner, outer)
+                        pieces.append((outer, (inner, k), None, 2 * count, self.place16(k, rx, ry)))
+            sides.append((arrays, pieces))
+        return sides
+
+    def heads_form(self, count, half):
+        shapes = [(2, 4, 2 * count, half)] * 2
+        forms = []
+        for which in range(2):
+            pieces = []
+            for outer in range(2):
+                for inner in range(2):
+                    for k in range(4):
+                        rx, ry = (outer, inner) if which == 0 else (inner, outer)
+                        pieces.append((outer, (inner, k), None, 2 * count, self.place16(k, rx, ry)))
+            forms.append((shapes, pieces))
+        return forms
+
+    def sum_heads(self, query, value):
+        totals = []
+        for parts, first, second in ((query, self.over_x, self.over_y), (value, self.over_y, self.over_x)):
+            made = wide_of(parts[0]) + wide_of(first(parts[1]))
+            made = made[0] + wide_of(second(low(made[1])))
+            totals.append(self.ring_sum([made[k] for k in range(4)]))
+        both = jnp.stack(totals)
+        count = both.shape[1] // 2
+        keep = pick(self.odd, both[:, count:], both[:, :count])
+        got = wide_of(self.core(low(pick(self.odd, both[:, :count], both[:, count:]))))
+        full = pick(self.odd, jnp.concatenate([got, keep], axis=2), jnp.concatenate([keep, got], axis=2))
+        return full[0], full[1]
+
+    def gather_inner(self, shard):
+        near = jnp.stack([shard, self.over_y(shard)])
+        plane = jnp.stack([near, self.over_x(near)])
+        made = self.ring(plane)
+        arrays = made + [self.core(m) for m in made]
+        count = shard.shape[0]
+        pieces = [
+            (rc * 4 + k, (rx, ry), None, count, self.place32(k, rx, ry, rc))
+            for rc in range(2)
+            for k in range(4)
+            for rx in range(2)
+            for ry in range(2)
+        ]
+        return arrays, pieces
+
+    def inner_form(self, count, hidden):
+        pieces = [
+            (rc * 4 + k, (rx, ry), None, count, self.place32(k, rx, ry, rc))
+            for rc in range(2)
+            for k in range(4)
+            for rx in range(2)
+            for ry in range(2)
+        ]
+        return [(2, 2, count, hidden)] * 8, pieces
+
+    def sum_inner(self, parts):
+        shares = [None] * 4
+        for k in (1, 2, 3, 0):
+            shares[k] = wide_of(parts[k]) + wide_of(self.core(parts[4 + k]))
+        made = self.ring_sum(shares)
+        made = made[0] + wide_of(self.over_x(low(made[1])))
+        return made[0] + wide_of(self.over_y(low(made[1])))
+
+    def gather_outer(self, outer, output):
+        count, extra = outer.shape[0], output.shape[0]
+        made = jnp.stack(self.ring(jnp.concatenate([outer, output])))
+        near = jnp.stack([made, self.over_y(made)])
+        across = self.over_x(near)
+        arrays = [near, across, self.core(near), self.core(across)]
+        steps = []
+        for rx in range(2):
+            for k in range(4):
+                pieces = [(rc * 2 + rx, (ry, k), 0, count, self.place4(ry, rc)) for ry in range(2) for rc in range(2)]
+                steps.append((self.place8(k, rx), pieces))
+        output_pieces = [
+            (rc * 2 + rx, (ry, k), count, extra, self.place32(k, rx, ry, rc))
+            for rc in range(2)
+            for rx in range(2)
+            for ry in range(2)
+            for k in range(4)
+        ]
+        return (arrays, steps), (arrays, output_pieces)
+
+    def outer_form(self, count, features):
+        steps = []
+        for rx in range(2):
+            for k in range(4):
+                steps.append([(rc * 2 + rx, (ry, k), None, count, self.place4(ry, rc)) for ry in range(2) for rc in range(2)])
+        return [(2, 4, count, features)] * 4, steps
+
+    def output_form(self, count, features):
+        pieces = [
+            (rc * 2 + rx, (ry, k), None, count, self.place32(k, rx, ry, rc))
+            for rc in range(2)
+            for rx in range(2)
+            for ry in range(2)
+            for k in range(4)
+        ]
+        return [(2, 4, count, features)] * 4, pieces
+
+    def sum_outer(self, outer, output):
+        halves = []
+        for parts in (outer, output):
+            sent = low(wide_of(parts[1]) + wide_of(self.core(parts[3])))
+            halves.append(wide_of(parts[0]) + wide_of(self.core(parts[2])) + wide_of(self.over_x(sent)))
+        made = jnp.concatenate([low(h[1]) for h in halves], axis=1)
+        made = wide_of(self.over_y(made)) + jnp.concatenate([h[0] for h in halves], axis=1)
+        total = self.ring_sum([made[k] for k in range(4)])
+        count = outer[0].shape[2]
+        return total[:count], total[count:]
+
+
+class PlainMoves:
+    def __init__(self, plan, wide):
+        self.plan = plan
+        self.wide = wide
+        self.coords = jnp.zeros((4,), jnp.int32)
+
+    @staticmethod
+    def start(co):
+        return co[0] * 0
+
+    def gather(self, shard):
+        return lax.all_gather(shard, AXES, axis=0, tiled=True)
+
+    def scatter(self, total):
+        return lax.psum_scatter(total, AXES, scatter_dimension=0, tiled=True)
+
+    def whole(self, rows):
+        return [(0, (), None, rows, self.start)]
+
+    def gather_small(self, shard):
+        return self.gather(shard)
+
+    def scatter_small(self, total):
+        return self.scatter(total)
+
+    def gather_heads(self, query, value):
+        sides = []
+        for shard in (query, value):
+            cols = lax.dynamic_slice_in_dim(self.gather(shard), self.plan.head_group * self.wide, self.wide, 1)
+            sides.append(([cols], self.whole(cols.shape[0])))
+        return sides
+
+    def heads_form(self, count, half):
+        features = H * DH
+        return [([(features, self.wide)], self.whole(features))] * 2
+
+    def sum_heads(self, query, value):
+        made = []
+        for cols in (query[0], value[0]):
+            full = jnp.zeros((cols.shape[0], H * DH), F32)
+            made.append(self.scatter(lax.dynamic_update_slice_in_dim(full, wide_of(cols), self.plan.head_group * self.wide, 1)))
+        return made
+
+    def gather_inner(self, shard):
+        full = self.gather(shard)
+        self.features, self.hidden = full.shape
+        return [full], self.whole(full.shape[0])
+
+    def inner_form(self, count, hidden):
+        return [(self.features, hidden)], self.whole(self.features)
+
+    def sum_inner(self, parts):
+        return self.scatter(wide_of(parts[0]))
+
+    def gather_outer(self, outer, output):
+        self.steps = self.hidden // 512
+        full = self.gather(outer).reshape(self.steps, -1, outer.shape[1])
+        steps = [((lambda co, s=s: co[0] * 0 + s), [(0, (s,), None, full.shape[1], self.start)]) for s in range(self.steps)]
+        other = self.gather(output)
+        return ([full], steps), ([other], self.whole(other.shape[0]))
+
+    def outer_form(self, count, features):
+        tile = self.hidden // self.steps
+        return [(self.steps, tile, features)], [[(0, (s,), None, tile, self.start)] for s in range(self.steps)]
+
+    def output_form(self, count, features):
+        return [(H * DH, features)], self.whole(H * DH)
+
+    def sum_outer(self, outer, output):
+        return self.scatter(wide_of(outer[0]).reshape(self.hidden, -1)), self.scatter(wide_of(output[0]))
 
 
 def per_device(
@@ -403,38 +951,36 @@
     segments = parents.shape[2]
     all_rows = trees * row_count
     devices = dp_size * fsdp_size
-    plan = PairPlan() if (fsdp_size, trees) == (4, 2) else GroupPlan(fsdp_size, trees)
     local_heads = H // (fsdp_size // trees)
     wide = local_heads * DH
+    linked = (dp_size, fsdp_size, trees) == (8, 4, 2)
+    plan = PairPlan() if linked else GroupPlan(fsdp_size, trees)
+    moves = LinkMoves() if linked else PlainMoves(plan, wide)
+    coords = moves.coords
 
     first = first_half[:, 0]
     second = second_half[:, 0]
-    grad_a = grad_first[:, 0]
     grad_b = grad_second[:, 0]
 
-    def gather(shard):
-        return lax.all_gather(shard, AXES, axis=0, tiled=True)
-
-    small_sizes = [v.shape[0] for v in (inner_bias, outer_bias, mixer_gain, mixer_shift, feed_gain, feed_shift)]
-    small = lax.all_gather(
-        jnp.concatenate([inner_bias, outer_bias, mixer_gain, mixer_shift, feed_gain, feed_shift])[None], AXES, axis=0, tiled=True
-    ).astype(F32)
+    def flat(value):
+        return value.reshape(all_rows, features)
+
+    small_parts = (inner_bias, outer_bias, mixer_gain, mixer_shift, feed_gain, feed_shift)
+    small_sizes = [v.shape[0] for v in small_parts]
+    small = wide_of(moves.gather_small(jnp.concatenate(small_parts)[None]))
     vectors = []
     begin = 0
     for size in small_sizes:
-        vectors.append(small[:, begin:begin + size].reshape(-1))
+        vectors.append(small[:, begin:begin + size].reshape(1, -1))
         begin += size
     bias_inner, bias_outer, gain_mix, shift_mix, gain_feed, shift_feed = vectors
 
-    query_full = gather(query_weight)
-    value_full = gather(value_weight)
-    output_full = gather(output_weight)
-    inner_full = gather(inner_weight)
-    outer_full = gather(outer_weight)
+    q_side, v_side = moves.gather_heads(query_weight, value_weight)
+    i_side = moves.gather_inner(inner_weight)
+    u_side, o_side = moves.gather_outer(outer_weight, output_weight)
 
     mix_unit, mix_factor = norm_stats(second)
-    mixed_low = (mix_unit * gain_mix + shift_mix).astype(BF)
-    mixed_tree = plan.rows_to_tree(mixed_low)
+    mixed_tree = plan.rows_to_tree(low(mix_unit * gain_mix + shift_mix))
     parent_row = lax.dynamic_index_in_dim(parents[:, 0], plan.tree, 0, False)
     bucket_rows = lax.dynamic_index_in_dim(buckets[:, 0], plan.tree, 0, False)
     branch = parent_row[jnp.clip(parent_row, 0, segments - 1)]
@@ -443,70 +989,59 @@
     codes = position_codes(bucket_rows)
     codes_q = jnp.pad(codes, ((0, 0), (0, 128 - rounds)))
     codes_k = jnp.pad(codes.T, ((0, 8 - rounds), (0, 0)))
-    query_cols = lax.dynamic_slice_in_dim(query_full, plan.head_group * wide, wide, 1)
-    value_cols = lax.dynamic_slice_in_dim(value_full, plan.head_group * wide, wide, 1)
-    query_key = jnp.dot(mixed_tree, query_cols, preferred_element_type=F32).astype(BF)
-    value_rows = jnp.dot(mixed_tree, value_cols, preferred_element_type=F32).astype(BF)
+    query_key, value_rows = project(coords, mixed_tree, q_side, v_side, wide)
     attend, attend_back = attention_calls(tree_len, local_heads, rounds, segments)
     attended, totals, counts = attend(info, query_key, value_rows, codes_q, codes_k)
-    attended_low = plan.heads_to_rows(attended)
-
-    first_out = first + jnp.dot(attended_low.reshape(all_rows, features), output_full, preferred_element_type=F32).reshape(first.shape)
-    feed_unit, feed_factor = norm_stats(first_out)
-    feed_low = (feed_unit * gain_feed + shift_feed).astype(BF).reshape(all_rows, features)
-    outer_low = grad_b.astype(BF).reshape(all_rows, features)
-    fed, grad_feed, inner_grad, outer_grad, inner_bias_sum = feed_call(all_rows, features, hidden, 512)(
-        feed_low, outer_low, inner_full, bias_inner[None], outer_full
+    attended_low = flat(plan.heads_to_rows(attended))
+
+    first_out, feed_low = out_project(coords, attended_low, flat(first), gain_feed, shift_feed, o_side)
+    outer_low = flat(low(grad_b))
+    i_form = moves.inner_form(inner_weight.shape[0], hidden)
+    u_form = moves.outer_form(outer_weight.shape[0], features)
+    fed, grad_feed, inner_bias_sum, inner_parts, outer_parts = feed_call(coords, feed_low, outer_low, bias_inner, i_side, u_side, i_form, u_form)
+    second_out = second + fed.reshape(second.shape) + bias_outer
+    outer_bias_sum = jnp.sum(wide_of(outer_low), axis=0)
+    (grad_first_in, grad_attended, feed_gain_sum, feed_shift_sum), output_parts = out_back(
+        coords,
+        grad_feed,
+        first_out,
+        flat(grad_first),
+        attended_low,
+        gain_feed,
+        o_side,
+        moves.output_form(output_weight.shape[0], features),
     )
-    second_out = second + fed.reshape(second.shape) + bias_outer
-    outer_bias_sum = jnp.sum(outer_low.astype(F32), axis=0)
-    grad_feed = grad_feed.reshape(first.shape)
-    feed_gain_sum = jnp.sum(grad_feed * feed_unit, axis=(0, 1))
-    feed_shift_sum = jnp.sum(grad_feed, axis=(0, 1))
-    grad_first_in = grad_a + norm_back(feed_unit, feed_factor, gain_feed, grad_feed)
-    branch_low = grad_first_in.astype(BF).reshape(all_rows, features)
-
-    output_grad = lax.dot_general(
-        attended_low.reshape(all_rows, features), branch_low, (((0,), (0,)), ((), ())), preferred_element_type=F32
-    ).astype(BF)
-    grad_attended = lax.dot_general(branch_low, output_full, (((1,), (1,)), ((), ())), preferred_element_type=F32).astype(BF)
+
     grad_heads = plan.rows_to_heads(grad_attended.reshape(trees, row_count, features))
     query_low, value_low = attend_back(info, query_key, value_rows, attended, grad_heads, totals, counts)
-    query_grad = lax.dot_general(mixed_tree, query_low, (((0,), (0,)), ((), ())), preferred_element_type=F32).astype(BF)
-    value_grad = lax.dot_general(mixed_tree, value_low, (((0,), (0,)), ((), ())), preferred_element_type=F32).astype(BF)
-    partial = lax.dot_general(query_low, query_cols, (((1,), (1,)), ((), ())), preferred_element_type=F32) + lax.dot_general(
-        value_low, value_cols, (((1,), (1,)), ((), ())), preferred_element_type=F32
-    )
+    q_form, v_form = moves.heads_form(query_weight.shape[0], wide)
+    partial, query_parts, value_parts = project_back(coords, mixed_tree, query_low, value_low, q_side, v_side, q_form, v_form)
     grad_mixed = plan.partial_to_rows(partial)
     mix_gain_sum = jnp.sum(grad_mixed * mix_unit, axis=(0, 1))
     mix_shift_sum = jnp.sum(grad_mixed, axis=(0, 1))
     grad_second_in = grad_b + norm_back(mix_unit, mix_factor, gain_mix, grad_mixed)
 
-    def scatter(total):
-        return lax.psum_scatter(total, AXES, scatter_dimension=0, tiled=True).astype(F32)
-
-    def spread(cols):
-        return lax.dynamic_update_slice_in_dim(jnp.zeros((features, features), BF), cols, plan.head_group * wide, 1)
-
-    small_sums = [inner_bias_sum[0], outer_bias_sum, mix_gain_sum, mix_shift_sum, feed_gain_sum, feed_shift_sum]
-    packed = jnp.concatenate([v.reshape(devices, -1) for v in small_sums], axis=1)
-    packed = lax.psum_scatter(packed, AXES, scatter_dimension=0, tiled=True)[0]
+    inner_grad = moves.sum_inner(inner_parts)
+    outer_grad, output_grad = moves.sum_outer(outer_parts, output_parts)
+    query_grad, value_grad = moves.sum_heads(query_parts, value_parts)
+    small_sums = [inner_bias_sum, outer_bias_sum, mix_gain_sum, mix_shift_sum, feed_gain_sum, feed_shift_sum]
+    packed = moves.scatter_small(jnp.concatenate([v.reshape(devices, -1) for v in small_sums], axis=1))[0]
     pieces = []
     begin = 0
     for size in small_sizes:
         pieces.append(packed[begin:begin + size])
         begin += size
     return (
-        first_out[:, None],
+        first_out.reshape(first_half.shape),
         second_out[:, None],
-        grad_first_in[:, None],
+        grad_first_in.reshape(first_half.shape),
         grad_second_in[:, None],
-        scatter(spread(query_grad)),
-        scatter(spread(value_grad)),
-        scatter(output_grad),
-        scatter(inner_grad),
+        query_grad,
+        value_grad,
+        output_grad,
+        inner_grad,
         pieces[0],
-        scatter(outer_grad),
+        outer_grad,
         pieces[1],
         pieces[2],
         pieces[3],

time: 1120 us -> 602 us (0.54)
  waiting for transfers between devices: 824 us -> 328 us
  blocking collectives: 84 us -> 0 us
  Pallas kernels: 83.3 us -> 133 us
  starting transfers between devices: 9.12 us -> 39.2 us
  matrix products: 28.6 us -> 1.02 us
  other arithmetic: 44 us -> 58.7 us
  between operations: 15.1 us -> 2.47 us
    reduce_scatter x5 -> x0, waiting for transfers between devices: 550 us -> none  [scatter(): lax.psum_scatter(total, AXES, scatter_dimension=0, tiled=True).astype(F32)]
    ppermute x0 -> x64, waiting for transfers between devices: none -> 295 us  [the longest x21 89.9 us: up_z(): return lax.ppermute(value, 'dp', [(i, (i + 2) % 8) for i in range(8)])]
    all_gather x5 -> x0, waiting for transfers between devices: 200 us -> none  [gather(): return lax.all_gather(shard, AXES, axis=0, tiled=True)]
    unnamed x2 -> x0, blocking collectives: 84 us -> none
    pallas_call x1 -> x5, Pallas kernels: 43.8 us -> 93.7 us  [the longest x1 53.6 us: feed_call(): kernel_call(functools.partial(feed_kernel, (i_pieces, i_outs, steps, step...]
    ppermute x0 -> x64, starting transfers between devices: none -> 35.6 us  [the longest x9 11.7 us: over_x(): return lax.ppermute(value, 'dp', swap_pairs(8, 1))]
    ppermute x4, waiting for transfers between devices: 60.1 us -> 31.9 us  [far(): return lax.ppermute(value, 'fsdp', [(i, i ^ 2) for i in range(4)])]
    dot_general x9 -> x0, matrix products: 27.6 us -> none  [the longest x1 4.41 us: per_device(): jnp.dot(attended_low.reshape(all_rows, features), output_full, preferred_...]
  transfers between devices with their start and end apart: 18 -> 72, of which waited for: 16 -> 35; matrix products, arithmetic and copies ran while one was open for 6% -> 13% of each run, Pallas kernels for 4% -> 11%
where the time goes in v2:
time: 602 us; the launch traced here: 595 us
  waiting for transfers between devices  328 us (54%)
  Pallas kernels  133 us (22%)
  other arithmetic  58.7 us (10%)
  starting transfers between devices  39.2 us (7%)
  local copies, waits for them, and re-layouts  32.6 us (5%)
    ppermute x21, waiting for transfers between devices, up_z(): return lax.ppermute(value, 'dp', [(i, (i + 2) % 8) for i in range(8)])  89.9 us
    ppermute x8, waiting for transfers between devices, over_y(): return lax.ppermute(value, 'fsdp', swap_pairs(4, 2))  77.1 us
    ppermute x9, waiting for transfers between devices, over_x(): return lax.ppermute(value, 'dp', swap_pairs(8, 1))  60.9 us
    ppermute x6, waiting for transfers between devices, bit_move(): return lax.ppermute(value, 'dp', swap_pairs(8, 1 << bit - 2))  59.6 us
    pallas_call x1, Pallas kernels, feed_call(): kernel_call(functools.partial(feed_kernel, (i_pieces, i_outs, steps, step...  53.6 us
    ppermute x4, waiting for transfers between devices, far(): return lax.ppermute(value, 'fsdp', [(i, i ^ 2) for i in range(4)])  31.9 us
    pallas_call x1, Pallas kernels, per_device(): attend_back(info, query_key, value_rows, attended, grad_heads, totals, co...  21.1 us
    pallas_call x1, Pallas kernels, per_device(): attend(info, query_key, value_rows, codes_q, codes_k)  18 us
  transfers between devices with their start and end apart: 72, of which 35 were waited for; matrix products, arithmetic and copies ran while one was open for 13% of the time, Pallas kernels for 11%

profile of v2, /device:TPU:0, one launch (start us, length us, event | category | flops | bytes accessed | tf_op | source)
XLA Modules:
  0.0 595.1 jit_solution(5061153856276436225)
XLA Ops:
  0.6 4.1 concatenate.71
  10.0 3.0 collective-permute-start.17
  23.9 3.1 collective-permute-done.1
  28.5 2.1 collective-permute-done.2
  32.3 2.0 collective-permute-done.3
  34.3 2.6 collective-permute-start.4
  37.6 4.7 collective-permute-done.4
  43.7 11.2 %collective-permute-done.18 = bf16[160,1024]{1,0:T(8,128)(2,1)S(1)} collective-permute-done((bf16[160,1024]{1,0:T(8,128)(2,1)}, bf16[160,1024]{1,0:T(8,128)(2,1)S(1)}, u32[]{:S(2)}, u32[]{:S(2)}) %collective-permute-start.18) | collective-permute-done | bytes 327712 | tf_op jit(solution)/shard_map/ppermute | solution.py:668
  56.5 7.6 %collective-permute-done.19 = bf16[160,1024]{1,0:T(8,128)(2,1)S(1)} collective-permute-done((bf16[160,1024]{1,0:T(8,128)(2,1)S(1)}, bf16[160,1024]{1,0:T(8,128)(2,1)S(1)}, u32[]{:S(2)}, u32[]{:S(2)}) %collective-permute-start.19) | collective-permute-done | bytes 327712 | tf_op jit(solution)/shard_map/ppermute | solution.py:668
  67.8 5.1 collective-permute-done.9
  73.1 18.1 %collective-permute-done.20 = bf16[4,160,1024]{2,1,0:T(8,128)(2,1)S(1)} collective-permute-done((bf16[4,160,1024]{2,1,0:T(8,128)(2,1)S(1)}, bf16[4,160,1024]{2,1,0:T(8,128)(2,1)S(1)}, u32[]{:S(2)}, u32[]{:S(2)}) %collective-permute-start.20) | collective-permute-done | bytes 1310752 | tf_op jit(solution)/shard_map/ppermute | solution.py:662
  98.0 7.5 %collective-permute-done.11 = bf16[4,64,512]{2,1,0:T(8,128)(2,1)S(1)} collective-permute-done((bf16[4,64,512]{2,1,0:T(8,128)(2,1)S(1)}, bf16[4,64,512]{2,1,0:T(8,128)(2,1)S(1)}, u32[]{:S(2)}, u32[]{:S(2)}) %collective-permute-start.11) | collective-permute-done | bytes 262176 | tf_op jit(solution)/shard_map/ppermute | solution.py:662
  106.1 47.5 %collective-permute-done.13 = bf16[4,64,512]{2,1,0:T(8,128)(2,1)S(1)} collective-permute-done((bf16[4,64,512]{2,1,0:T(8,128)(2,1)S(1)}, bf16[4,64,512]{2,1,0:T(8,128)(2,1)S(1)}, u32[]{:S(2)}, u32[]{:S(2)}) %collective-permute-start.13) | collective-permute-done | bytes 262176 | tf_op jit(solution)/shard_map/ppermute | solution.py:665
  159.3 9.8 %collective-permute-done.14.refs_3_ = bf16[2,4,64,512]{3,2,1,0:T(8,128)(2,1)} collective-permute-done((bf16[2,4,64,512]{3,2,1,0:T(8,128)(2,1)}, bf16[2,4,64,512]{3,2,1,0:T(8,128)(2,1)}, u32[]{:S(2)}, u32[]{:S(2)}) %collective-permute-start.14) | collective-permute-done | bytes 524320 | tf_op jit(solution)/shard_map/ppermute | solution.py:662
  169.1 5.7 project.1
  174.8 18.0 %attention_forward.1 = (bf16[1280,512]{1,0:T(8,128)(2,1)S(1)}, f32[1280,128]{1,0:T(8,128)S(1)}, bf16[1280,768]{1,0:T(8,128)(2,1)S(1)}) custom-call(s32[20]{0:T(128)S(1)} %pad_add_fusion.1.info_ref, bf16[1280,512]{1,0:T(8,128)(2,1)S(1)} %get-tuple-element.52.q_ref, bf16[1280,512]{1,0:T(8,128)(2,1)S(1)} %get-tuple-element.53.v_ref, ...), custom_call_target="tpu_custom_call" | custom-call | tf_op jit(solution)/shard_map/attention_forward/pallas_call | solution.py:994
  196.1 16.3 %collective-permute-done.16 = bf16[320,1024]{1,0:T(8,128)(2,1)S(1)} collective-permute-done((bf16[320,1024]{1,0:T(8,128)(2,1)S(1)}, bf16[320,1024]{1,0:T(8,128)(2,1)S(1)}, u32[]{:S(2)}, u32[]{:S(2)}) %collective-permute-start.16) | collective-permute-done | bytes 655392 | tf_op jit(solution)/shard_map/ppermute | solution.py:568
  213.2 7.6 %collective-permute-done.28.refs_3_ = bf16[2,2,32,4096]{3,2,1,0:T(8,128)(2,1)} collective-permute-done((bf16[2,2,32,4096]{3,2,1,0:T(8,128)(2,1)}, bf16[2,2,32,4096]{3,2,1,0:T(8,128)(2,1)}, u32[]{:S(2)}, u32[]{:S(2)}) %collective-permute-start.28) | collective-permute-done | bytes 1048608 | tf_op jit(solution)/shard_map/ppermute | solution.py:668
  225.1 7.3 %out_project.1 = (f32[640,1024]{1,0:T(8,128)}, bf16[640,1024]{1,0:T(8,128)(2,1)S(1)}) custom-call(s32[4]{0:T(128)S(1)} %pad_add_fusion.coords_ref, bf16[640,1024]{1,0:T(8,128)(2,1)S(1)} %bitcast.294, f32[640,1024]{1,0:T(8,128)} %bitcast.306, f32[1,1024]{1,0:T(1,128)S(1)} %reshape.312.gain_ref, f32[1,1024]{1,0:T(1,128)S(1)} %reshape.313.shift_ref, ...), custom_call_target="tpu_custom_call" | custom-call | tf_op jit(solution)/shard_map/out_project/pallas_call | solution.py:377
  233.4 53.6 %feed_forward_backward.1 = (f32[640,1024]{1,0:T(8,128)}, f32[640,1024]{1,0:T(8,128)}, f32[1,4096]{1,0:T(1,128)}, bf16[2,2,32,4096]{3,2,1,0:T(8,128)(2,1)}, bf16[...) custom-call(s32[4]{0:T(128)} %copy-done.14, ...), custom_call_target="tpu_custom_call" | custom-call | tf_op jit(solution)/shard_map/feed_forward_backward/pallas_call | solution.py:526
  287.1 11.8 %out_back.1 = (f32[640,1024]{1,0:T(8,128)}, bf16[640,1024]{1,0:T(8,128)(2,1)}, f32[1,1024]{1,0:T(1,128)}, f32[1,1024]{1,0:T(1,128)}, bf16[2,4,32,1024]{3,2,1,0:T...) custom-call(s32[4]{0:T(128)} %copy-done.14, ...), custom_call_target="tpu_custom_call" | custom-call | tf_op jit(solution)/shard_map/out_back/pallas_call | solution.py:422
  299.0 2.3 broadcast_select_fusion.7
  310.1 8.6 %collective-permute-done.33 = bf16[320,1024]{1,0:T(8,128)(2,1)} collective-permute-done((bf16[320,1024]{1,0:T(8,128)(2,1)}, bf16[320,1024]{1,0:T(8,128)(2,1)}, u32[]{:S(2)}, u32[]{:S(2)}) %collective-permute-start.33) | collective-permute-done | bytes 655392 | tf_op jit(solution)/shard_map/ppermute | solution.py:568
  323.1 8.9 %collective-permute-done.53 = bf16[2,4,32,1024]{3,2,1,0:T(8,128)(2,1)S(1)} collective-permute-done((bf16[2,4,32,1024]{3,2,1,0:T(8,128)(2,1)S(1)}, bf16[2,4,32,1024]{3,2,1,0:T(8,128)(2,1)S(1)}, u32[]{:S(2)}, u32[]{:S(2)}) %collective-permute-start.53) | collective-permute-done | bytes 524320 | tf_op jit(solution)/shard_map/ppermute | solution.py:665
  337.0 21.1 %attention_backward.1 = (bf16[1280,512]{1,0:T(8,128)(2,1)S(1)}, bf16[1280,512]{1,0:T(8,128)(2,1)S(1)}) custom-call(s32[20]{0:T(128)S(1)} %pad_add_fusion.1.info_ref, bf16[1280,512]{1,0:T(8,128)(2,1)S(1)} %copy-done.3, bf16[1280,512]{1,0:T(8,128)(2,1)S(1)} %copy-done.5, bf16[1280,512]{1,0:T(8,128)(2,1)S(1)} %get-tuple-element.54.out_ref, ...), custom_call_target="tpu_custom_call" | custom-call | tf_op jit(solution)/shard_map/attention_backward/pallas_call | solution.py:1016
  360.3 15.4 %project_back.1 = (bf16[1280,1024]{1,0:T(8,128)(2,1)}, bf16[2,4,64,512]{3,2,1,0:T(8,128)(2,1)S(1)}, bf16[2,4,64,512]{3,2,1,0:T(8,128)(2,1)S(1)}, bf16[2,4,64,512...) custom-call(s32[4]{0:T(128)S(1)} %copy-done.15, bf16[1280,1024]{1,0:T(8,128)(2,1)} %bitcast.293, ...), custom_call_target="tpu_custom_call" | custom-call | tf_op jit(solution)/shard_map/project_back/pallas_call | solution.py:340
  379.7 8.6 %collective-permute-done.42 = bf16[2,4,64,512]{3,2,1,0:T(8,128)(2,1)S(1)} collective-permute-done((bf16[2,4,64,512]{3,2,1,0:T(8,128)(2,1)S(1)}, bf16[2,4,64,512]{3,2,1,0:T(8,128)(2,1)S(1)}, u32[]{:S(2)}, u32[]{:S(2)}) %collective-permute-start.42) | collective-permute-done | bytes 524320 | tf_op jit(solution)/shard_map/ppermute | solution.py:662
  392.9 4.0 add_convert_fusion
  396.9 3.0 collective-permute-done.43
  401.3 6.3 %collective-permute-done.38 = bf16[4,64,512]{2,1,0:T(8,128)(2,1)S(1)} collective-permute-done((bf16[4,64,512]{2,1,0:T(8,128)(2,1)S(1)}, bf16[4,64,512]{2,1,0:T(8,128)(2,1)S(1)}, u32[]{:S(2)}, u32[]{:S(2)}) %collective-permute-start.38) | collective-permute-done | bytes 262176 | tf_op jit(solution)/shard_map/ppermute | solution.py:662
  407.7 6.0 %collective-permute-done.44 = bf16[64,512]{1,0:T(8,128)(2,1)S(1)} collective-permute-done((bf16[64,512]{1,0:T(8,128)(2,1)S(1)}, bf16[64,512]{1,0:T(8,128)(2,1)S(1)}, u32[]{:S(2)}, u32[]{:S(2)}) %collective-permute-start.44) | collective-permute-done | bytes 65568 | tf_op jit(solution)/shard_map/ppermute | solution.py:668
  413.7 6.0 %collective-permute-done.39 = bf16[64,512]{1,0:T(8,128)(2,1)S(1)} collective-permute-done((bf16[64,512]{1,0:T(8,128)(2,1)S(1)}, bf16[64,512]{1,0:T(8,128)(2,1)S(1)}, u32[]{:S(2)}, u32[]{:S(2)}) %collective-permute-start.39) | collective-permute-done | bytes 65568 | tf_op jit(solution)/shard_map/ppermute | solution.py:668
  419.8 6.5 %collective-permute-done.45 = bf16[64,512]{1,0:T(8,128)(2,1)S(1)} collective-permute-done((bf16[64,512]{1,0:T(8,128)(2,1)S(1)}, bf16[64,512]{1,0:T(8,128)(2,1)S(1)}, u32[]{:S(2)}, u32[]{:S(2)}) %collective-permute-start.45) | collective-permute-done | bytes 65568 | tf_op jit(solution)/shard_map/ppermute | solution.py:668
  426.3 6.6 %collective-permute-done.40 = bf16[64,512]{1,0:T(8,128)(2,1)S(1)} collective-permute-done((bf16[64,512]{1,0:T(8,128)(2,1)S(1)}, bf16[64,512]{1,0:T(8,128)(2,1)S(1)}, u32[]{:S(2)}, u32[]{:S(2)}) %collective-permute-start.40) | collective-permute-done | bytes 65568 | tf_op jit(solution)/shard_map/ppermute | solution.py:668
  433.9 5.0 collective-permute-done.46
  442.5 7.1 %collective-permute-done.36 = bf16[320,1024]{1,0:T(8,128)(2,1)S(1)} collective-permute-done((bf16[320,1024]{1,0:T(8,128)(2,1)S(1)}, bf16[320,1024]{1,0:T(8,128)(2,1)S(1)}, u32[]{:S(2)}, u32[]{:S(2)}) %collective-permute-start.36) | collective-permute-done | bytes 655392 | tf_op jit(solution)/shard_map/ppermute | solution.py:568
  451.6 1.9 fusion.4
  459.5 10.5 %collective-permute-done.67 = f32[16,288]{1,0:T(8,128)S(1)} collective-permute-done((f32[16,288]{1,0:T(8,128)S(1)}, f32[16,288]{1,0:T(8,128)S(1)}, u32[]{:S(2)}, u32[]{:S(2)}) %collective-permute-start.67) | collective-permute-done | bytes 18464 | tf_op jit(solution)/shard_map/ppermute | solution.py:673
  472.5 2.5 add_convert_fusion.2
  475.0 1.9 collective-permute-start.63
  477.6 40.3 %collective-permute-done.69 = f32[4,288]{1,0:T(4,128)S(1)} collective-permute-done((f32[4,288]{1,0:T(4,128)S(1)}, f32[4,288]{1,0:T(4,128)S(1)}, u32[]{:S(2)}, u32[]{:S(2)}) %collective-permute-start.69) | collective-permute-done | bytes 4640 | tf_op jit(solution)/shard_map/ppermute | solution.py:673
  518.7 2.9 collective-permute-done.70
  521.7 4.8 multiply_add_fusion
  527.1 3.0 convert_add_fusion
  534.8 26.8 %collective-permute-done.54 = bf16[4,160,1024]{2,1,0:T(8,128)(2,1)S(1)} collective-permute-done((bf16[4,160,1024]{2,1,0:T(8,128)(2,1)S(1)}, bf16[4,160,1024]{2,1,0:T(8,128)(2,1)S(1)}, u32[]{:S(2)}, u32[]{:S(2)}) %collective-permute-start.54) | collective-permute-done | bytes 1310752 | tf_op jit(solution)/shard_map/ppermute | solution.py:662
  562.3 11.0 %collective-permute-done.55 = bf16[160,1024]{1,0:T(8,128)(2,1)S(1)} collective-permute-done((bf16[160,1024]{1,0:T(8,128)(2,1)S(1)}, bf16[160,1024]{1,0:T(8,128)(2,1)S(1)}, u32[]{:S(2)}, u32[]{:S(2)}) %collective-permute-start.55) | collective-permute-done | bytes 327712 | tf_op jit(solution)/shard_map/ppermute | solution.py:668
  574.7 8.9 %collective-permute-done.56 = bf16[160,1024]{1,0:T(8,128)(2,1)S(1)} collective-permute-done((bf16[160,1024]{1,0:T(8,128)(2,1)S(1)}, bf16[160,1024]{1,0:T(8,128)(2,1)S(1)}, u32[]{:S(2)}, u32[]{:S(2)}) %collective-permute-start.56) | collective-permute-done | bytes 327712 | tf_op jit(solution)/shard_map/ppermute | solution.py:668
  584.6 8.4 %collective-permute-done.57 = bf16[160,1024]{1,0:T(8,128)(2,1)S(1)} collective-permute-done((bf16[160,1024]{1,0:T(8,128)(2,1)S(1)}, bf16[160,1024]{1,0:T(8,128)(2,1)S(1)}, u32[]{:S(2)}, u32[]{:S(2)}) %collective-permute-start.57) | collective-permute-done | bytes 327712 | tf_op jit(solution)/shard_map/ppermute | solution.py:668
  (339 shorter events, 105.9 us)
Async XLA Ops:
  4.7 17.8 %collective-permute-start = (bf16[1,288]{1,0:T(2,128)(2,1)S(1)}, bf16[1,288]{1,0:T(2,128)(2,1)}, u32[]{:S(2)}, u32[]{:S(2)}) collective-permute-start(bf16[1,288]{1,0:T(2,128)(2,1)S(1)} %broadcast_in_dim.4), channel_id=1, source_target_pairs={{0,1},{1,0},{2,3},{3,2},{4,5},{5,4},{6,7},{7,6},{8,9},{9,8},{10,11... | collective-permute-start | bytes 1736 | tf_op jit(solution)/shard_map/ppermute | solution.py:672
  6.8 48.8 %collective-permute-start.7 = (bf16[2,32,512]{2,1,0:T(8,128)(2,1)}, bf16[2,32,512]{2,1,0:T(8,128)(2,1)}, u32[]{:S(2)}, u32[]{:S(2)}) collective-permute-start(bf16[2,32,512]{2,1,0:T(8,128)(2,1)} %get-tuple-element.177), channel_id=1, source_target_pairs={{0,1},{1,0},{2,3},{3,2},{4,5},{5,4},{6,7},{7,6},{8,9},{9,8},{10,11... | collective-permute-start | bytes 196616 | tf_op jit(solution)/shard_map/ppermute | solution.py:659
  10.0 32.3 %collective-permute-start.17 = (bf16[160,1024]{1,0:T(8,128)(2,1)}, bf16[160,1024]{1,0:T(8,128)(2,1)}, u32[]{:S(2)}, u32[]{:S(2)}) collective-permute-start(bf16[160,1024]{1,0:T(8,128)(2,1)} %constant_dynamic-update-slice_fusion), channel_id=1, source_target_pairs={{0,8},{4,12},{8,16},{12,20},{16,24},{20,28},{24,0},{28,4},{1,9},{5... | collective-permute-start | bytes 983048 | tf_op jit(solution)/shard_map/ppermute | solution.py:668
  13.0 53.2 %collective-permute-start.24 = (bf16[32,4096]{1,0:T(8,128)(2,1)}, bf16[32,4096]{1,0:T(8,128)(2,1)S(1)}, u32[]{:S(2)}, u32[]{:S(2)}) collective-permute-start(bf16[32,4096]{1,0:T(8,128)(2,1)} %param.25), channel_id=1, source_target_pairs={{0,2},{1,3},{2,0},{3,1},{4,6},{5,7},{6,4},{7,5},{8,10},{9,11},{10,... | collective-permute-start | bytes 786440 | tf_op jit(solution)/shard_map/ppermute | solution.py:662
  42.3 12.6 %collective-permute-start.18 = (bf16[160,1024]{1,0:T(8,128)(2,1)}, bf16[160,1024]{1,0:T(8,128)(2,1)S(1)}, u32[]{:S(2)}, u32[]{:S(2)}) collective-permute-start(bf16[160,1024]{1,0:T(8,128)(2,1)} %collective-permute-done.17), channel_id=1, source_target_pairs={{0,8},{4,12},{8,16},{12,20},{16,24},{20,28},{24,0},{28,4},{1,9},{5... | collective-permute-start | bytes 983048 | tf_op jit(solution)/shard_map/ppermute | solution.py:668
  54.9 18.0 %collective-permute-start.5 = (bf16[320,1024]{1,0:T(8,128)(2,1)S(1)}, bf16[320,1024]{1,0:T(8,128)(2,1)S(1)}, u32[]{:S(2)}, u32[]{:S(2)}) collective-permute-start(bf16[320,1024]{1,0:T(8,128)(2,1)S(1)} %select_bitcast_fusion.10), channel_id=1, source_target_pairs={{0,2},{1,3},{2,0},{3,1},{4,6},{5,7},{6,4},{7,5},{8,10},{9,11},{10,... | collective-permute-start | bytes 1966088 | tf_op jit(solution)/shard_map/ppermute | solution.py:568
  65.5 25.7 %collective-permute-start.20 = (bf16[4,160,1024]{2,1,0:T(8,128)(2,1)S(1)}, bf16[4,160,1024]{2,1,0:T(8,128)(2,1)S(1)}, u32[]{:S(2)}, u32[]{:S(2)}) collective-permute-start(bf16[4,160,1024]{2,1,0:T(8,128)(2,1)S(1)} %get-tuple-element.160), channel_id=1, source_target_pairs={{0,2},{1,3},{2,0},{3,1},{4,6},{5,7},{6,4},{7,5},{8,10},{9,11},{10,... | collective-permute-start | bytes 3932168 | tf_op jit(solution)/shard_map/ppermute | solution.py:662
  66.3 29.3 %collective-permute-start.25 = (bf16[2,32,4096]{2,1,0:T(8,128)(2,1)S(1)}, bf16[2,32,4096]{2,1,0:T(8,128)(2,1)S(1)}, u32[]{:S(2)}, u32[]{:S(2)}) collective-permute-start(bf16[2,32,4096]{2,1,0:T(8,128)(2,1)S(1)} %get-tuple-element.162), channel_id=1, source_target_pairs={{0,4},{4,0},{8,12},{12,8},{16,20},{20,16},{24,28},{28,24},{1,5},{5... | collective-permute-start | bytes 1572872 | tf_op jit(solution)/shard_map/ppermute | solution.py:665
  72.9 23.7 %collective-permute-start.10 = (bf16[2,64,512]{2,1,0:T(8,128)(2,1)S(1)}, bf16[2,64,512]{2,1,0:T(8,128)(2,1)S(1)}, u32[]{:S(2)}, u32[]{:S(2)}) collective-permute-start(bf16[2,64,512]{2,1,0:T(8,128)(2,1)S(1)} %collective-permute-done.9), channel_id=1, source_target_pairs={{0,8},{4,12},{8,16},{12,20},{16,24},{20,28},{24,0},{28,4},{1,9},{5... | collective-permute-start | bytes 393224 | tf_op jit(solution)/shard_map/ppermute | solution.py:668
  92.9 100.1 %collective-permute-start.21 = (bf16[2,4,160,1024]{3,2,1,0:T(8,128)(2,1)}, bf16[2,4,160,1024]{3,2,1,0:T(8,128)(2,1)}, u32[]{:S(2)}, u32[]{:S(2)}) collective-permute-start(bf16[2,4,160,1024]{3,2,1,0:T(8,128)(2,1)} %pad_maximum_fusion.1.refs_0_.refs_8_), channel_id=1, source_target_pairs={{0,4},{4,0},{8,12},{12,8},{16,20},{20,16},{24,28},{28,24},{1,5},{5... | collective-permute-start | bytes 7864328 | tf_op jit(solution)/shard_map/ppermute | solution.py:665
  95.5 59.8 %collective-permute-start.6 = (bf16[2,320,1024]{2,1,0:T(8,128)(2,1)}, bf16[2,320,1024]{2,1,0:T(8,128)(2,1)}, u32[]{:S(2)}, u32[]{:S(2)}) collective-permute-start(bf16[2,320,1024]{2,1,0:T(8,128)(2,1)} %pad_maximum_fusion.2), channel_id=1, source_target_pairs={{0,1},{1,0},{2,3},{3,2},{4,5},{5,4},{6,7},{7,6},{8,9},{9,8},{10,11... | collective-permute-start | bytes 3932168 | tf_op jit(solution)/shard_map/ppermute | solution.py:565
  96.6 57.8 %collective-permute-start.26 = (bf16[2,2,32,4096]{3,2,1,0:T(8,128)(2,1)}, bf16[2,2,32,4096]{3,2,1,0:T(8,128)(2,1)}, u32[]{:S(2)}, u32[]{:S(2)}) collective-permute-start(bf16[2,2,32,4096]{3,2,1,0:T(8,128)(2,1)} %pad_maximum_fusion.8.refs_0_), channel_id=1, source_target_pairs={{0,8},{4,12},{8,16},{12,20},{16,24},{20,28},{24,0},{28,4},{1,9},{5... | collective-permute-start | bytes 3145736 | tf_op jit(solution)/shard_map/ppermute | solution.py:668
  97.3 56.3 %collective-permute-start.13 = (bf16[4,64,512]{2,1,0:T(8,128)(2,1)S(1)}, bf16[4,64,512]{2,1,0:T(8,128)(2,1)S(1)}, u32[]{:S(2)}, u32[]{:S(2)}) collective-permute-start(bf16[4,64,512]{2,1,0:T(8,128)(2,1)S(1)} %get-tuple-element.166), channel_id=1, source_target_pairs={{0,4},{4,0},{8,12},{12,8},{16,20},{20,16},{24,28},{28,24},{1,5},{5... | collective-permute-start | bytes 786440 | tf_op jit(solution)/shard_map/ppermute | solution.py:665
  105.5 53.8 %collective-permute-start.12 = (bf16[2,4,64,512]{3,2,1,0:T(8,128)(2,1)S(1)}, bf16[2,4,64,512]{3,2,1,0:T(8,128)(2,1)}, u32[]{:S(2)}, u32[]{:S(2)}) collective-permute-start(bf16[2,4,64,512]{3,2,1,0:T(8,128)(2,1)S(1)} %pad_maximum_fusion.11.refs_0_), channel_id=1, source_target_pairs={{0,4},{4,0},{8,12},{12,8},{16,20},{20,16},{24,28},{28,24},{1,5},{5... | collective-permute-start | bytes 1572872 | tf_op jit(solution)/shard_map/ppermute | solution.py:665
  153.6 67.2 %collective-permute-start.22 = (bf16[2,4,160,1024]{3,2,1,0:T(8,128)(2,1)}, bf16[2,4,160,1024]{3,2,1,0:T(8,128)(2,1)}, u32[]{:S(2)}, u32[]{:S(2)}) collective-permute-start(bf16[2,4,160,1024]{3,2,1,0:T(8,128)(2,1)} %pad_maximum_fusion.1.refs_0_.refs_8_), channel_id=1, source_target_pairs={{0,1},{1,0},{2,3},{3,2},{4,5},{5,4},{6,7},{7,6},{8,9},{9,8},{10,11... | collective-permute-start | bytes 7864328 | tf_op jit(solution)/shard_map/ppermute | solution.py:659
  154.4 14.7 %collective-permute-start.14 = (bf16[2,4,64,512]{3,2,1,0:T(8,128)(2,1)}, bf16[2,4,64,512]{3,2,1,0:T(8,128)(2,1)}, u32[]{:S(2)}, u32[]{:S(2)}) collective-permute-start(bf16[2,4,64,512]{3,2,1,0:T(8,128)(2,1)} %pad_maximum_fusion.12.refs_2_), channel_id=1, source_target_pairs={{0,2},{1,3},{2,0},{3,1},{4,6},{5,7},{6,4},{7,5},{8,10},{9,11},{10,... | collective-permute-start | bytes 1572872 | tf_op jit(solution)/shard_map/ppermute | solution.py:662
  155.3 38.2 %collective-permute-start.27 = (bf16[2,2,32,4096]{3,2,1,0:T(8,128)(2,1)}, bf16[2,2,32,4096]{3,2,1,0:T(8,128)(2,1)}, u32[]{:S(2)}, u32[]{:S(2)}) collective-permute-start(bf16[2,2,32,4096]{3,2,1,0:T(8,128)(2,1)} %collective-permute-done.26.refs_1_), channel_id=1, source_target_pairs={{0,8},{4,12},{8,16},{12,20},{16,24},{20,28},{24,0},{28,4},{1,9},{5... | collective-permute-start | bytes 3145736 | tf_op jit(solution)/shard_map/ppermute | solution.py:668
  193.0 32.0 %collective-permute-start.23 = (bf16[2,4,160,1024]{3,2,1,0:T(8,128)(2,1)}, bf16[2,4,160,1024]{3,2,1,0:T(8,128)(2,1)}, u32[]{:S(2)}, u32[]{:S(2)}) collective-permute-start(bf16[2,4,160,1024]{3,2,1,0:T(8,128)(2,1)} %collective-permute-done.21.refs_1_.refs_9_), channel_id=1, source_target_pairs={{0,1},{1,0},{2,3},{3,2},{4,5},{5,4},{6,7},{7,6},{8,9},{9,8},{10,11... | collective-permute-start | bytes 7864328 | tf_op jit(solution)/shard_map/ppermute | solution.py:659
  193.5 27.3 %collective-permute-start.28 = (bf16[2,2,32,4096]{3,2,1,0:T(8,128)(2,1)}, bf16[2,2,32,4096]{3,2,1,0:T(8,128)(2,1)}, u32[]{:S(2)}, u32[]{:S(2)}) collective-permute-start(bf16[2,2,32,4096]{3,2,1,0:T(8,128)(2,1)} %collective-permute-done.27.refs_2_), channel_id=1, source_target_pairs={{0,8},{4,12},{8,16},{12,20},{16,24},{20,28},{24,0},{28,4},{1,9},{5... | collective-permute-start | bytes 3145736 | tf_op jit(solution)/shard_map/ppermute | solution.py:668
  195.5 16.8 %collective-permute-start.16 = (bf16[320,1024]{1,0:T(8,128)(2,1)S(1)}, bf16[320,1024]{1,0:T(8,128)(2,1)S(1)}, u32[]{:S(2)}, u32[]{:S(2)}) collective-permute-start(bf16[320,1024]{1,0:T(8,128)(2,1)S(1)} %select_bitcast_fusion.8), channel_id=1, source_target_pairs={{0,2},{1,3},{2,0},{3,1},{4,6},{5,7},{6,4},{7,5},{8,10},{9,11},{10,... | collective-permute-start | bytes 1966088 | tf_op jit(solution)/shard_map/ppermute | solution.py:568
  196.1 37.4 %collective-permute-start.29 = (bf16[2,2,32,4096]{3,2,1,0:T(8,128)(2,1)}, bf16[2,2,32,4096]{3,2,1,0:T(8,128)(2,1)}, u32[]{:S(2)}, u32[]{:S(2)}) collective-permute-start(bf16[2,2,32,4096]{3,2,1,0:T(8,128)(2,1)} %pad_maximum_fusion.8.refs_0_), channel_id=1, source_target_pairs={{0,1},{1,0},{2,3},{3,2},{4,5},{5,4},{6,7},{7,6},{8,9},{9,8},{10,11... | collective-permute-start | bytes 3145736 | tf_op jit(solution)/shard_map/ppermute | solution.py:659
  213.2 20.3 %collective-permute-start.30 = (bf16[2,2,32,4096]{3,2,1,0:T(8,128)(2,1)}, bf16[2,2,32,4096]{3,2,1,0:T(8,128)(2,1)}, u32[]{:S(2)}, u32[]{:S(2)}) collective-permute-start(bf16[2,2,32,4096]{3,2,1,0:T(8,128)(2,1)} %collective-permute-done.26.refs_1_), channel_id=1, source_target_pairs={{0,1},{1,0},{2,3},{3,2},{4,5},{5,4},{6,7},{7,6},{8,9},{9,8},{10,11... | collective-permute-start | bytes 3145736 | tf_op jit(solution)/shard_map/ppermute | solution.py:659
  220.8 12.7 %collective-permute-start.31 = (bf16[2,2,32,4096]{3,2,1,0:T(8,128)(2,1)}, bf16[2,2,32,4096]{3,2,1,0:T(8,128)(2,1)}, u32[]{:S(2)}, u32[]{:S(2)}) collective-permute-start(bf16[2,2,32,4096]{3,2,1,0:T(8,128)(2,1)} %collective-permute-done.27.refs_2_), channel_id=1, source_target_pairs={{0,1},{1,0},{2,3},{3,2},{4,5},{5,4},{6,7},{7,6},{8,9},{9,8},{10,11... | collective-permute-start | bytes 3145736 | tf_op jit(solution)/shard_map/ppermute | solution.py:659
  220.8 12.7 %collective-permute-start.32 = (bf16[2,2,32,4096]{3,2,1,0:T(8,128)(2,1)}, bf16[2,2,32,4096]{3,2,1,0:T(8,128)(2,1)}, u32[]{:S(2)}, u32[]{:S(2)}) collective-permute-start(bf16[2,2,32,4096]{3,2,1,0:T(8,128)(2,1)} %collective-permute-done.28.refs_3_), channel_id=1, source_target_pairs={{0,1},{1,0},{2,3},{3,2},{4,5},{5,4},{6,7},{7,6},{8,9},{9,8},{10,11... | collective-permute-start | bytes 3145736 | tf_op jit(solution)/shard_map/ppermute | solution.py:659
  301.2 17.4 %collective-permute-start.33 = (bf16[320,1024]{1,0:T(8,128)(2,1)}, bf16[320,1024]{1,0:T(8,128)(2,1)}, u32[]{:S(2)}, u32[]{:S(2)}) collective-permute-start(bf16[320,1024]{1,0:T(8,128)(2,1)} %broadcast_select_fusion.7), channel_id=1, source_target_pairs={{0,2},{1,3},{2,0},{3,1},{4,6},{5,7},{6,4},{7,5},{8,10},{9,11},{10,... | collective-permute-start | bytes 1966088 | tf_op jit(solution)/shard_map/ppermute | solution.py:568
  301.7 19.7 %collective-permute-start.58 = (bf16[2,2,32,4096]{3,2,1,0:T(8,128)(2,1)}, bf16[2,2,32,4096]{3,2,1,0:T(8,128)(2,1)}, u32[]{:S(2)}, u32[]{:S(2)}) collective-permute-start(bf16[2,2,32,4096]{3,2,1,0:T(8,128)(2,1)} %get-tuple-element.79), channel_id=1, source_target_pairs={{0,1},{1,0},{2,3},{3,2},{4,5},{5,4},{6,7},{7,6},{8,9},{9,8},{10,11... | collective-permute-start | bytes 3145736 | tf_op jit(solution)/shard_map/ppermute | solution.py:659
  303.2 19.8 %collective-permute-start.51 = (bf16[2,4,32,1024]{3,2,1,0:T(8,128)(2,1)}, bf16[2,4,32,1024]{3,2,1,0:T(8,128)(2,1)}, u32[]{:S(2)}, u32[]{:S(2)}) collective-permute-start(bf16[2,4,32,1024]{3,2,1,0:T(8,128)(2,1)} %get-tuple-element.75), channel_id=1, source_target_pairs={{0,1},{1,0},{2,3},{3,2},{4,5},{5,4},{6,7},{7,6},{8,9},{9,8},{10,11... | collective-permute-start | bytes 1572872 | tf_op jit(solution)/shard_map/ppermute | solution.py:659
  303.6 87.8 %collective-permute-start.49 = (bf16[2,4,128,1024]{3,2,1,0:T(8,128)(2,1)}, bf16[2,4,128,1024]{3,2,1,0:T(8,128)(2,1)}, u32[]{:S(2)}, u32[]{:S(2)}) collective-permute-start(bf16[2,4,128,1024]{3,2,1,0:T(8,128)(2,1)} %get-tuple-element.73), channel_id=1, source_target_pairs={{0,1},{1,0},{2,3},{3,2},{4,5},{5,4},{6,7},{7,6},{8,9},{9,8},{10,11... | collective-permute-start | bytes 6291464 | tf_op jit(solution)/shard_map/ppermute | solution.py:659
  308.3 81.0 %collective-permute-start.60 = (bf16[2,2,32,4096]{3,2,1,0:T(8,128)(2,1)}, bf16[2,2,32,4096]{3,2,1,0:T(8,128)(2,1)S(1)}, u32[]{:S(2)}, u32[]{:S(2)}) collective-permute-start(bf16[2,2,32,4096]{3,2,1,0:T(8,128)(2,1)} %get-tuple-element.81), channel_id=1, source_target_pairs={{0,1},{1,0},{2,3},{3,2},{4,5},{5,4},{6,7},{7,6},{8,9},{9,8},{10,11... | collective-permute-start | bytes 3145736 | tf_op jit(solution)/shard_map/ppermute | solution.py:659
  318.6 13.5 %collective-permute-start.53 = (bf16[2,4,32,1024]{3,2,1,0:T(8,128)(2,1)S(1)}, bf16[2,4,32,1024]{3,2,1,0:T(8,128)(2,1)S(1)}, u32[]{:S(2)}, u32[]{:S(2)}) collective-permute-start(bf16[2,4,32,1024]{3,2,1,0:T(8,128)(2,1)S(1)} %add_convert_fusion.5), channel_id=1, source_target_pairs={{0,4},{4,0},{8,12},{12,8},{16,20},{20,16},{24,28},{28,24},{1,5},{5... | collective-permute-start | bytes 1572872 | tf_op jit(solution)/shard_map/ppermute | solution.py:665
  321.5 12.8 %collective-permute-start.34 = (bf16[2,320,512]{2,1,0:T(8,128)(2,1)S(1)}, bf16[2,320,512]{2,1,0:T(8,128)(2,1)S(1)}, u32[]{:S(2)}, u32[]{:S(2)}) collective-permute-start(bf16[2,320,512]{2,1,0:T(8,128)(2,1)S(1)} %broadcast_select_fusion.2), channel_id=1, source_target_pairs={{0,1},{1,0},{2,3},{3,2},{4,5},{5,4},{6,7},{7,6},{8,9},{9,8},{10,11... | collective-permute-start | bytes 1966088 | tf_op jit(solution)/shard_map/ppermute | solution.py:565
  323.1 66.4 %collective-permute-start.59 = (bf16[2,2,32,4096]{3,2,1,0:T(8,128)(2,1)S(1)}, bf16[2,2,32,4096]{3,2,1,0:T(8,128)(2,1)S(1)}, u32[]{:S(2)}, u32[]{:S(2)}) collective-permute-start(bf16[2,2,32,4096]{3,2,1,0:T(8,128)(2,1)S(1)} %add_convert_fusion.4), channel_id=1, source_target_pairs={{0,8},{4,12},{8,16},{12,20},{16,24},{20,28},{24,0},{28,4},{1,9},{5... | collective-permute-start | bytes 3145736 | tf_op jit(solution)/shard_map/ppermute | solution.py:668
  375.7 12.6 %collective-permute-start.42 = (bf16[2,4,64,512]{3,2,1,0:T(8,128)(2,1)S(1)}, bf16[2,4,64,512]{3,2,1,0:T(8,128)(2,1)S(1)}, u32[]{:S(2)}, u32[]{:S(2)}) collective-permute-start(bf16[2,4,64,512]{3,2,1,0:T(8,128)(2,1)S(1)} %get-tuple-element.69), channel_id=1, source_target_pairs={{0,2},{1,3},{2,0},{3,1},{4,6},{5,7},{6,4},{7,5},{8,10},{9,11},{10,... | collective-permute-start | bytes 1572872 | tf_op jit(solution)/shard_map/ppermute | solution.py:662
  376.3 12.3 %collective-permute-start.37 = (bf16[2,4,64,512]{3,2,1,0:T(8,128)(2,1)S(1)}, bf16[2,4,64,512]{3,2,1,0:T(8,128)(2,1)S(1)}, u32[]{:S(2)}, u32[]{:S(2)}) collective-permute-start(bf16[2,4,64,512]{3,2,1,0:T(8,128)(2,1)S(1)} %get-tuple-element.67), channel_id=1, source_target_pairs={{0,4},{4,0},{8,12},{12,8},{16,20},{20,16},{24,28},{28,24},{1,5},{5... | collective-permute-start | bytes 1572872 | tf_op jit(solution)/shard_map/ppermute | solution.py:665
  388.4 138.7 %collective-permute-start.48 = (bf16[2,4,128,1024]{3,2,1,0:T(8,128)(2,1)}, bf16[2,4,128,1024]{3,2,1,0:T(8,128)(2,1)}, u32[]{:S(2)}, u32[]{:S(2)}) collective-permute-start(bf16[2,4,128,1024]{3,2,1,0:T(8,128)(2,1)} %get-tuple-element.71), channel_id=1, source_target_pairs={{0,1},{1,0},{2,3},{3,2},{4,5},{5,4},{6,7},{7,6},{8,9},{9,8},{10,11... | collective-permute-start | bytes 6291464 | tf_op jit(solution)/shard_map/ppermute | solution.py:659
  388.7 142.4 %collective-permute-start.64 = (bf16[2,2,32,4096]{3,2,1,0:T(8,128)(2,1)}, bf16[2,2,32,4096]{3,2,1,0:T(8,128)(2,1)}, u32[]{:S(2)}, u32[]{:S(2)}) collective-permute-start(bf16[2,2,32,4096]{3,2,1,0:T(8,128)(2,1)} %get-tuple-element.85), channel_id=1, source_target_pairs={{0,1},{1,0},{2,3},{3,2},{4,5},{5,4},{6,7},{7,6},{8,9},{9,8},{10,11... | collective-permute-start | bytes 3145736 | tf_op jit(solution)/shard_map/ppermute | solution.py:659
  389.3 82.9 %collective-permute-start.62 = (bf16[2,2,32,4096]{3,2,1,0:T(8,128)(2,1)}, bf16[2,2,32,4096]{3,2,1,0:T(8,128)(2,1)}, u32[]{:S(2)}, u32[]{:S(2)}) collective-permute-start(bf16[2,2,32,4096]{3,2,1,0:T(8,128)(2,1)} %get-tuple-element.83), channel_id=1, source_target_pairs={{0,1},{1,0},{2,3},{3,2},{4,5},{5,4},{6,7},{7,6},{8,9},{9,8},{10,11... | collective-permute-start | bytes 3145736 | tf_op jit(solution)/shard_map/ppermute | solution.py:659
  389.5 43.4 %collective-permute-start.35 = (bf16[2,320,1024]{2,1,0:T(8,128)(2,1)S(1)}, bf16[2,320,1024]{2,1,0:T(8,128)(2,1)S(1)}, u32[]{:S(2)}, u32[]{:S(2)}) collective-permute-start(bf16[2,320,1024]{2,1,0:T(8,128)(2,1)S(1)} %select_bitcast_fusion), channel_id=1, source_target_pairs={{0,1},{1,0},{2,3},{3,2},{4,5},{5,4},{6,7},{7,6},{8,9},{9,8},{10,11... | collective-permute-start | bytes 3932168 | tf_op jit(solution)/shard_map/ppermute | solution.py:565
  439.0 10.6 %collective-permute-start.36 = (bf16[320,1024]{1,0:T(8,128)(2,1)S(1)}, bf16[320,1024]{1,0:T(8,128)(2,1)S(1)}, u32[]{:S(2)}, u32[]{:S(2)}) collective-permute-start(bf16[320,1024]{1,0:T(8,128)(2,1)S(1)} %select_bitcast_fusion.3), channel_id=1, source_target_pairs={{0,2},{1,3},{2,0},{3,1},{4,6},{5,7},{6,4},{7,5},{8,10},{9,11},{10,... | collective-permute-start | bytes 1966088 | tf_op jit(solution)/shard_map/ppermute | solution.py:568
  441.7 30.7 %collective-permute-start.61 = (bf16[2,2,32,4096]{3,2,1,0:T(8,128)(2,1)}, bf16[2,2,32,4096]{3,2,1,0:T(8,128)(2,1)}, u32[]{:S(2)}, u32[]{:S(2)}) collective-permute-start(bf16[2,2,32,4096]{3,2,1,0:T(8,128)(2,1)} %add_convert_fusion.3), channel_id=1, source_target_pairs={{0,8},{4,12},{8,16},{12,20},{16,24},{20,28},{24,0},{28,4},{1,9},{5... | collective-permute-start | bytes 3145736 | tf_op jit(solution)/shard_map/ppermute | solution.py:668
  457.9 12.2 %collective-permute-start.67 = (f32[16,288]{1,0:T(8,128)S(1)}, f32[16,288]{1,0:T(8,128)S(1)}, u32[]{:S(2)}, u32[]{:S(2)}) collective-permute-start(f32[16,288]{1,0:T(8,128)S(1)} %slice_select_fusion), channel_id=1, source_target_pairs={{0,16},{4,20},{8,24},{12,28},{16,0},{20,4},{24,8},{28,12},{1,17},{... | collective-permute-start | bytes 55304 | tf_op jit(solution)/shard_map/ppermute | solution.py:673
  470.0 57.1 %collective-permute-start.50 = (bf16[2,4,128,1024]{3,2,1,0:T(8,128)(2,1)}, bf16[2,4,128,1024]{3,2,1,0:T(8,128)(2,1)S(1)}, u32[]{:S(2)}, u32[]{:S(2)}) collective-permute-start(bf16[2,4,128,1024]{3,2,1,0:T(8,128)(2,1)} %add_convert_fusion), channel_id=1, source_target_pairs={{0,4},{4,0},{8,12},{12,8},{16,20},{20,16},{24,28},{28,24},{1,5},{5... | collective-permute-start | bytes 6291464 | tf_op jit(solution)/shard_map/ppermute | solution.py:665
  475.0 56.1 %collective-permute-start.63 = (bf16[2,2,32,4096]{3,2,1,0:T(8,128)(2,1)S(1)}, bf16[2,2,32,4096]{3,2,1,0:T(8,128)(2,1)S(1)}, u32[]{:S(2)}, u32[]{:S(2)}) collective-permute-start(bf16[2,2,32,4096]{3,2,1,0:T(8,128)(2,1)S(1)} %add_convert_fusion.2), channel_id=1, source_target_pairs={{0,8},{4,12},{8,16},{12,20},{16,24},{20,28},{24,0},{28,4},{1,9},{5... | collective-permute-start | bytes 3145736 | tf_op jit(solution)/shard_map/ppermute | solution.py:668
  477.0 40.9 %collective-permute-start.69 = (f32[4,288]{1,0:T(4,128)S(1)}, f32[4,288]{1,0:T(4,128)S(1)}, u32[]{:S(2)}, u32[]{:S(2)}) collective-permute-start(f32[4,288]{1,0:T(4,128)S(1)} %slice_select_fusion.2), channel_id=1, source_target_pairs={{0,4},{4,0},{8,12},{12,8},{16,20},{20,16},{24,28},{28,24},{1,5},{5... | collective-permute-start | bytes 13832 | tf_op jit(solution)/shard_map/ppermute | solution.py:673
  530.4 31.2 %collective-permute-start.54 = (bf16[4,160,1024]{2,1,0:T(8,128)(2,1)S(1)}, bf16[4,160,1024]{2,1,0:T(8,128)(2,1)S(1)}, u32[]{:S(2)}, u32[]{:S(2)}) collective-permute-start(bf16[4,160,1024]{2,1,0:T(8,128)(2,1)S(1)} %pad_maximum_fusion.7), channel_id=1, source_target_pairs={{0,2},{1,3},{2,0},{3,1},{4,6},{5,7},{6,4},{7,5},{8,10},{9,11},{10,... | collective-permute-start | bytes 3932168 | tf_op jit(solution)/shard_map/ppermute | solution.py:662
  533.0 29.1 %collective-permute-start.65 = (bf16[2,32,4096]{2,1,0:T(8,128)(2,1)S(1)}, bf16[2,32,4096]{2,1,0:T(8,128)(2,1)S(1)}, u32[]{:S(2)}, u32[]{:S(2)}) collective-permute-start(bf16[2,32,4096]{2,1,0:T(8,128)(2,1)S(1)} %fusion.20), channel_id=1, source_target_pairs={{0,4},{4,0},{8,12},{12,8},{16,20},{20,16},{24,28},{28,24},{1,5},{5... | collective-permute-start | bytes 1572872 | tf_op jit(solution)/shard_map/ppermute | solution.py:665
  562.1 11.1 %collective-permute-start.55 = (bf16[160,1024]{1,0:T(8,128)(2,1)S(1)}, bf16[160,1024]{1,0:T(8,128)(2,1)S(1)}, u32[]{:S(2)}, u32[]{:S(2)}) collective-permute-start(bf16[160,1024]{1,0:T(8,128)(2,1)S(1)} %fusion.24), channel_id=1, source_target_pairs={{0,8},{4,12},{8,16},{12,20},{16,24},{20,28},{24,0},{28,4},{1,9},{5... | collective-permute-start | bytes 983048 | tf_op jit(solution)/shard_map/ppermute | solution.py:668
  573.4 10.3 %collective-permute-start.66 = (bf16[32,4096]{1,0:T(8,128)(2,1)S(1)}, bf16[32,4096]{1,0:T(8,128)(2,1)S(1)}, u32[]{:S(2)}, u32[]{:S(2)}) collective-permute-start(bf16[32,4096]{1,0:T(8,128)(2,1)S(1)} %fusion.28), channel_id=1, source_target_pairs={{0,2},{1,3},{2,0},{3,1},{4,6},{5,7},{6,4},{7,5},{8,10},{9,11},{10,... | collective-permute-start | bytes 786440 | tf_op jit(solution)/shard_map/ppermute | solution.py:662
  (68 other events, 830.5 us)

commit v3 on v2

--- a/solution.py
+++ b/solution.py
@@ -207,6 +207,7 @@
             jax.ShapeDtypeStruct((tree_len, (TRUNK + 2) * SEG), BF),
         ],
         compiler_params=pltpu.CompilerParams(vmem_limit_bytes=40 << 20),
+        cost_estimate=cost(18),
         name="attention_forward",
     )
     backward = pl.pallas_call(
@@ -222,6 +223,7 @@
         ),
         out_shape=[jax.ShapeDtypeStruct((tree_len, wide), BF)] * 2,
         compiler_params=pltpu.CompilerParams(vmem_limit_bytes=40 << 20),
+        cost_estimate=cost(21),
         name="attention_backward",
     )
     return forward, backward
@@ -233,23 +235,31 @@
 
 def piece_view(refs, piece):
     view = refs[piece[0]].at[piece[1]] if piece[1] else refs[piece[0]]
-    return view if piece[2] is None else view.at[pl.ds(piece[2], piece[3])]
+    if piece[2] is None:
+        return view
+    return view.at[pl.ds(piece[2][0], piece[3]), pl.ds(piece[2][1], piece[5][1])]
+
+
+def whole_view(whole, coords_ref, piece):
+    rows = row_block(piece[4], coords_ref, piece[3])
+    first = piece[5][0]
+    if callable(first):
+        first = pl.multiple_of(first(coords_ref) * piece[5][1], piece[5][1])
+    return whole.at[rows, pl.ds(first, piece[5][1])]
 
 
 def load_pieces(coords_ref, refs, pieces, target, sems, first):
-    copies = []
-    for number, piece in enumerate(pieces):
-        span = piece[3]
-        copies.append(pltpu.make_async_copy(piece_view(refs, piece), target.at[row_block(piece[4], coords_ref, span)], sems.at[first + number]))
-    return copies
+    return [
+        pltpu.make_async_copy(piece_view(refs, piece), whole_view(target, coords_ref, piece), sems.at[first + number])
+        for number, piece in enumerate(pieces)
+    ]
 
 
 def store_pieces(coords_ref, source, refs, pieces, sems, first):
-    copies = []
-    for number, piece in enumerate(pieces):
-        span = piece[3]
-        copies.append(pltpu.make_async_copy(source.at[row_block(piece[4], coords_ref, span)], piece_view(refs, piece), sems.at[first + number]))
-    return copies
+    return [
+        pltpu.make_async_copy(whole_view(source, coords_ref, piece), piece_view(refs, piece), sems.at[first + number])
+        for number, piece in enumerate(pieces)
+    ]
 
 
 def project_kernel(q_pieces, v_pieces, q_count, v_count, coords_ref, mixed_ref, *refs):
@@ -271,12 +281,17 @@
 ANYWHERE = pl.BlockSpec(memory_space=pl.ANY)
 
 
-def kernel_call(body, ins, outs, scratch, name, limit, grid=(), semantics=None):
+def cost(micros):
+    return pl.CostEstimate(flops=int(micros * 1e9), transcendentals=0, bytes_accessed=0)
+
+
+def kernel_call(body, ins, outs, scratch, name, limit, micros, grid=()):
     return pl.pallas_call(
         body,
         grid_spec=pltpu.PrefetchScalarGridSpec(num_scalar_prefetch=1, grid=grid, in_specs=ins, out_specs=outs[0], scratch_shapes=scratch),
         out_shape=outs[1],
         compiler_params=pltpu.CompilerParams(vmem_limit_bytes=limit << 20),
+        cost_estimate=cost(micros),
         name=name,
     )
 
@@ -293,15 +308,17 @@
         [pltpu.VMEM((features, wide), BF)] * 2 + [pltpu.SemaphoreType.DMA((len(q_pieces) + len(v_pieces),))],
         "project",
         40,
+        7,
     )(coords, mixed_tree, *q_arrays, *v_arrays)
 
 
-def project_back_kernel(q_pieces, v_pieces, q_count, v_count, q_outs, v_outs, q_made, v_made, coords_ref, mixed_ref, dq_ref, dv_ref, *refs):
+def project_back_kernel(q_pieces, v_pieces, q_count, v_count, q_outs, v_outs, q_made, v_made, coords_ref, mixed_ref, unit_ref, dq_ref, dv_ref, *refs):
     q_refs, v_refs = refs[:q_count], refs[q_count:q_count + v_count]
     rest = refs[q_count + v_count:]
-    partial_ref = rest[0]
-    q_grads, v_grads = rest[1:1 + q_made], rest[1 + q_made:1 + q_made + v_made]
-    q_weight, v_weight, q_sum, v_sum, sems = rest[1 + q_made + v_made:]
+    partial_ref, gain_sum, shift_sum = rest[:3]
+    rest = rest[3:]
+    q_grads, v_grads = rest[:q_made], rest[q_made:q_made + v_made]
+    q_weight, v_weight, q_sum, v_sum, sems = rest[q_made + v_made:]
     to_q = load_pieces(coords_ref, q_refs, q_pieces, q_weight, sems, 0)
     to_v = load_pieces(coords_ref, v_refs, v_pieces, v_weight, sems, len(q_pieces))
     for copy in to_q + to_v:
@@ -319,15 +336,17 @@
         copy.start()
     for copy in to_q + to_v:
         copy.wait()
-    partial_ref[...] = (
-        lax.dot_general(dq_ref[...], q_weight[...], crossed, preferred_element_type=F32)
-        + lax.dot_general(dv_ref[...], v_weight[...], crossed, preferred_element_type=F32)
-    ).astype(BF)
+    partial = lax.dot_general(dq_ref[...], q_weight[...], crossed, preferred_element_type=F32) + lax.dot_general(
+        dv_ref[...], v_weight[...], crossed, preferred_element_type=F32
+    )
+    partial_ref[...] = partial.astype(BF)
+    gain_sum[...] = jnp.sum(partial * unit_ref[...].astype(F32), axis=0, keepdims=True)
+    shift_sum[...] = jnp.sum(partial, axis=0, keepdims=True)
     for copy in from_q + from_v:
         copy.wait()
 
 
-def project_back(coords, mixed_tree, dq, dv, q_side, v_side, q_form, v_form):
+def project_back(coords, mixed_tree, unit_tree, dq, dv, q_side, v_side, q_form, v_form):
     q_arrays, q_pieces = q_side
     v_arrays, v_pieces = v_side
     q_shapes, q_outs = q_form
@@ -339,17 +358,20 @@
     )
     made = kernel_call(
         body,
-        [VM] * 3 + [ANYWHERE] * (len(q_arrays) + len(v_arrays)),
+        [VM] * 4 + [ANYWHERE] * (len(q_arrays) + len(v_arrays)),
         (
-            [VM] + [ANYWHERE] * (len(q_shapes) + len(v_shapes)),
-            [jax.ShapeDtypeStruct((rows, features), BF)] + [jax.ShapeDtypeStruct(s, BF) for s in q_shapes + v_shapes],
+            [VM] * 3 + [ANYWHERE] * (len(q_shapes) + len(v_shapes)),
+            [jax.ShapeDtypeStruct((rows, features), BF)]
+            + [jax.ShapeDtypeStruct((1, features), F32)] * 2
+            + [jax.ShapeDtypeStruct(s, BF) for s in q_shapes + v_shapes],
         ),
         [pltpu.VMEM((features, wide), BF)] * 4
         + [pltpu.SemaphoreType.DMA((len(q_pieces) + len(v_pieces) + len(q_outs) + len(v_outs),))],
         "project_back",
         50,
-    )(coords, mixed_tree, dq, dv, *q_arrays, *v_arrays)
-    return made[0], made[1:1 + len(q_shapes)], made[1 + len(q_shapes):]
+        18,
+    )(coords, mixed_tree, unit_tree, dq, dv, *q_arrays, *v_arrays)
+    return made[:3], made[3:3 + len(q_shapes)], made[3 + len(q_shapes):]
 
 
 def normalised(values):
@@ -381,6 +403,7 @@
         [pltpu.VMEM((features, features), BF), pltpu.SemaphoreType.DMA((len(pieces),))],
         "out_project",
         50,
+        8,
     )(coords, att, first, gain, shift, *arrays)
 
 
@@ -429,128 +452,186 @@
         [pltpu.VMEM((features, features), BF)] * 2 + [pltpu.SemaphoreType.DMA((len(pieces) + len(outs),))],
         "out_back",
         60,
+        12,
     )(coords, back, first_out, grad, att, gain, *arrays)
     return made[:4], made[4:]
 
 
-def feed_kernel(plan, counts, coords_ref, feed_ref, grad_ref, bias_ref, *refs):
-    i_pieces, i_outs, steps, step_outs = plan
-    i_count, u_count, i_made, u_made = counts
+def feed_in_kernel(plan, counts, coords_ref, feed_ref, grad_ref, bias_ref, *refs):
+    pieces, step_outs, block_of = plan
+    i_count, made = counts
+    i_refs = refs[:i_count]
+    active_ref, slope_ref = refs[i_count:i_count + 2]
+    grads = refs[i_count + 2:i_count + 2 + made]
+    weight, outer_sum, in_sems, out_sems = refs[i_count + 2 + made:]
+    step = pl.program_id(0)
+    slot = lax.rem(step, 2)
+    tile = outer_sum.shape[1]
+    count = len(step_outs)
+
+    def store(number):
+        return store_pieces(coords_ref, outer_sum.at[number % 2], grads, step_outs[number], out_sems.at[number % 2], 0)
+
+    @pl.when(step == 0)
+    def _():
+        copies = load_pieces(coords_ref, i_refs, pieces, weight, in_sems, 0)
+        for copy in copies:
+            copy.start()
+        for copy in copies:
+            copy.wait()
+
+    for number in range(2, count):
+
+        @pl.when(step == number)
+        def _(number=number):
+            for copy in store(number - 2):
+                copy.wait()
+
+    columns = pl.ds(pl.multiple_of(block_of(step, coords_ref) * tile, tile), tile)
+    value = jnp.dot(feed_ref[...], weight[:, columns], preferred_element_type=F32) + bias_ref[:, columns]
+    square = value * value
+    bend = jnp.tanh(GELU_A * (value + GELU_B * (square * value)))
+    half = 0.5 * (1.0 + bend)
+    active = (value * half).astype(BF)
+    active_ref[...] = active
+    slope_ref[...] = (half + 0.5 * value * (1.0 - bend * bend) * (GELU_A * (1.0 + 3.0 * GELU_B * square))).astype(BF)
+    outer_sum[slot] = lax.dot_general(active, grad_ref[...], (((0,), (0,)), ((), ())), preferred_element_type=F32).astype(BF)
+
+    for number in range(count):
+
+        @pl.when(step == number)
+        def _(number=number):
+            for copy in store(number):
+                copy.start()
+            if number == count - 1:
+                for last in range(max(0, number - 1), count):
+                    for copy in store(last):
+                        copy.wait()
+
+
+def feed_in(coords, feed, grad, bias, side, form, block_of):
+    arrays, pieces = side
+    shapes, step_outs = form
+    rows, features = feed.shape
+    hidden = bias.shape[1]
+    tile = hidden // len(step_outs)
+    most = max(len(outs) for outs in step_outs)
+    block = pl.BlockSpec((rows, tile), lambda j, co: (0, block_of(j, co)))
+    made = kernel_call(
+        functools.partial(feed_in_kernel, (pieces, step_outs, block_of), (len(arrays), len(shapes))),
+        [VM] * 3 + [ANYWHERE] * len(arrays),
+        (
+            [block, block] + [ANYWHERE] * len(shapes),
+            [jax.ShapeDtypeStruct((rows, hidden), BF)] * 2 + [jax.ShapeDtypeStruct(s, BF) for s in shapes],
+        ),
+        [
+            pltpu.VMEM((features, hidden), BF),
+            pltpu.VMEM((2, tile, features), BF),
+            pltpu.SemaphoreType.DMA((len(pieces),)),
+            pltpu.SemaphoreType.DMA((2, most)),
+        ],
+        "feed_in",
+        60,
+        29,
+        grid=(len(step_outs),),
+    )(coords, feed, grad, bias, *arrays)
+    return made[0], made[1], made[2:]
+
+
+def feed_out_kernel(plan, counts, coords_ref, feed_ref, grad_ref, base_ref, bias_ref, active_ref, slope_ref, *refs):
+    i_pieces, i_outs, steps, block_of = plan
+    i_count, u_count, made = counts
     i_refs, u_refs = refs[:i_count], refs[i_count:i_count + u_count]
     rest = refs[i_count + u_count:]
     out_ref, back_ref, bias_sum = rest[:3]
-    i_grads, u_grads = rest[3:3 + i_made], rest[3 + i_made:3 + i_made + u_made]
-    weight, weight_sum, outer, outer_sum, i_sems, u_sems, iout_sems, uout_sems = rest[3 + i_made + u_made:]
+    grads = rest[3:3 + made]
+    weight, weight_sum, outer, i_sems, u_sems, out_sems = rest[3 + made:]
     step = pl.program_id(0)
     slot = lax.rem(step, 2)
     tile = outer.shape[1]
     count = len(steps)
 
     def u_load(number):
-        return load_pieces(coords_ref, u_refs, steps[number][1], outer.at[number % 2], u_sems.at[number % 2], 0)
-
-    def u_store(number):
-        return store_pieces(coords_ref, outer_sum.at[number % 2], u_grads, step_outs[number], uout_sems.at[number % 2], 0)
+        return load_pieces(coords_ref, u_refs, steps[number], outer.at[number % 2], u_sems.at[number % 2], 0)
 
     @pl.when(step == 0)
     def _():
         copies = load_pieces(coords_ref, i_refs, i_pieces, weight, i_sems, 0)
-        for copy in copies + u_load(0):
+        for copy in u_load(0) + copies:
             copy.start()
-        out_ref[...] = jnp.zeros_like(out_ref)
+        out_ref[...] = base_ref[...] + bias_ref[...]
         back_ref[...] = jnp.zeros_like(back_ref)
         for copy in copies:
             copy.wait()
 
-    block = jnp.int32(0)
     for number in range(count):
-        block = jnp.where(step == number, steps[number][0](coords_ref), block)
 
         @pl.when(step == number)
         def _(number=number):
             if number + 1 < count:
                 for copy in u_load(number + 1):
                     copy.start()
-            if number >= 2:
-                for copy in u_store(number - 2):
-                    copy.wait()
             for copy in u_load(number):
                 copy.wait()
 
-    columns = pl.ds(pl.multiple_of(block * tile, tile), tile)
-    feed = feed_ref[...]
+    columns = pl.ds(pl.multiple_of(block_of(step, coords_ref) * tile, tile), tile)
     grad = grad_ref[...]
-    inner = weight[:, columns]
-    value = jnp.dot(feed, inner, preferred_element_type=F32) + bias_ref[:, columns]
-    square = value * value
-    bend = jnp.tanh(GELU_A * (value + GELU_B * (square * value)))
-    half = 0.5 * (1.0 + bend)
-    active = (value * half).astype(BF)
-    slope = half + 0.5 * value * (1.0 - bend * bend) * (GELU_A * (1.0 + 3.0 * GELU_B * square))
-    out_ref[...] += jnp.dot(active, outer[slot], preferred_element_type=F32)
-    outer_sum[slot] = lax.dot_general(active, grad, (((0,), (0,)), ((), ())), preferred_element_type=F32).astype(BF)
+    out_ref[...] += jnp.dot(active_ref[...], outer[slot], preferred_element_type=F32)
     pulled = lax.dot_general(grad, outer[slot], (((1,), (1,)), ((), ())), preferred_element_type=F32)
-    inner_low = (pulled * slope).astype(BF)
+    inner_low = (pulled * slope_ref[...].astype(F32)).astype(BF)
     bias_sum[:, columns] = jnp.sum(inner_low.astype(F32), axis=0, keepdims=True)
-    weight_sum[:, columns] = lax.dot_general(feed, inner_low, (((0,), (0,)), ((), ())), preferred_element_type=F32).astype(BF)
-    back_ref[...] += lax.dot_general(inner_low, inner, (((1,), (1,)), ((), ())), preferred_element_type=F32)
-
-    for number in range(count):
-
-        @pl.when(step == number)
-        def _(number=number):
-            for copy in u_store(number):
-                copy.start()
-            if number == count - 1:
-                copies = store_pieces(coords_ref, weight_sum, i_grads, i_outs, iout_sems, 0)
-                for copy in copies:
-                    copy.start()
-                if count > 1:
-                    for copy in u_store(number - 1):
-                        copy.wait()
-                for copy in u_store(number):
-                    copy.wait()
-                for copy in copies:
-                    copy.wait()
-
-
-def feed_call(coords, feed, grad, bias, i_side, u_side, i_form, u_form):
+    weight_sum[:, columns] = lax.dot_general(feed_ref[...], inner_low, (((0,), (0,)), ((), ())), preferred_element_type=F32).astype(BF)
+    back_ref[...] += lax.dot_general(inner_low, weight[:, columns], (((1,), (1,)), ((), ())), preferred_element_type=F32)
+
+    @pl.when(step == count - 1)
+    def _():
+        copies = store_pieces(coords_ref, weight_sum, grads, i_outs, out_sems, 0)
+        for copy in copies:
+            copy.start()
+        for copy in copies:
+            copy.wait()
+
+
+def feed_out(coords, feed, grad, base, bias, active, slope, i_side, u_side, i_form, block_of):
     i_arrays, i_pieces = i_side
     u_arrays, steps = u_side
-    i_shapes, i_outs = i_form
-    u_shapes, step_outs = u_form
+    shapes, i_outs = i_form
     rows, features = feed.shape
-    hidden = bias.shape[1]
+    hidden = active.shape[1]
     tile = hidden // len(steps)
-    most = max(len(pieces) for _, pieces in steps)
+    most = max(len(pieces) for pieces in steps)
+    block = pl.BlockSpec((rows, tile), lambda j, co: (0, block_of(j, co)))
     made = kernel_call(
-        functools.partial(feed_kernel, (i_pieces, i_outs, steps, step_outs), (len(i_arrays), len(u_arrays), len(i_shapes), len(u_shapes))),
-        [VM] * 3 + [ANYWHERE] * (len(i_arrays) + len(u_arrays)),
+        functools.partial(feed_out_kernel, (i_pieces, i_outs, steps, block_of), (len(i_arrays), len(u_arrays), len(shapes))),
+        [VM] * 4 + [block, block] + [ANYWHERE] * (len(i_arrays) + len(u_arrays)),
         (
-            [VM] * 3 + [ANYWHERE] * (len(i_shapes) + len(u_shapes)),
+            [VM] * 3 + [ANYWHERE] * len(shapes),
             [jax.ShapeDtypeStruct((rows, features), F32)] * 2
             + [jax.ShapeDtypeStruct((1, hidden), F32)]
-            + [jax.ShapeDtypeStruct(s, BF) for s in i_shapes + u_shapes],
+            + [jax.ShapeDtypeStruct(s, BF) for s in shapes],
         ),
         [
             pltpu.VMEM((features, hidden), BF),
             pltpu.VMEM((features, hidden), BF),
             pltpu.VMEM((2, tile, features), BF),
-            pltpu.VMEM((2, tile, features), BF),
             pltpu.SemaphoreType.DMA((len(i_pieces),)),
             pltpu.SemaphoreType.DMA((2, most)),
             pltpu.SemaphoreType.DMA((len(i_outs),)),
-            pltpu.SemaphoreType.DMA((2, most)),
         ],
-        "feed_forward_backward",
+        "feed_out",
         60,
+        40,
         grid=(len(steps),),
-    )(coords, feed, grad, bias, *i_arrays, *u_arrays)
-    return made[0], made[1], made[2], made[3:3 + len(i_shapes)], made[3 + len(i_shapes):]
+    )(coords, feed, grad, base, bias, active, slope, *i_arrays, *u_arrays)
+    return made[0], made[1], made[2], made[3:]
 
 
 def pick(flag, when_true, when_false):
     return jnp.where(flag, when_true, when_false)
+
+
+def after(value, *earlier):
+    return lax.optimization_barrier((value,) + earlier)[0]
 
 
 class PairPlan:
@@ -560,12 +641,15 @@
         self.odd = me % 2 == 1
         self.tree = me // 2
         self.head_group = me % 2
+        self.far_made = []
 
     def near(self, value):
         return lax.ppermute(value, "fsdp", [(i, i ^ 1) for i in range(4)])
 
     def far(self, value):
-        return lax.ppermute(value, "fsdp", [(i, i ^ 2) for i in range(4)])
+        made = lax.ppermute(value, "fsdp", [(i, i ^ 2) for i in range(4)])
+        self.far_made = [made]
+        return made
 
     def rows_to_tree(self, rows):
         mine = pick(self.upper, rows[1], rows[0])
@@ -597,11 +681,11 @@
         whole = jnp.stack([pick(self.odd, other, keep), pick(self.odd, keep, other)], axis=1)
         return whole.reshape((-1, wide))
 
-    def partial_to_rows(self, partial):
+    def partial_to_rows(self, partial, *earlier):
         blocks = partial.reshape(2, 2, -1, partial.shape[1])
         keep = pick(self.odd, blocks[:, 1], blocks[:, 0])
         got = self.near(pick(self.odd, blocks[:, 0], blocks[:, 1]).astype(BF))
-        return self.swap_trees((keep.astype(F32) + got.astype(F32)).astype(BF)).astype(F32)
+        return self.swap_trees(after((keep.astype(F32) + got.astype(F32)).astype(BF), *earlier)).astype(F32)
 
 
 class GroupPlan:
@@ -613,6 +697,7 @@
         self.tree = me // self.group
         self.head_group = me % self.group
         self.me = me
+        self.far_made = []
 
     def rows_to_tree(self, rows):
         every = lax.all_gather(rows, "fsdp", axis=1, tiled=True)
@@ -630,7 +715,7 @@
         whole = self.rows_to_tree(rows)
         return lax.dynamic_slice_in_dim(whole, self.head_group * wide, wide, 1)
 
-    def partial_to_rows(self, partial):
+    def partial_to_rows(self, partial, *earlier):
         every = jnp.zeros((self.trees,) + partial.shape, F32)
         every = lax.dynamic_update_index_in_dim(every, partial.astype(F32), self.tree, 0)
         return lax.psum_scatter(every, "fsdp", scatter_dimension=1, tiled=True)
@@ -649,7 +734,8 @@
 
 
 class LinkMoves:
-    def __init__(self):
+    def __init__(self, plan):
+        self.plan = plan
         dp, fsdp = lax.axis_index("dp"), lax.axis_index("fsdp")
         self.bits = [fsdp % 2, fsdp // 2, dp % 2, dp // 2 % 2, dp // 4]
         self.coords = jnp.stack([dp // 2, dp % 2, fsdp // 2, fsdp % 2]).astype(jnp.int32)
@@ -684,16 +770,13 @@
             total = wide_of(self.up_z(low(total))) + blocks[k]
         return total
 
-    def gather_small(self, shard):
-        made = shard
-        for bit in range(5):
-            got = self.bit_move(bit, made)
-            one = self.bits[bit] == 1
-            made = pick(one, jnp.concatenate([got, made]), jnp.concatenate([made, got]))
-        return made
+    def small_step(self, bit, made):
+        got = self.bit_move(bit, made)
+        one = self.bits[bit] == 1
+        return pick(one, jnp.concatenate([got, made]), jnp.concatenate([made, got]))
 
     def scatter_small(self, total):
-        made = total
+        made = after(total, *self.heads_first)
         for bit in (4, 3, 2, 1, 0):
             half = made.shape[0] // 2
             one = self.bits[bit] == 1
@@ -710,141 +793,244 @@
         return lambda co: (((co[0] + 4 - k) & 3) * 2 + (co[1] ^ rx)) * 2 + (co[2] ^ ry)
 
     @staticmethod
-    def place8(k, rx):
-        return lambda co: ((co[0] + 4 - k) & 3) * 2 + (co[1] ^ rx)
-
-    @staticmethod
     def place4(ry, rc):
         return lambda co: (co[2] ^ ry) * 2 + (co[3] ^ rc)
 
-    def gather_heads(self, query, value):
+    @staticmethod
+    def block_of(step, co):
+        return ((co[0] + 4 - (step >> 1)) & 3) * 2 + (co[1] ^ (step & 1))
+
+    def heads_pieces(self, which, rows, half):
+        pieces = []
+        for outer in range(2):
+            for inner in range(2):
+                for k in range(4):
+                    rx, ry = (outer, inner) if which == 0 else (inner, outer)
+                    pieces.append((outer, (inner, k), None, rows, self.place16(k, rx, ry), (0, half)))
+        return pieces
+
+    def gather_first(self, small, query, value, output, rows_of):
         count, features = query.shape
         half = features // 2
-        both = jnp.stack([query, value])
+        both = jnp.stack([query, value, output])
         keep = pick(self.odd, both[:, :, half:], both[:, :, :half])
         got = self.core(pick(self.odd, both[:, :, :half], both[:, :, half:]))
         chip = pick(self.odd, jnp.concatenate([got, keep], axis=1), jnp.concatenate([keep, got], axis=1))
-        made = self.ring(chip)
+        made = [chip, self.up_z(chip)]
+        small = self.small_step(1, after(self.small_step(0, small), chip))
+        self.small_early = [small]
+        tree = rows_of(small)
+        made.append(self.up_z(after(made[1], small)))
+        small = self.small_step(2, after(small, made[1]))
+        made.append(self.up_z(after(made[2], small, *self.plan.far_made)))
+        small = self.small_step(4, after(self.small_step(3, small), made[2]))
+        self.heads_ring = made[3]
         sides = []
         for which, first, second in ((0, self.over_y, self.over_x), (1, self.over_x, self.over_y)):
             near = jnp.stack([m[which] for m in made])
             near = jnp.stack([near, first(near)])
-            arrays = [near, second(near)]
-            pieces = []
-            for outer in range(2):
-                for inner in range(2):
+            sides.append(([near, second(after(near, *self.plan.far_made))], self.heads_pieces(which, 2 * count, half)))
+        self.heads_last = [sides[0][0][1], sides[1][0][1]]
+        self.output_near = jnp.stack([m[2] for m in made])
+        self.output_got = self.over_y(after(self.output_near, *self.heads_last))
+        self.output_pieces_in = self.output_parts(2 * count, half)
+        return small, sides, tree
+
+    def output_plane(self, made):
+        near = jnp.stack([self.output_near, after(self.output_got, made)])
+        arrays = [near, self.over_x(near)]
+        self.output_last = [arrays[1]]
+        arrays += [self.core(m) for m in arrays]
+        return arrays, self.output_pieces_in
+
+    def output_parts(self, rows, half):
+        pieces = []
+        for rc in range(2):
+            for rx in range(2):
+                for ry in range(2):
                     for k in range(4):
-                        rx, ry = (outer, inner) if which == 0 else (inner, outer)
-                        pieces.append((outer, (inner, k), None, 2 * count, self.place16(k, rx, ry)))
-            sides.append((arrays, pieces))
-        return sides
+                        columns = ((lambda co, rc=rc: co[3] ^ rc), half)
+                        pieces.append((rc * 2 + rx, (ry, k), None, rows, self.place16(k, rx, ry), columns))
+        return pieces
 
     def heads_form(self, count, half):
         shapes = [(2, 4, 2 * count, half)] * 2
-        forms = []
-        for which in range(2):
-            pieces = []
-            for outer in range(2):
-                for inner in range(2):
-                    for k in range(4):
-                        rx, ry = (outer, inner) if which == 0 else (inner, outer)
-                        pieces.append((outer, (inner, k), None, 2 * count, self.place16(k, rx, ry)))
-            forms.append((shapes, pieces))
-        return forms
-
-    def sum_heads(self, query, value):
+        return [(shapes, self.heads_pieces(which, 2 * count, half)) for which in range(2)]
+
+    def sum_heads(self, query, value, *earlier):
         totals = []
+        self.heads_first = []
+        self.heads_sum = []
         for parts, first, second in ((query, self.over_x, self.over_y), (value, self.over_y, self.over_x)):
-            made = wide_of(parts[0]) + wide_of(first(parts[1]))
-            made = made[0] + wide_of(second(low(made[1])))
-            totals.append(self.ring_sum([made[k] for k in range(4)]))
-        both = jnp.stack(totals)
+            got = first(after(parts[1], *earlier))
+            self.heads_first.append(got)
+            made = wide_of(parts[0]) + wide_of(got)
+            got = second(low(made[1]))
+            self.heads_sum.append(got)
+            totals.append(made[0] + wide_of(got))
+        self.heads_total = jnp.stack(totals, axis=1)
+
+    def sum_heads_last(self, *earlier):
+        made = self.heads_total
+        total = made[1]
+        for k in (2, 3, 0):
+            if k == 0:
+                total = after(total, *earlier)
+            total = wide_of(self.up_z(low(total))) + made[k]
+        both = total
         count = both.shape[1] // 2
         keep = pick(self.odd, both[:, count:], both[:, :count])
         got = wide_of(self.core(low(pick(self.odd, both[:, :count], both[:, count:]))))
         full = pick(self.odd, jnp.concatenate([got, keep], axis=2), jnp.concatenate([keep, got], axis=2))
         return full[0], full[1]
 
-    def gather_inner(self, shard):
-        near = jnp.stack([shard, self.over_y(shard)])
-        plane = jnp.stack([near, self.over_x(near)])
-        made = self.ring(plane)
-        arrays = made + [self.core(m) for m in made]
-        count = shard.shape[0]
-        pieces = [
-            (rc * 4 + k, (rx, ry), None, count, self.place32(k, rx, ry, rc))
-            for rc in range(2)
-            for k in range(4)
-            for rx in range(2)
-            for ry in range(2)
-        ]
-        return arrays, pieces
+
+    def inner_cut(self, hidden):
+        return hidden * 11 // 16
+
+    def inner_pieces(self, count, hidden):
+        cut = self.inner_cut(hidden)
+        pieces = []
+        for part in range(2):
+            for rc in range(2):
+                for outer in range(2):
+                    for inner in range(2):
+                        for k in range(4):
+                            rx, ry = (outer, inner) if part == 0 else (inner, outer)
+                            columns = (0, cut) if part == 0 else (cut, hidden - cut)
+                            pieces.append((rc * 4 + part * 2 + outer, (inner, k), None, count, self.place32(k, rx, ry, rc), columns))
+        return pieces
+
+    def output_pieces(self, count, features):
+        pieces = []
+        for rc in range(2):
+            for ry in range(2):
+                for rx in range(2):
+                    for k in range(4):
+                        pieces.append((rc * 2 + ry, (rx, k), None, count, self.place32(k, rx, ry, rc), (0, features)))
+        return pieces
+
+    def gather_inner(self, inner):
+        count, hidden = inner.shape
+        cut = self.inner_cut(hidden)
+        made = [after(inner, self.heads_ring)]
+        made.append(self.up_z(made[0]))
+        made.append(self.up_z(made[1]))
+        made.append(self.up_z(after(made[2], *self.heads_last)))
+        self.inner_ring = [made[3]]
+        self.inner_made = made
+
+    def inner_plane(self, made):
+        blocks = self.inner_made[:3] + [after(self.inner_made[3], made)]
+        self.inner_ring = blocks[3:]
+        hidden = blocks[0].shape[1]
+        cut = self.inner_cut(hidden)
+        self.inner_near = []
+        self.inner_first = []
+        for part, first in ((0, self.over_y), (1, self.over_x)):
+            near = jnp.stack([m[:, :cut] if part == 0 else m[:, cut:] for m in blocks])
+            self.inner_first.append(first(near))
+            self.inner_near.append(near)
+
+    def inner_across(self, *earlier):
+        near = [jnp.stack(pair) for pair in zip(self.inner_near, self.inner_first)]
+        self.inner_arrays = [near[0], self.over_x(near[0]), near[1], self.over_y(after(near[1], *earlier))]
+
+    def inner_finish(self, made):
+        arrays = list(self.inner_arrays)
+        arrays[1] = after(arrays[1], made)
+        arrays[3] = after(arrays[3], made)
+        count = arrays[0].shape[2]
+        hidden = arrays[0].shape[3] + arrays[2].shape[3]
+        return arrays + [self.core(m) for m in arrays], self.inner_pieces(count, hidden)
 
     def inner_form(self, count, hidden):
-        pieces = [
-            (rc * 4 + k, (rx, ry), None, count, self.place32(k, rx, ry, rc))
-            for rc in range(2)
-            for k in range(4)
-            for rx in range(2)
-            for ry in range(2)
-        ]
-        return [(2, 2, count, hidden)] * 8, pieces
-
-    def sum_inner(self, parts):
-        shares = [None] * 4
+        cut = self.inner_cut(hidden)
+        shapes = ([(2, 4, count, cut)] * 2 + [(2, 4, count, hidden - cut)] * 2) * 2
+        return shapes, self.inner_pieces(count, hidden)
+
+    def output_form(self, count, features):
+        return [(2, 4, count, features)] * 4, self.output_pieces(count, features)
+
+    def sum_inner_cores(self, inner):
+        self.inner_cores = [self.core(part) for part in inner[4:]]
+        return self.inner_cores
+
+    def sum_inner(self, inner, output, *earlier):
+        hidden = inner[0].shape[3] + inner[2].shape[3]
+        first = [wide_of(inner[which]) + wide_of(self.inner_cores[which]) for which in range(2)]
+        first_got = self.over_x(low(first[1]))
+        first_keep = first[0] + wide_of(first_got)
+        halves = []
+        for which in (1, 0):
+            both = [wide_of(inner[2 + which]) + wide_of(self.inner_cores[2 + which])]
+            both.append(wide_of(output[which]) + wide_of(self.core(output[2 + which])))
+            halves.append(both)
+        second_got = self.over_y(after(jnp.concatenate([low(half) for half in halves[0]], axis=3), *earlier))
+        second_keep = jnp.concatenate(halves[1], axis=3) + wide_of(second_got)
+        self.inner_sum_first = [first_got, second_got]
+        self.inner_sum_sent = [low(first_keep[1]), low(second_keep[1])]
+        first_last = self.over_y(self.inner_sum_sent[0])
+        second_last = self.over_x(self.inner_sum_sent[1])
+        self.inner_sum_last = [first_last, second_last]
+        made = jnp.concatenate([first_keep[0] + wide_of(first_last), second_keep[0] + wide_of(second_last)], axis=2)
+        total = self.ring_sum([made[k] for k in range(4)])
+        return total[:, :hidden], total[:, hidden:]
+
+
+    def outer_steps(self, count, features):
+        steps = []
+        for k in range(4):
+            for rx in range(2):
+                steps.append(
+                    [(rc * 4 + k, (rx, ry), None, count, self.place4(ry, rc), (0, features)) for ry in range(2) for rc in range(2)]
+                )
+        return steps
+
+    def gather_outer(self, outer):
+        near = jnp.stack([outer, self.over_x(outer)])
+        self.outer_near = near
+        self.outer_got_y = self.over_y(after(near, *self.heads_last))
+
+    def outer_plane(self, made):
+        plane = jnp.stack([self.outer_near, after(self.outer_got_y, made)], axis=1)
+        self.outer_ring = [plane, self.up_z(after(plane, *self.inner_ring))]
+
+    def outer_next(self, made):
+        self.outer_ring[-1] = after(self.outer_ring[-1], made)
+        self.outer_ring.append(self.up_z(self.outer_ring[-1]))
+
+    def outer_finish(self):
+        arrays = self.outer_ring + [self.core(m) for m in self.outer_ring]
+        return arrays, self.outer_steps(*arrays[0].shape[2:])
+
+    def outer_form(self, count, features):
+        return [(2, 2, count, features)] * 8, self.outer_steps(count, features)
+
+    def sum_outer_first(self, parts):
+        self.shares = [None] * 4
+        cores = []
         for k in (1, 2, 3, 0):
-            shares[k] = wide_of(parts[k]) + wide_of(self.core(parts[4 + k]))
-        made = self.ring_sum(shares)
-        made = made[0] + wide_of(self.over_x(low(made[1])))
-        return made[0] + wide_of(self.over_y(low(made[1])))
-
-    def gather_outer(self, outer, output):
-        count, extra = outer.shape[0], output.shape[0]
-        made = jnp.stack(self.ring(jnp.concatenate([outer, output])))
-        near = jnp.stack([made, self.over_y(made)])
-        across = self.over_x(near)
-        arrays = [near, across, self.core(near), self.core(across)]
-        steps = []
-        for rx in range(2):
-            for k in range(4):
-                pieces = [(rc * 2 + rx, (ry, k), 0, count, self.place4(ry, rc)) for ry in range(2) for rc in range(2)]
-                steps.append((self.place8(k, rx), pieces))
-        output_pieces = [
-            (rc * 2 + rx, (ry, k), count, extra, self.place32(k, rx, ry, rc))
-            for rc in range(2)
-            for rx in range(2)
-            for ry in range(2)
-            for k in range(4)
-        ]
-        return (arrays, steps), (arrays, output_pieces)
-
-    def outer_form(self, count, features):
-        steps = []
-        for rx in range(2):
-            for k in range(4):
-                steps.append([(rc * 2 + rx, (ry, k), None, count, self.place4(ry, rc)) for ry in range(2) for rc in range(2)])
-        return [(2, 4, count, features)] * 4, steps
-
-    def output_form(self, count, features):
-        pieces = [
-            (rc * 2 + rx, (ry, k), None, count, self.place32(k, rx, ry, rc))
-            for rc in range(2)
-            for rx in range(2)
-            for ry in range(2)
-            for k in range(4)
-        ]
-        return [(2, 4, count, features)] * 4, pieces
-
-    def sum_outer(self, outer, output):
-        halves = []
-        for parts in (outer, output):
-            sent = low(wide_of(parts[1]) + wide_of(self.core(parts[3])))
-            halves.append(wide_of(parts[0]) + wide_of(self.core(parts[2])) + wide_of(self.over_x(sent)))
-        made = jnp.concatenate([low(h[1]) for h in halves], axis=1)
-        made = wide_of(self.over_y(made)) + jnp.concatenate([h[0] for h in halves], axis=1)
-        total = self.ring_sum([made[k] for k in range(4)])
-        count = outer[0].shape[2]
-        return total[:count], total[count:]
+            cores.append(self.core(parts[4 + k]))
+            self.shares[k] = wide_of(parts[k]) + wide_of(cores[-1])
+        self.outer_got = self.up_z(low(self.shares[1]))
+        return [self.outer_got] + cores
+
+    def sum_outer_step(self, k, *earlier):
+        if earlier:
+            self.outer_got = after(self.outer_got, *earlier)
+        total = low(wide_of(self.outer_got) + self.shares[k])
+        self.outer_got = self.up_z(total)
+        return [self.outer_got]
+
+    def sum_outer_x(self, *earlier):
+        total = wide_of(after(self.outer_got, *earlier)) + self.shares[0]
+        got = self.over_x(low(total[1]))
+        self.outer_total = total[0] + wide_of(got)
+        return [got]
+
+    def sum_outer_last(self, *earlier):
+        return self.outer_total[0] + wide_of(self.over_y(after(low(self.outer_total[1]), *earlier)))
 
 
 class PlainMoves:
@@ -852,6 +1038,8 @@
         self.plan = plan
         self.wide = wide
         self.coords = jnp.zeros((4,), jnp.int32)
+        self.small_early = self.inner_ring = self.inner_first = self.inner_sum_first = self.inner_sum_last = self.heads_sum = []
+        self.output_last = self.inner_sum_sent = []
 
     @staticmethod
     def start(co):
@@ -863,60 +1051,107 @@
     def scatter(self, total):
         return lax.psum_scatter(total, AXES, scatter_dimension=0, tiled=True)
 
-    def whole(self, rows):
-        return [(0, (), None, rows, self.start)]
-
-    def gather_small(self, shard):
-        return self.gather(shard)
+    def whole(self, rows, columns):
+        return [(0, (), None, rows, self.start, (0, columns))]
+
+    @staticmethod
+    def block_of(step, co):
+        return step
 
     def scatter_small(self, total):
         return self.scatter(total)
 
-    def gather_heads(self, query, value):
+    def gather_first(self, small, query, value, output, rows_of):
         sides = []
         for shard in (query, value):
             cols = lax.dynamic_slice_in_dim(self.gather(shard), self.plan.head_group * self.wide, self.wide, 1)
-            sides.append(([cols], self.whole(cols.shape[0])))
-        return sides
+            sides.append(([cols], self.whole(*cols.shape)))
+        self.output_full = self.gather(output)
+        small = self.gather(small)
+        return small, sides, rows_of(small)
 
     def heads_form(self, count, half):
         features = H * DH
-        return [([(features, self.wide)], self.whole(features))] * 2
-
-    def sum_heads(self, query, value):
+        return [([(features, self.wide)], self.whole(features, self.wide))] * 2
+
+    def sum_heads(self, query, value, *earlier):
+        self.heads_parts = (query[0], value[0])
+
+    def sum_heads_last(self, *earlier):
         made = []
-        for cols in (query[0], value[0]):
+        for cols in self.heads_parts:
             full = jnp.zeros((cols.shape[0], H * DH), F32)
             made.append(self.scatter(lax.dynamic_update_slice_in_dim(full, wide_of(cols), self.plan.head_group * self.wide, 1)))
         return made
 
-    def gather_inner(self, shard):
-        full = self.gather(shard)
-        self.features, self.hidden = full.shape
-        return [full], self.whole(full.shape[0])
+    def gather_inner(self, inner):
+        self.inner_full = self.gather(inner)
+        self.features, self.hidden = self.inner_full.shape
+
+    def inner_plane(self, made):
+        pass
+
+    def inner_across(self, *earlier):
+        pass
+
+    def inner_finish(self, made):
+        return [self.inner_full], self.whole(*self.inner_full.shape)
+
+    def output_plane(self, made):
+        return [self.output_full], self.whole(*self.output_full.shape)
 
     def inner_form(self, count, hidden):
-        return [(self.features, hidden)], self.whole(self.features)
-
-    def sum_inner(self, parts):
-        return self.scatter(wide_of(parts[0]))
-
-    def gather_outer(self, outer, output):
-        self.steps = self.hidden // 512
-        full = self.gather(outer).reshape(self.steps, -1, outer.shape[1])
-        steps = [((lambda co, s=s: co[0] * 0 + s), [(0, (s,), None, full.shape[1], self.start)]) for s in range(self.steps)]
-        other = self.gather(output)
-        return ([full], steps), ([other], self.whole(other.shape[0]))
+        return [(self.features, hidden)], self.whole(self.features, hidden)
+
+    def output_form(self, count, features):
+        return [(H * DH, features)], self.whole(H * DH, features)
+
+    def sum_inner_cores(self, inner):
+        return []
+
+    def sum_inner(self, inner, output, *earlier):
+        return self.scatter(wide_of(inner[0])), self.scatter(wide_of(output[0]))
+
+    def outer_steps(self, features):
+        return [[(0, (s,), None, 512, self.start, (0, features))] for s in range(self.hidden // 512)]
+
+    def gather_outer(self, outer):
+        self.outer_full = self.gather(outer)
+
+    def outer_plane(self, made):
+        pass
+
+    def outer_next(self, made):
+        pass
+
+    def outer_finish(self):
+        features = self.outer_full.shape[1]
+        return [self.outer_full.reshape(-1, 512, features)], self.outer_steps(features)
 
     def outer_form(self, count, features):
-        tile = self.hidden // self.steps
-        return [(self.steps, tile, features)], [[(0, (s,), None, tile, self.start)] for s in range(self.steps)]
-
-    def output_form(self, count, features):
-        return [(H * DH, features)], self.whole(H * DH)
-
-    def sum_outer(self, outer, output):
-        return self.scatter(wide_of(outer[0]).reshape(self.hidden, -1)), self.scatter(wide_of(output[0]))
+        return [(self.hidden // 512, 512, features)], self.outer_steps(features)
+
+    def sum_outer_first(self, parts):
+        self.outer_total = wide_of(parts[0]).reshape(self.hidden, -1)
+        return []
+
+    def sum_outer_step(self, k, *earlier):
+        return []
+
+    def sum_outer_x(self, *earlier):
+        return []
+
+    def sum_outer_last(self, *earlier):
+        return self.scatter(self.outer_total)
+
+
+def join_vectors(parts):
+    total = sum(part.shape[0] for part in parts)
+    made, begin = 0.0, 0
+    for part in parts:
+        made = made + jnp.pad(wide_of(part), (begin, total - begin - part.shape[0]))
+        begin += part.shape[0]
+    return low(made)
 
 
 def per_device(
@@ -955,7 +1190,7 @@
     wide = local_heads * DH
     linked = (dp_size, fsdp_size, trees) == (8, 4, 2)
     plan = PairPlan() if linked else GroupPlan(fsdp_size, trees)
-    moves = LinkMoves() if linked else PlainMoves(plan, wide)
+    moves = LinkMoves(plan) if linked else PlainMoves(plan, wide)
     coords = moves.coords
 
     first = first_half[:, 0]
@@ -967,7 +1202,15 @@
 
     small_parts = (inner_bias, outer_bias, mixer_gain, mixer_shift, feed_gain, feed_shift)
     small_sizes = [v.shape[0] for v in small_parts]
-    small = wide_of(moves.gather_small(jnp.concatenate(small_parts)[None]))
+    mix_unit, mix_factor = norm_stats(second)
+    small, (q_side, v_side), unit_tree = moves.gather_first(
+        join_vectors(small_parts)[None],
+        query_weight,
+        value_weight,
+        output_weight,
+        lambda early: plan.rows_to_tree(after(low(mix_unit), early)),
+    )
+    small = wide_of(small)
     vectors = []
     begin = 0
     for size in small_sizes:
@@ -975,14 +1218,12 @@
         begin += size
     bias_inner, bias_outer, gain_mix, shift_mix, gain_feed, shift_feed = vectors
 
-    q_side, v_side = moves.gather_heads(query_weight, value_weight)
-    i_side = moves.gather_inner(inner_weight)
-    u_side, o_side = moves.gather_outer(outer_weight, output_weight)
-
-    mix_unit, mix_factor = norm_stats(second)
-    mixed_tree = plan.rows_to_tree(low(mix_unit * gain_mix + shift_mix))
-    parent_row = lax.dynamic_index_in_dim(parents[:, 0], plan.tree, 0, False)
-    bucket_rows = lax.dynamic_index_in_dim(buckets[:, 0], plan.tree, 0, False)
+    moves.gather_inner(inner_weight)
+    moves.gather_outer(outer_weight)
+
+    mixed_tree = low(wide_of(unit_tree) * gain_mix + shift_mix)
+    parent_row = lax.dynamic_index_in_dim(after(parents, *moves.small_early)[:, 0], plan.tree, 0, False)
+    bucket_rows = lax.dynamic_index_in_dim(after(buckets, *moves.small_early)[:, 0], plan.tree, 0, False)
     branch = parent_row[jnp.clip(parent_row, 0, segments - 1)]
     trunk_end = jnp.where(jnp.arange(segments) >= TRUNK + BRANCHES, branch, parent_row)
     info = jnp.concatenate([parent_row, trunk_end])
@@ -991,19 +1232,39 @@
     codes_k = jnp.pad(codes.T, ((0, 8 - rounds), (0, 0)))
     query_key, value_rows = project(coords, mixed_tree, q_side, v_side, wide)
     attend, attend_back = attention_calls(tree_len, local_heads, rounds, segments)
+    moves.inner_plane(query_key)
+    o_side = moves.output_plane(query_key)
+    moves.outer_plane(query_key)
     attended, totals, counts = attend(info, query_key, value_rows, codes_q, codes_k)
-    attended_low = flat(plan.heads_to_rows(attended))
+    moves.outer_next(attended)
+    attended_low = flat(plan.heads_to_rows(after(attended, *moves.inner_first, *moves.output_last)))
+    moves.inner_across(*plan.far_made)
 
     first_out, feed_low = out_project(coords, attended_low, flat(first), gain_feed, shift_feed, o_side)
+    i_side = moves.inner_finish(feed_low)
+    moves.outer_next(feed_low)
     outer_low = flat(low(grad_b))
-    i_form = moves.inner_form(inner_weight.shape[0], hidden)
-    u_form = moves.outer_form(outer_weight.shape[0], features)
-    fed, grad_feed, inner_bias_sum, inner_parts, outer_parts = feed_call(coords, feed_low, outer_low, bias_inner, i_side, u_side, i_form, u_form)
-    second_out = second + fed.reshape(second.shape) + bias_outer
+    active, slope, outer_parts = feed_in(
+        coords, feed_low, outer_low, bias_inner, i_side, moves.outer_form(*outer_weight.shape), moves.block_of
+    )
+    outer_ring = moves.sum_outer_first(outer_parts)
+    second_out, grad_feed, inner_bias_sum, inner_parts = feed_out(
+        coords,
+        feed_low,
+        outer_low,
+        flat(second),
+        bias_outer,
+        active,
+        slope,
+        i_side,
+        moves.outer_finish(),
+        moves.inner_form(*inner_weight.shape),
+        moves.block_of,
+    )
     outer_bias_sum = jnp.sum(wide_of(outer_low), axis=0)
     (grad_first_in, grad_attended, feed_gain_sum, feed_shift_sum), output_parts = out_back(
         coords,
-        grad_feed,
+        after(grad_feed, *outer_ring),
         first_out,
         flat(grad_first),
         attended_low,
@@ -1012,18 +1273,32 @@
         moves.output_form(output_weight.shape[0], features),
     )
 
+
+    outer_ring = moves.sum_outer_step(2, grad_feed)
+    grad_attended = after(grad_attended, *moves.sum_inner_cores(inner_parts))
     grad_heads = plan.rows_to_heads(grad_attended.reshape(trees, row_count, features))
+    inner_grad, output_grad = moves.sum_inner(inner_parts, output_parts, *plan.far_made)
     query_low, value_low = attend_back(info, query_key, value_rows, attended, grad_heads, totals, counts)
+    outer_ring = moves.sum_outer_step(3, query_low)
     q_form, v_form = moves.heads_form(query_weight.shape[0], wide)
-    partial, query_parts, value_parts = project_back(coords, mixed_tree, query_low, value_low, q_side, v_side, q_form, v_form)
-    grad_mixed = plan.partial_to_rows(partial)
-    mix_gain_sum = jnp.sum(grad_mixed * mix_unit, axis=(0, 1))
-    mix_shift_sum = jnp.sum(grad_mixed, axis=(0, 1))
+    (partial, mix_gain_sum, mix_shift_sum), query_parts, value_parts = project_back(
+        coords,
+        mixed_tree,
+        unit_tree,
+        after(query_low, *moves.inner_sum_first, *moves.inner_sum_sent),
+        value_low,
+        q_side,
+        v_side,
+        q_form,
+        v_form,
+    )
+    moves.sum_heads(query_parts, value_parts, *moves.inner_sum_last)
+    moves.sum_outer_x(*moves.heads_sum)
+    grad_mixed = plan.partial_to_rows(partial, *moves.heads_sum[:1])
+    query_grad, value_grad = moves.sum_heads_last(*plan.far_made)
+    outer_grad = moves.sum_outer_last()
     grad_second_in = grad_b + norm_back(mix_unit, mix_factor, gain_mix, grad_mixed)
 
-    inner_grad = moves.sum_inner(inner_parts)
-    outer_grad, output_grad = moves.sum_outer(outer_parts, output_parts)
-    query_grad, value_grad = moves.sum_heads(query_parts, value_parts)
     small_sums = [inner_bias_sum, outer_bias_sum, mix_gain_sum, mix_shift_sum, feed_gain_sum, feed_shift_sum]
     packed = moves.scatter_small(jnp.concatenate([v.reshape(devices, -1) for v in small_sums], axis=1))[0]
     pieces = []
@@ -1033,7 +1308,7 @@
         begin += size
     return (
         first_out.reshape(first_half.shape),
-        second_out[:, None],
+        second_out.reshape(first_half.shape),
         grad_first_in.reshape(first_half.shape),
         grad_second_in[:, None],
         query_grad,

time: 602 us -> 461 us (0.77)
  waiting for transfers between devices: 328 us -> 153 us
  starting transfers between devices: 39.2 us -> 60.6 us
  Pallas kernels: 133 us -> 153 us
    ppermute x8 -> x11, waiting for transfers between devices: 77.1 us -> 13 us  [over_y(): return lax.ppermute(value, 'fsdp', swap_pairs(4, 2))]
    ppermute x9 -> x11, waiting for transfers between devices: 60.9 us -> 5.82 us  [over_x(): return lax.ppermute(value, 'dp', swap_pairs(8, 1))]
    ppermute x6, waiting for transfers between devices: 59.6 us -> 9.42 us  [bit_move(): return lax.ppermute(value, 'dp', swap_pairs(8, 1 << bit - 2))]
    ppermute x4, waiting for transfers between devices: 31.9 us -> 11.7 us  [far(): made = lax.ppermute(value, 'fsdp', [(i, i ^ 2) for i in range(4)])]
    pallas_call x2 -> x3, Pallas kernels: 69 us -> 87.2 us  [the longest x1 40.4 us: feed_out(): kernel_call(functools.partial(feed_out_kernel, (i_pieces, i_outs, steps,...]
    ppermute x21 -> x18, waiting for transfers between devices: 89.9 us -> 106 us  [up_z(): return lax.ppermute(value, 'dp', [(i, (i + 2) % 8) for i in range(8)])]
    ppermute x21 -> x18, starting transfers between devices: 6.04 us -> 13.4 us  [up_z(): return lax.ppermute(value, 'dp', [(i, (i + 2) % 8) for i in range(8)])]
    convert_element_type x13 -> x14, other arithmetic: 11.5 us -> 16.1 us  [low(): return value.astype(BF)]
  transfers between devices with their start and end apart: 72 -> 80, of which waited for: 35 -> 28; matrix products, arithmetic and copies ran while one was open for 13% -> 16% of each run, Pallas kernels for 11% -> 34%
where the time goes in v3:
time: 461 us; the launch traced here: 455 us
  waiting for transfers between devices  153 us (33%)
  Pallas kernels  153 us (33%)
  starting transfers between devices  60.6 us (13%)
  other arithmetic  57.2 us (12%)
  local copies, waits for them, and re-layouts  27.9 us (6%)
    ppermute x18, waiting for transfers between devices, up_z(): return lax.ppermute(value, 'dp', [(i, (i + 2) % 8) for i in range(8)])  106 us
    pallas_call x1, Pallas kernels, feed_out(): kernel_call(functools.partial(feed_out_kernel, (i_pieces, i_outs, steps,...  40.4 us
    pallas_call x1, Pallas kernels, feed_in(): kernel_call(functools.partial(feed_in_kernel, (pieces, step_outs, block_o...  29 us
    pallas_call x1, Pallas kernels, per_device(): attend_back(info, query_key, value_rows, attended, grad_heads, totals, co...  20.9 us
    pallas_call x1, Pallas kernels, per_device(): attend(info, query_key, value_rows, codes_q, codes_k)  17.9 us
    pallas_call x1, Pallas kernels, project_back(): kernel_call(body, [VM] * 4 + [ANYWHERE] * (len(q_arrays) + len(v_arrays))...  17.8 us
    convert_element_type x14, other arithmetic, low(): return value.astype(BF)  16.1 us
    ppermute x11, starting transfers between devices, over_x(): return lax.ppermute(value, 'dp', swap_pairs(8, 1))  15.8 us
  transfers between devices with their start and end apart: 80, of which 28 were waited for; matrix products, arithmetic and copies ran while one was open for 16% of the time, Pallas kernels for 34%

profile of v3, /device:TPU:0, one launch (start us, length us, event | category | flops | bytes accessed | tf_op | source)
XLA Modules:
  0.0 454.9 jit_solution(3298495595787055708)
XLA Ops:
  3.1 2.9 collective-permute-start.32
  6.0 1.9 reduce_sum.63
  13.1 2.0 collective-permute-done.2
  22.3 2.1 fusion.55
  29.6 2.2 collective-permute-done.8
  33.2 3.2 collective-permute-done.9
  39.3 6.6 %collective-permute-done.10 = bf16[3,64,512]{2,1,0:T(8,128)(2,1)S(1)} collective-permute-done((bf16[3,64,512]{2,1,0:T(8,128)(2,1)S(1)}, bf16[3,64,512]{2,1,0:T(8,128)(2,1)S(1)}, u32[]{:S(2)}, u32[]{:S(2)}) %collective-permute-start.10) | collective-permute-done | bytes 196640 | tf_op jit(solution)/shard_map/ppermute | solution.py:754
  48.4 6.2 %collective-permute-done.11 = bf16[4,64,512]{2,1,0:T(8,128)(2,1)S(1)} collective-permute-done((bf16[4,64,512]{2,1,0:T(8,128)(2,1)S(1)}, bf16[4,64,512]{2,1,0:T(8,128)(2,1)S(1)}, u32[]{:S(2)}, u32[]{:S(2)}) %collective-permute-start.11) | collective-permute-done | bytes 262176 | tf_op jit(solution)/shard_map/ppermute | solution.py:748
  54.6 2.4 collective-permute-start.12
  57.6 10.4 %collective-permute-done.16 = bf16[32,4096]{1,0:T(8,128)(2,1)S(1)} collective-permute-done((bf16[32,4096]{1,0:T(8,128)(2,1)S(1)}, bf16[32,4096]{1,0:T(8,128)(2,1)S(1)}, u32[]{:S(2)}, u32[]{:S(2)}) %collective-permute-start.16) | collective-permute-done | bytes 262176 | tf_op jit(solution)/shard_map/ppermute | solution.py:754
  68.1 3.8 collective-permute-done.14.refs_3_
  72.1 2.0 collective-permute-start.33
  76.8 7.1 %project.1 = (bf16[1280,512]{1,0:T(8,128)(2,1)S(1)}, bf16[1280,512]{1,0:T(8,128)(2,1)S(1)}) custom-call(s32[4]{0:T(128)S(1)} %pad_add_fusion.coords_ref, bf16[1280,1024]{1,0:T(8,128)(2,1)S(1)} %add_convert_fusion.mixed_ref, bf16[2,4,64,512]{3,2,1,0:T(8,128)(2,1)S(1)} %pad_maximum_fusion.14.refs_0_, ...), custom_call_target="tpu_custom_call" | custom-call | flops 7000000000 | tf_op jit(solution)/shard_map/project/pallas_call | solution.py:304
  84.3 2.1 collective-permute-start.19
  86.6 17.9 %attention_forward.1 = (bf16[1280,512]{1,0:T(8,128)(2,1)S(1)}, f32[1280,128]{1,0:T(8,128)S(1)}, bf16[1280,768]{1,0:T(8,128)(2,1)S(1)}) custom-call(s32[20]{0:T(128)S(1)} %pad_add_fusion.1.info_ref, bf16[1280,512]{1,0:T(8,128)(2,1)S(1)} %get-tuple-element.105.q_ref, bf16[1280,512]{1,0:T(8,128)(2,1)S(1)} %get-tuple-element.106.v_ref, ...), custom_call_target="tpu_custom_call" | custom-call | flops 17999998976 | tf_op jit(solution)/shard_map/attention_forward/pallas_call | solution.py:1238
  108.2 2.4 select_bitcast_fusion.8
  110.5 1.9 collective-permute-start.23
  114.5 19.8 %collective-permute-done.34.refs_9_ = bf16[2,2,128,1024]{3,2,1,0:T(8,128)(2,1)} collective-permute-done((bf16[2,2,128,1024]{3,2,1,0:T(8,128)(2,1)}, bf16[2,2,128,1024]{3,2,1,0:T(8,128)(2,1)}, u32[]{:S(2)}, u32[]{:S(2)}) %collective-permute-start.34) | collective-permute-done | bytes 1048608 | tf_op jit(solution)/shard_map/ppermute | solution.py:754
  135.0 2.2 fusion.23
  138.4 7.9 %out_project.1 = (f32[640,1024]{1,0:T(8,128)}, bf16[640,1024]{1,0:T(8,128)(2,1)S(1)}) custom-call(s32[4]{0:T(128)S(1)} %pad_add_fusion.coords_ref, bf16[640,1024]{1,0:T(8,128)(2,1)} %bitcast.305, f32[640,1024]{1,0:T(8,128)} %bitcast.321, f32[1,1024]{1,0:T(1,128)S(1)} %reshape.315.gain_ref, f32[1,1024]{1,0:T(1,128)S(1)} %reshape.316.shift_ref, ...), custom_call_target="tpu_custom_call" | custom-call | flops 8000000000 | tf_op jit(solution)/shard_map/out_project/pallas_call | solution.py:399
  148.4 14.0 %collective-permute-done.35.refs_10_ = bf16[2,2,128,1024]{3,2,1,0:T(8,128)(2,1)} collective-permute-done((bf16[2,2,128,1024]{3,2,1,0:T(8,128)(2,1)}, bf16[2,2,128,1024]{3,2,1,0:T(8,128)(2,1)}, u32[]{:S(2)}, u32[]{:S(2)}) %collective-permute-start.35) | collective-permute-done | bytes 1048608 | tf_op jit(solution)/shard_map/ppermute | solution.py:754
  162.4 2.0 collective-permute-done.27.refs_3_
  168.0 21.2 %collective-permute-done.36.refs_11_ = bf16[2,2,128,1024]{3,2,1,0:T(8,128)(2,1)S(1)} collective-permute-done((bf16[2,2,128,1024]{3,2,1,0:T(8,128)(2,1)}, bf16[2,2,128,1024]{3,2,1,0:T(8,128)(2,1)S(1)}, u32[]{:S(2)}, u32[]{:S(2)}) %collective-permute-start.36) | collective-permute-done | bytes 1048608 | tf_op jit(solution)/shard_map/ppermute | solution.py:754
  189.2 29.0 %feed_in.1 = (bf16[640,4096]{1,0:T(8,128)(2,1)}, bf16[640,4096]{1,0:T(8,128)(2,1)}, bf16[2,2,128,1024]{3,2,1,0:T(8,128)(2,1)}, bf16[2,2,128,1024]{3,2,1,0:T(8,12...) custom-call(s32[4]{0:T(128)} %copy-done.7, ...), custom_call_target="tpu_custom_call" | custom-call | flops 28999999488 | tf_op jit(solution)/shard_map/feed_in/pallas_call | solution.py:520
  218.7 40.4 %feed_out.1 = (f32[640,1024]{1,0:T(8,128)}, f32[640,1024]{1,0:T(8,128)}, f32[1,4096]{1,0:T(1,128)}, bf16[2,4,32,2816]{3,2,1,0:T(8,128)(2,1)}, bf16[2,4,32,2816]{...) custom-call(s32[4]{0:T(128)} %copy-done.7, ...), custom_call_target="tpu_custom_call" | custom-call | flops 40000000000 | tf_op jit(solution)/shard_map/feed_out/pallas_call | solution.py:604
  262.9 2.2 add_convert_fusion.5
  265.1 1.9 collective-permute-done.48
  268.7 21.5 %collective-permute-done.42 = bf16[2,2,128,1024]{3,2,1,0:T(8,128)(2,1)S(1)} collective-permute-done((bf16[2,2,128,1024]{3,2,1,0:T(8,128)(2,1)S(1)}, bf16[2,2,128,1024]{3,2,1,0:T(8,128)(2,1)S(1)}, u32[]{:S(2)}, u32[]{:S(2)}) %collective-permute-start.42) | collective-permute-done | bytes 1048608 | tf_op jit(solution)/shard_map/ppermute | solution.py:754
  291.2 11.8 %out_back.1 = (f32[640,1024]{1,0:T(8,128)}, bf16[640,1024]{1,0:T(8,128)(2,1)}, f32[1,1024]{1,0:T(1,128)}, f32[1,1024]{1,0:T(1,128)}, bf16[2,4,32,1024]{3,2,1,0:T...) custom-call(s32[4]{0:T(128)} %copy-done.7, ...), custom_call_target="tpu_custom_call" | custom-call | flops 12000000000 | tf_op jit(solution)/shard_map/out_back/pallas_call | solution.py:445
  308.2 2.6 add_convert_fusion.3
  312.6 1.7 add_convert_fusion.1
  314.4 1.7 collective-permute-start.52
  316.1 11.7 %collective-permute-done.50 = bf16[320,1024]{1,0:T(8,128)(2,1)S(1)} collective-permute-done((bf16[320,1024]{1,0:T(8,128)(2,1)S(1)}, bf16[320,1024]{1,0:T(8,128)(2,1)S(1)}, u32[]{:S(2)}, u32[]{:S(2)}) %collective-permute-start.50) | collective-permute-done | bytes 655392 | tf_op jit(solution)/shard_map/ppermute | solution.py:650
  335.8 20.9 %attention_backward.1 = (bf16[1280,512]{1,0:T(8,128)(2,1)S(1)}, bf16[1280,512]{1,0:T(8,128)(2,1)S(1)}) custom-call(s32[20]{0:T(128)S(1)} %pad_add_fusion.1.info_ref, bf16[1280,512]{1,0:T(8,128)(2,1)S(1)} %copy-done.15, bf16[1280,512]{1,0:T(8,128)(2,1)S(1)} %copy-done.17, bf16[1280,512]{1,0:T(8,128)(2,1)S(1)} %get-tuple-element.114.out_ref, ...), custom_call_target="tpu_custom_call" | custom-call | flops 20999999488 | tf_op jit(solution)/shard_map/attention_backward/pallas_call | solution.py:1281
  363.1 17.8 %project_back.1 = (bf16[1280,1024]{1,0:T(8,128)(2,1)}, f32[1,1024]{1,0:T(1,128)S(1)}, f32[1,1024]{1,0:T(1,128)S(1)}, bf16[2,4,64,512]{3,2,1,0:T(8,128)(2,1)S(1)}...) custom-call(s32[4]{0:T(128)S(1)} %copy-done.8, ...), custom_call_target="tpu_custom_call" | custom-call | flops 17999998976 | tf_op jit(solution)/shard_map/project_back/pallas_call | solution.py:359
  391.4 2.5 collective-permute-done.59
  395.7 2.7 collective-permute-start.71
  402.8 3.5 collective-permute-done.72
  411.9 1.7 collective-permute-done.74
  417.3 2.5 collective-permute-start.70
  419.9 2.2 fusion.1
  423.5 2.5 collective-permute-start.64
  426.1 2.1 add_add_fusion
  429.6 1.9 collective-permute-done.64
  434.1 4.5 collective-permute-done.65
  438.6 2.6 collective-permute-done.78
  447.0 2.0 multiply_add_fusion
  449.0 3.5 collective-permute-done.66
  (426 shorter events, 110.6 us)
Async XLA Ops:
  3.1 19.2 %collective-permute-start.32 = (bf16[128,1024]{1,0:T(8,128)(2,1)}, bf16[128,1024]{1,0:T(8,128)(2,1)}, u32[]{:S(2)}, u32[]{:S(2)}) collective-permute-start(bf16[128,1024]{1,0:T(8,128)(2,1)} %param.27), channel_id=1, source_target_pairs={{0,4},{4,0},{8,12},{12,8},{16,20},{20,16},{24,28},{28,24},{1,5},{5... | collective-permute-start | bytes 786440 | tf_op jit(solution)/shard_map/ppermute | solution.py:751
  10.0 11.7 %collective-permute-start.5 = (bf16[3,64,512]{2,1,0:T(8,128)(2,1)S(1)}, bf16[3,64,512]{2,1,0:T(8,128)(2,1)S(1)}, u32[]{:S(2)}, u32[]{:S(2)}) collective-permute-start(bf16[3,64,512]{2,1,0:T(8,128)(2,1)S(1)} %maximum_select_fusion.1), channel_id=1, source_target_pairs={{0,8},{4,12},{8,16},{12,20},{16,24},{20,28},{24,0},{28,4},{1,9},{5... | collective-permute-start | bytes 589832 | tf_op jit(solution)/shard_map/ppermute | solution.py:754
  19.7 18.1 %collective-permute-start.3 = (bf16[320,1024]{1,0:T(8,128)(2,1)}, bf16[320,1024]{1,0:T(8,128)(2,1)}, u32[]{:S(2)}, u32[]{:S(2)}) collective-permute-start(bf16[320,1024]{1,0:T(8,128)(2,1)} %select_bitcast_fusion.10), channel_id=1, source_target_pairs={{0,2},{1,3},{2,0},{3,1},{4,6},{5,7},{6,4},{7,5},{8,10},{9,11},{10,... | collective-permute-start | bytes 1966088 | tf_op jit(solution)/shard_map/ppermute | solution.py:650
  39.2 35.0 %collective-permute-start.4 = (bf16[2,320,1024]{2,1,0:T(8,128)(2,1)S(1)}, bf16[2,320,1024]{2,1,0:T(8,128)(2,1)S(1)}, u32[]{:S(2)}, u32[]{:S(2)}) collective-permute-start(bf16[2,320,1024]{2,1,0:T(8,128)(2,1)S(1)} %pad_maximum_fusion.2), channel_id=1, source_target_pairs={{0,1},{1,0},{2,3},{3,2},{4,5},{5,4},{6,7},{7,6},{8,9},{9,8},{10,11... | collective-permute-start | bytes 3932168 | tf_op jit(solution)/shard_map/ppermute | solution.py:647
  54.6 13.4 %collective-permute-start.12 = (bf16[2,4,64,512]{3,2,1,0:T(8,128)(2,1)S(1)}, bf16[2,4,64,512]{3,2,1,0:T(8,128)(2,1)S(1)}, u32[]{:S(2)}, u32[]{:S(2)}) collective-permute-start(bf16[2,4,64,512]{3,2,1,0:T(8,128)(2,1)S(1)} %pad_maximum_fusion.14.refs_0_), channel_id=1, source_target_pairs={{0,4},{4,0},{8,12},{12,8},{16,20},{20,16},{24,28},{28,24},{1,5},{5... | collective-permute-start | bytes 1572872 | tf_op jit(solution)/shard_map/ppermute | solution.py:751
  57.0 14.9 %collective-permute-start.14 = (bf16[2,4,64,512]{3,2,1,0:T(8,128)(2,1)S(1)}, bf16[2,4,64,512]{3,2,1,0:T(8,128)(2,1)S(1)}, u32[]{:S(2)}, u32[]{:S(2)}) collective-permute-start(bf16[2,4,64,512]{3,2,1,0:T(8,128)(2,1)S(1)} %pad_maximum_fusion.15.refs_2_), channel_id=1, source_target_pairs={{0,2},{1,3},{2,0},{3,1},{4,6},{5,7},{6,4},{7,5},{8,10},{9,11},{10,... | collective-permute-start | bytes 1572872 | tf_op jit(solution)/shard_map/ppermute | solution.py:748
  71.9 12.1 %collective-permute-start.17 = (bf16[32,4096]{1,0:T(8,128)(2,1)S(1)}, bf16[32,4096]{1,0:T(8,128)(2,1)S(1)}, u32[]{:S(2)}, u32[]{:S(2)}) collective-permute-start(bf16[32,4096]{1,0:T(8,128)(2,1)S(1)} %collective-permute-done.16), channel_id=1, source_target_pairs={{0,8},{4,12},{8,16},{12,20},{16,24},{20,28},{24,0},{28,4},{1,9},{5... | collective-permute-start | bytes 786440 | tf_op jit(solution)/shard_map/ppermute | solution.py:754
  72.1 14.4 %collective-permute-start.20 = (bf16[4,64,512]{2,1,0:T(8,128)(2,1)S(1)}, bf16[4,64,512]{2,1,0:T(8,128)(2,1)S(1)}, u32[]{:S(2)}, u32[]{:S(2)}) collective-permute-start(bf16[4,64,512]{2,1,0:T(8,128)(2,1)S(1)} %get-tuple-element.112), channel_id=1, source_target_pairs={{0,2},{1,3},{2,0},{3,1},{4,6},{5,7},{6,4},{7,5},{8,10},{9,11},{10,... | collective-permute-start | bytes 786440 | tf_op jit(solution)/shard_map/ppermute | solution.py:748
  72.1 32.7 %collective-permute-start.33 = (bf16[2,128,1024]{2,1,0:T(8,128)(2,1)}, bf16[2,128,1024]{2,1,0:T(8,128)(2,1)S(1)}, u32[]{:S(2)}, u32[]{:S(2)}) collective-permute-start(bf16[2,128,1024]{2,1,0:T(8,128)(2,1)} %get-tuple-element.122), channel_id=1, source_target_pairs={{0,2},{1,3},{2,0},{3,1},{4,6},{5,7},{6,4},{7,5},{8,10},{9,11},{10,... | collective-permute-start | bytes 1572872 | tf_op jit(solution)/shard_map/ppermute | solution.py:748
  84.1 20.5 %collective-permute-start.18 = (bf16[4,32,2816]{2,1,0:T(8,128)(2,1)S(1)}, bf16[4,32,2816]{2,1,0:T(8,128)(2,1)S(1)}, u32[]{:S(2)}, u32[]{:S(2)}) collective-permute-start(bf16[4,32,2816]{2,1,0:T(8,128)(2,1)S(1)} %get-tuple-element.246), channel_id=1, source_target_pairs={{0,2},{1,3},{2,0},{3,1},{4,6},{5,7},{6,4},{7,5},{8,10},{9,11},{10,... | collective-permute-start | bytes 2162696 | tf_op jit(solution)/shard_map/ppermute | solution.py:748
  84.3 20.3 %collective-permute-start.19 = (bf16[4,32,1280]{2,1,0:T(8,128)(2,1)S(1)}, bf16[4,32,1280]{2,1,0:T(8,128)(2,1)S(1)}, u32[]{:S(2)}, u32[]{:S(2)}) collective-permute-start(bf16[4,32,1280]{2,1,0:T(8,128)(2,1)S(1)} %get-tuple-element.250), channel_id=1, source_target_pairs={{0,4},{4,0},{8,12},{12,8},{16,20},{20,16},{24,28},{28,24},{1,5},{5... | collective-permute-start | bytes 983048 | tf_op jit(solution)/shard_map/ppermute | solution.py:751
  86.5 18.1 %collective-permute-start.21 = (bf16[2,4,64,512]{3,2,1,0:T(8,128)(2,1)S(1)}, bf16[2,4,64,512]{3,2,1,0:T(8,128)(2,1)S(1)}, u32[]{:S(2)}, u32[]{:S(2)}) collective-permute-start(bf16[2,4,64,512]{3,2,1,0:T(8,128)(2,1)S(1)} %pad_maximum_fusion.16.refs_0_), channel_id=1, source_target_pairs={{0,4},{4,0},{8,12},{12,8},{16,20},{20,16},{24,28},{28,24},{1,5},{5... | collective-permute-start | bytes 1572872 | tf_op jit(solution)/shard_map/ppermute | solution.py:751
  107.1 27.1 %collective-permute-start.34 = (bf16[2,2,128,1024]{3,2,1,0:T(8,128)(2,1)}, bf16[2,2,128,1024]{3,2,1,0:T(8,128)(2,1)}, u32[]{:S(2)}, u32[]{:S(2)}) collective-permute-start(bf16[2,2,128,1024]{3,2,1,0:T(8,128)(2,1)} %pad_maximum_fusion.8.refs_8_), channel_id=1, source_target_pairs={{0,8},{4,12},{8,16},{12,20},{16,24},{20,28},{24,0},{28,4},{1,9},{5... | collective-permute-start | bytes 3145736 | tf_op jit(solution)/shard_map/ppermute | solution.py:754
  110.5 23.7 %collective-permute-start.23 = (bf16[320,1024]{1,0:T(8,128)(2,1)}, bf16[320,1024]{1,0:T(8,128)(2,1)}, u32[]{:S(2)}, u32[]{:S(2)}) collective-permute-start(bf16[320,1024]{1,0:T(8,128)(2,1)} %select_bitcast_fusion.8), channel_id=1, source_target_pairs={{0,2},{1,3},{2,0},{3,1},{4,6},{5,7},{6,4},{7,5},{8,10},{9,11},{10,... | collective-permute-start | bytes 1966088 | tf_op jit(solution)/shard_map/ppermute | solution.py:650
  113.6 33.3 %collective-permute-start.26 = (bf16[2,4,32,2816]{3,2,1,0:T(8,128)(2,1)}, bf16[2,4,32,2816]{3,2,1,0:T(8,128)(2,1)}, u32[]{:S(2)}, u32[]{:S(2)}) collective-permute-start(bf16[2,4,32,2816]{3,2,1,0:T(8,128)(2,1)} %pad_maximum_fusion.1.refs_0_), channel_id=1, source_target_pairs={{0,4},{4,0},{8,12},{12,8},{16,20},{20,16},{24,28},{28,24},{1,5},{5... | collective-permute-start | bytes 4325384 | tf_op jit(solution)/shard_map/ppermute | solution.py:751
  113.8 24.5 %collective-permute-start.24 = (bf16[2,4,64,512]{3,2,1,0:T(8,128)(2,1)S(1)}, bf16[2,4,64,512]{3,2,1,0:T(8,128)(2,1)S(1)}, u32[]{:S(2)}, u32[]{:S(2)}) collective-permute-start(bf16[2,4,64,512]{3,2,1,0:T(8,128)(2,1)S(1)} %pad_maximum_fusion.16.refs_0_), channel_id=1, source_target_pairs={{0,1},{1,0},{2,3},{3,2},{4,5},{5,4},{6,7},{7,6},{8,9},{9,8},{10,11... | collective-permute-start | bytes 1572872 | tf_op jit(solution)/shard_map/ppermute | solution.py:745
  113.8 24.5 %collective-permute-start.25 = (bf16[2,4,64,512]{3,2,1,0:T(8,128)(2,1)S(1)}, bf16[2,4,64,512]{3,2,1,0:T(8,128)(2,1)}, u32[]{:S(2)}, u32[]{:S(2)}) collective-permute-start(bf16[2,4,64,512]{3,2,1,0:T(8,128)(2,1)S(1)} %collective-permute-done.21.refs_1_), channel_id=1, source_target_pairs={{0,1},{1,0},{2,3},{3,2},{4,5},{5,4},{6,7},{7,6},{8,9},{9,8},{10,11... | collective-permute-start | bytes 1572872 | tf_op jit(solution)/shard_map/ppermute | solution.py:745
  134.3 33.2 %collective-permute-start.28 = (bf16[2,4,32,2816]{3,2,1,0:T(8,128)(2,1)}, bf16[2,4,32,2816]{3,2,1,0:T(8,128)(2,1)}, u32[]{:S(2)}, u32[]{:S(2)}) collective-permute-start(bf16[2,4,32,2816]{3,2,1,0:T(8,128)(2,1)} %pad_maximum_fusion.1.refs_0_), channel_id=1, source_target_pairs={{0,1},{1,0},{2,3},{3,2},{4,5},{5,4},{6,7},{7,6},{8,9},{9,8},{10,11... | collective-permute-start | bytes 4325384 | tf_op jit(solution)/shard_map/ppermute | solution.py:745
  134.3 28.1 %collective-permute-start.35 = (bf16[2,2,128,1024]{3,2,1,0:T(8,128)(2,1)}, bf16[2,2,128,1024]{3,2,1,0:T(8,128)(2,1)}, u32[]{:S(2)}, u32[]{:S(2)}) collective-permute-start(bf16[2,2,128,1024]{3,2,1,0:T(8,128)(2,1)} %collective-permute-done.34.refs_9_), channel_id=1, source_target_pairs={{0,8},{4,12},{8,16},{12,20},{16,24},{20,28},{24,0},{28,4},{1,9},{5... | collective-permute-start | bytes 3145736 | tf_op jit(solution)/shard_map/ppermute | solution.py:754
  146.9 42.2 %collective-permute-start.29 = (bf16[2,4,32,2816]{3,2,1,0:T(8,128)(2,1)}, bf16[2,4,32,2816]{3,2,1,0:T(8,128)(2,1)}, u32[]{:S(2)}, u32[]{:S(2)}) collective-permute-start(bf16[2,4,32,2816]{3,2,1,0:T(8,128)(2,1)} %collective-permute-done.26.refs_1_), channel_id=1, source_target_pairs={{0,1},{1,0},{2,3},{3,2},{4,5},{5,4},{6,7},{7,6},{8,9},{9,8},{10,11... | collective-permute-start | bytes 4325384 | tf_op jit(solution)/shard_map/ppermute | solution.py:745
  147.0 17.3 %collective-permute-start.27 = (bf16[2,4,32,1280]{3,2,1,0:T(8,128)(2,1)S(1)}, bf16[2,4,32,1280]{3,2,1,0:T(8,128)(2,1)}, u32[]{:S(2)}, u32[]{:S(2)}) collective-permute-start(bf16[2,4,32,1280]{3,2,1,0:T(8,128)(2,1)S(1)} %pad_maximum_fusion.13.refs_2_), channel_id=1, source_target_pairs={{0,2},{1,3},{2,0},{3,1},{4,6},{5,7},{6,4},{7,5},{8,10},{9,11},{10,... | collective-permute-start | bytes 1966088 | tf_op jit(solution)/shard_map/ppermute | solution.py:748
  162.4 26.8 %collective-permute-start.36 = (bf16[2,2,128,1024]{3,2,1,0:T(8,128)(2,1)}, bf16[2,2,128,1024]{3,2,1,0:T(8,128)(2,1)S(1)}, u32[]{:S(2)}, u32[]{:S(2)}) collective-permute-start(bf16[2,2,128,1024]{3,2,1,0:T(8,128)(2,1)} %collective-permute-done.35.refs_10_), channel_id=1, source_target_pairs={{0,8},{4,12},{8,16},{12,20},{16,24},{20,28},{24,0},{28,4},{1,9},{5... | collective-permute-start | bytes 3145736 | tf_op jit(solution)/shard_map/ppermute | solution.py:754
  166.9 51.8 %collective-permute-start.37 = (bf16[2,2,128,1024]{3,2,1,0:T(8,128)(2,1)}, bf16[2,2,128,1024]{3,2,1,0:T(8,128)(2,1)}, u32[]{:S(2)}, u32[]{:S(2)}) collective-permute-start(bf16[2,2,128,1024]{3,2,1,0:T(8,128)(2,1)} %pad_maximum_fusion.8.refs_8_), channel_id=1, source_target_pairs={{0,1},{1,0},{2,3},{3,2},{4,5},{5,4},{6,7},{7,6},{8,9},{9,8},{10,11... | collective-permute-start | bytes 3145736 | tf_op jit(solution)/shard_map/ppermute | solution.py:745
  167.5 51.3 %collective-permute-start.38 = (bf16[2,2,128,1024]{3,2,1,0:T(8,128)(2,1)}, bf16[2,2,128,1024]{3,2,1,0:T(8,128)(2,1)}, u32[]{:S(2)}, u32[]{:S(2)}) collective-permute-start(bf16[2,2,128,1024]{3,2,1,0:T(8,128)(2,1)} %collective-permute-done.34.refs_9_), channel_id=1, source_target_pairs={{0,1},{1,0},{2,3},{3,2},{4,5},{5,4},{6,7},{7,6},{8,9},{9,8},{10,11... | collective-permute-start | bytes 3145736 | tf_op jit(solution)/shard_map/ppermute | solution.py:745
  167.5 51.2 %collective-permute-start.39 = (bf16[2,2,128,1024]{3,2,1,0:T(8,128)(2,1)}, bf16[2,2,128,1024]{3,2,1,0:T(8,128)(2,1)}, u32[]{:S(2)}, u32[]{:S(2)}) collective-permute-start(bf16[2,2,128,1024]{3,2,1,0:T(8,128)(2,1)} %collective-permute-done.35.refs_10_), channel_id=1, source_target_pairs={{0,1},{1,0},{2,3},{3,2},{4,5},{5,4},{6,7},{7,6},{8,9},{9,8},{10,11... | collective-permute-start | bytes 3145736 | tf_op jit(solution)/shard_map/ppermute | solution.py:745
  189.2 29.6 %collective-permute-start.40 = (bf16[2,2,128,1024]{3,2,1,0:T(8,128)(2,1)S(1)}, bf16[2,2,128,1024]{3,2,1,0:T(8,128)(2,1)}, u32[]{:S(2)}, u32[]{:S(2)}) collective-permute-start(bf16[2,2,128,1024]{3,2,1,0:T(8,128)(2,1)S(1)} %collective-permute-done.36.refs_11_), channel_id=1, source_target_pairs={{0,1},{1,0},{2,3},{3,2},{4,5},{5,4},{6,7},{7,6},{8,9},{9,8},{10,11... | collective-permute-start | bytes 3145736 | tf_op jit(solution)/shard_map/ppermute | solution.py:745
  218.2 42.8 %collective-permute-start.41 = (bf16[2,2,128,1024]{3,2,1,0:T(8,128)(2,1)}, bf16[2,2,128,1024]{3,2,1,0:T(8,128)(2,1)}, u32[]{:S(2)}, u32[]{:S(2)}) collective-permute-start(bf16[2,2,128,1024]{3,2,1,0:T(8,128)(2,1)} %get-tuple-element.130), channel_id=1, source_target_pairs={{0,1},{1,0},{2,3},{3,2},{4,5},{5,4},{6,7},{7,6},{8,9},{9,8},{10,11... | collective-permute-start | bytes 3145736 | tf_op jit(solution)/shard_map/ppermute | solution.py:745
  262.7 27.6 %collective-permute-start.42 = (bf16[2,2,128,1024]{3,2,1,0:T(8,128)(2,1)S(1)}, bf16[2,2,128,1024]{3,2,1,0:T(8,128)(2,1)S(1)}, u32[]{:S(2)}, u32[]{:S(2)}) collective-permute-start(bf16[2,2,128,1024]{3,2,1,0:T(8,128)(2,1)S(1)} %add_convert_fusion.4), channel_id=1, source_target_pairs={{0,8},{4,12},{8,16},{12,20},{16,24},{20,28},{24,0},{28,4},{1,9},{5... | collective-permute-start | bytes 3145736 | tf_op jit(solution)/shard_map/ppermute | solution.py:754
  267.0 43.9 %collective-permute-start.46 = (bf16[2,4,32,2816]{3,2,1,0:T(8,128)(2,1)}, bf16[2,4,32,2816]{3,2,1,0:T(8,128)(2,1)S(1)}, u32[]{:S(2)}, u32[]{:S(2)}) collective-permute-start(bf16[2,4,32,2816]{3,2,1,0:T(8,128)(2,1)} %get-tuple-element.137), channel_id=1, source_target_pairs={{0,1},{1,0},{2,3},{3,2},{4,5},{5,4},{6,7},{7,6},{8,9},{9,8},{10,11... | collective-permute-start | bytes 4325384 | tf_op jit(solution)/shard_map/ppermute | solution.py:745
  268.4 42.4 %collective-permute-start.47 = (bf16[2,4,32,2816]{3,2,1,0:T(8,128)(2,1)}, bf16[2,4,32,2816]{3,2,1,0:T(8,128)(2,1)}, u32[]{:S(2)}, u32[]{:S(2)}) collective-permute-start(bf16[2,4,32,2816]{3,2,1,0:T(8,128)(2,1)} %get-tuple-element.138), channel_id=1, source_target_pairs={{0,1},{1,0},{2,3},{3,2},{4,5},{5,4},{6,7},{7,6},{8,9},{9,8},{10,11... | collective-permute-start | bytes 4325384 | tf_op jit(solution)/shard_map/ppermute | solution.py:745
  303.0 25.1 %collective-permute-start.53 = (bf16[2,4,32,1024]{3,2,1,0:T(8,128)(2,1)}, bf16[2,4,32,1024]{3,2,1,0:T(8,128)(2,1)}, u32[]{:S(2)}, u32[]{:S(2)}) collective-permute-start(bf16[2,4,32,1024]{3,2,1,0:T(8,128)(2,1)} %get-tuple-element.148), channel_id=1, source_target_pairs={{0,1},{1,0},{2,3},{3,2},{4,5},{5,4},{6,7},{7,6},{8,9},{9,8},{10,11... | collective-permute-start | bytes 1572872 | tf_op jit(solution)/shard_map/ppermute | solution.py:745
  303.1 27.0 %collective-permute-start.55 = (bf16[2,4,32,1024]{3,2,1,0:T(8,128)(2,1)}, bf16[2,4,32,1024]{3,2,1,0:T(8,128)(2,1)}, u32[]{:S(2)}, u32[]{:S(2)}) collective-permute-start(bf16[2,4,32,1024]{3,2,1,0:T(8,128)(2,1)} %get-tuple-element.153), channel_id=1, source_target_pairs={{0,1},{1,0},{2,3},{3,2},{4,5},{5,4},{6,7},{7,6},{8,9},{9,8},{10,11... | collective-permute-start | bytes 1572872 | tf_op jit(solution)/shard_map/ppermute | solution.py:745
  310.8 46.0 %collective-permute-start.76 = (bf16[2,2,128,1024]{3,2,1,0:T(8,128)(2,1)S(1)}, bf16[2,2,128,1024]{3,2,1,0:T(8,128)(2,1)S(1)}, u32[]{:S(2)}, u32[]{:S(2)}) collective-permute-start(bf16[2,2,128,1024]{3,2,1,0:T(8,128)(2,1)S(1)} %add_convert_fusion.3), channel_id=1, source_target_pairs={{0,8},{4,12},{8,16},{12,20},{16,24},{20,28},{24,0},{28,4},{1,9},{5... | collective-permute-start | bytes 3145736 | tf_op jit(solution)/shard_map/ppermute | solution.py:754
  311.0 16.8 %collective-permute-start.50 = (bf16[320,1024]{1,0:T(8,128)(2,1)S(1)}, bf16[320,1024]{1,0:T(8,128)(2,1)S(1)}, u32[]{:S(2)}, u32[]{:S(2)}) collective-permute-start(bf16[320,1024]{1,0:T(8,128)(2,1)S(1)} %broadcast_select_fusion.7), channel_id=1, source_target_pairs={{0,2},{1,3},{2,0},{3,1},{4,6},{5,7},{6,4},{7,5},{8,10},{9,11},{10,... | collective-permute-start | bytes 1966088 | tf_op jit(solution)/shard_map/ppermute | solution.py:650
  314.4 44.4 %collective-permute-start.52 = (bf16[2,4,32,2816]{3,2,1,0:T(8,128)(2,1)S(1)}, bf16[2,4,32,2816]{3,2,1,0:T(8,128)(2,1)S(1)}, u32[]{:S(2)}, u32[]{:S(2)}) collective-permute-start(bf16[2,4,32,2816]{3,2,1,0:T(8,128)(2,1)S(1)} %add_convert_fusion.1), channel_id=1, source_target_pairs={{0,4},{4,0},{8,12},{12,8},{16,20},{20,16},{24,28},{28,24},{1,5},{5... | collective-permute-start | bytes 4325384 | tf_op jit(solution)/shard_map/ppermute | solution.py:751
  331.6 29.5 %collective-permute-start.54 = (bf16[2,4,32,2304]{3,2,1,0:T(8,128)(2,1)S(1)}, bf16[2,4,32,2304]{3,2,1,0:T(8,128)(2,1)S(1)}, u32[]{:S(2)}, u32[]{:S(2)}) collective-permute-start(bf16[2,4,32,2304]{3,2,1,0:T(8,128)(2,1)S(1)} %pad_maximum_fusion.7), channel_id=1, source_target_pairs={{0,2},{1,3},{2,0},{3,1},{4,6},{5,7},{6,4},{7,5},{8,10},{9,11},{10,... | collective-permute-start | bytes 3538952 | tf_op jit(solution)/shard_map/ppermute | solution.py:748
  358.6 67.5 %collective-permute-start.77 = (bf16[2,2,128,1024]{3,2,1,0:T(8,128)(2,1)}, bf16[2,2,128,1024]{3,2,1,0:T(8,128)(2,1)}, u32[]{:S(2)}, u32[]{:S(2)}) collective-permute-start(bf16[2,2,128,1024]{3,2,1,0:T(8,128)(2,1)} %add_convert_fusion.2), channel_id=1, source_target_pairs={{0,8},{4,12},{8,16},{12,20},{16,24},{20,28},{24,0},{28,4},{1,9},{5... | collective-permute-start | bytes 3145736 | tf_op jit(solution)/shard_map/ppermute | solution.py:754
  360.5 20.4 %collective-permute-start.57 = (bf16[4,32,2816]{2,1,0:T(8,128)(2,1)S(1)}, bf16[4,32,2816]{2,1,0:T(8,128)(2,1)S(1)}, u32[]{:S(2)}, u32[]{:S(2)}) collective-permute-start(bf16[4,32,2816]{2,1,0:T(8,128)(2,1)S(1)} %fusion.8), channel_id=1, source_target_pairs={{0,2},{1,3},{2,0},{3,1},{4,6},{5,7},{6,4},{7,5},{8,10},{9,11},{10,... | collective-permute-start | bytes 2162696 | tf_op jit(solution)/shard_map/ppermute | solution.py:748
  362.0 19.0 %collective-permute-start.58 = (bf16[4,32,2304]{2,1,0:T(8,128)(2,1)S(1)}, bf16[4,32,2304]{2,1,0:T(8,128)(2,1)S(1)}, u32[]{:S(2)}, u32[]{:S(2)}) collective-permute-start(bf16[4,32,2304]{2,1,0:T(8,128)(2,1)S(1)} %fusion.27), channel_id=1, source_target_pairs={{0,4},{4,0},{8,12},{12,8},{16,20},{20,16},{24,28},{28,24},{1,5},{5... | collective-permute-start | bytes 1769480 | tf_op jit(solution)/shard_map/ppermute | solution.py:751
  381.0 12.9 %collective-permute-start.59 = (bf16[2,4,64,512]{3,2,1,0:T(8,128)(2,1)S(1)}, bf16[2,4,64,512]{3,2,1,0:T(8,128)(2,1)}, u32[]{:S(2)}, u32[]{:S(2)}) collective-permute-start(bf16[2,4,64,512]{3,2,1,0:T(8,128)(2,1)S(1)} %get-tuple-element.159), channel_id=1, source_target_pairs={{0,4},{4,0},{8,12},{12,8},{16,20},{20,16},{24,28},{28,24},{1,5},{5... | collective-permute-start | bytes 1572872 | tf_op jit(solution)/shard_map/ppermute | solution.py:751
  382.1 12.8 %collective-permute-start.62 = (bf16[2,4,64,512]{3,2,1,0:T(8,128)(2,1)S(1)}, bf16[2,4,64,512]{3,2,1,0:T(8,128)(2,1)}, u32[]{:S(2)}, u32[]{:S(2)}) collective-permute-start(bf16[2,4,64,512]{3,2,1,0:T(8,128)(2,1)S(1)} %get-tuple-element.163), channel_id=1, source_target_pairs={{0,2},{1,3},{2,0},{3,1},{4,6},{5,7},{6,4},{7,5},{8,10},{9,11},{10,... | collective-permute-start | bytes 1572872 | tf_op jit(solution)/shard_map/ppermute | solution.py:748
  384.9 13.5 %collective-permute-start.68 = (bf16[32,5120]{1,0:T(8,128)(2,1)}, bf16[32,5120]{1,0:T(8,128)(2,1)}, u32[]{:S(2)}, u32[]{:S(2)}) collective-permute-start(bf16[32,5120]{1,0:T(8,128)(2,1)} %fusion.34), channel_id=1, source_target_pairs={{0,8},{4,12},{8,16},{12,20},{16,24},{20,28},{24,0},{28,4},{1,9},{5... | collective-permute-start | bytes 983048 | tf_op jit(solution)/shard_map/ppermute | solution.py:754
  387.2 32.7 %collective-permute-start.56 = (bf16[2,320,1024]{2,1,0:T(8,128)(2,1)}, bf16[2,320,1024]{2,1,0:T(8,128)(2,1)}, u32[]{:S(2)}, u32[]{:S(2)}) collective-permute-start(bf16[2,320,1024]{2,1,0:T(8,128)(2,1)} %select_bitcast_fusion), channel_id=1, source_target_pairs={{0,1},{1,0},{2,3},{3,2},{4,5},{5,4},{6,7},{7,6},{8,9},{9,8},{10,11... | collective-permute-start | bytes 3932168 | tf_op jit(solution)/shard_map/ppermute | solution.py:647
  399.5 17.7 %collective-permute-start.69 = (bf16[32,5120]{1,0:T(8,128)(2,1)S(1)}, bf16[32,5120]{1,0:T(8,128)(2,1)S(1)}, u32[]{:S(2)}, u32[]{:S(2)}) collective-permute-start(bf16[32,5120]{1,0:T(8,128)(2,1)S(1)} %fusion.20), channel_id=1, source_target_pairs={{0,8},{4,12},{8,16},{12,20},{16,24},{20,28},{24,0},{28,4},{1,9},{5... | collective-permute-start | bytes 983048 | tf_op jit(solution)/shard_map/ppermute | solution.py:754
  407.0 15.1 %collective-permute-start.60 = (bf16[4,64,512]{2,1,0:T(8,128)(2,1)S(1)}, bf16[4,64,512]{2,1,0:T(8,128)(2,1)S(1)}, u32[]{:S(2)}, u32[]{:S(2)}) collective-permute-start(bf16[4,64,512]{2,1,0:T(8,128)(2,1)S(1)} %fusion.35), channel_id=1, source_target_pairs={{0,2},{1,3},{2,0},{3,1},{4,6},{5,7},{6,4},{7,5},{8,10},{9,11},{10,... | collective-permute-start | bytes 786440 | tf_op jit(solution)/shard_map/ppermute | solution.py:748
  417.3 15.2 %collective-permute-start.70 = (bf16[32,5120]{1,0:T(8,128)(2,1)S(1)}, bf16[32,5120]{1,0:T(8,128)(2,1)S(1)}, u32[]{:S(2)}, u32[]{:S(2)}) collective-permute-start(bf16[32,5120]{1,0:T(8,128)(2,1)S(1)} %fusion.14), channel_id=1, source_target_pairs={{0,8},{4,12},{8,16},{12,20},{16,24},{20,28},{24,0},{28,4},{1,9},{5... | collective-permute-start | bytes 983048 | tf_op jit(solution)/shard_map/ppermute | solution.py:754
  422.1 20.7 %collective-permute-start.61 = (bf16[320,1024]{1,0:T(8,128)(2,1)S(1)}, bf16[320,1024]{1,0:T(8,128)(2,1)S(1)}, u32[]{:S(2)}, u32[]{:S(2)}) collective-permute-start(bf16[320,1024]{1,0:T(8,128)(2,1)S(1)} %select_bitcast_fusion.3), channel_id=1, source_target_pairs={{0,2},{1,3},{2,0},{3,1},{4,6},{5,7},{6,4},{7,5},{8,10},{9,11},{10,... | collective-permute-start | bytes 1966088 | tf_op jit(solution)/shard_map/ppermute | solution.py:650
  428.3 13.0 %collective-permute-start.78 = (bf16[2,128,1024]{2,1,0:T(8,128)(2,1)S(1)}, bf16[2,128,1024]{2,1,0:T(8,128)(2,1)S(1)}, u32[]{:S(2)}, u32[]{:S(2)}) collective-permute-start(bf16[2,128,1024]{2,1,0:T(8,128)(2,1)S(1)} %fusion.28), channel_id=1, source_target_pairs={{0,4},{4,0},{8,12},{12,8},{16,20},{20,16},{24,28},{28,24},{1,5},{5... | collective-permute-start | bytes 1572872 | tf_op jit(solution)/shard_map/ppermute | solution.py:751
  (104 other events, 887.9 us)
